TPU v7x, 32 devices: a whole 2x2x4 slice. The times are simulated.
32 devices in a mesh: table: 16 (over z, y, core), dp: 2 (over x).
Axes of the slice: x: 2, y: 2, z: 4, core: 2. Of those that a mesh axis runs over, the one named last changes fastest.
Arguments:
- owners: int32 [16384, 8], P(('table', 'dp')), may hold values from 0 to 15, all different within a row; in each aligned block of 512 rows (0 to 511, 512 to 1023, ...) at most 512 rows name the same one
- local_rows: int32 [16384, 8], P(('table', 'dp')), may hold values from 0 to 4095
- grad_pooled: bfloat16 [16384, 128], P(('table', 'dp')), may hold values from -4 to 4
- table: float32 [65536, 128], P('table'), may hold values from -6 to 6
- accum: float32 [65536], P('table'), may hold values from 0.1 to 4
- parity: float32 [8192, 128], P('table'), may hold values from -6 to 6
- parity_slot: int32 [65536], P('table'), may hold values from 0 to 8191, as said below
Outputs:
- pooled: bfloat16 [16384, 128], P(('table', 'dp'))
- new_table: float32 [65536, 128], P('table')
- new_accum: float32 [65536], P('table')
- new_parity: float32 [8192, 128], P('table')
Inputs may be any that keep to these rules, and one draw needn't show every extreme that they name: `owners`: each bag names 8 different table devices. Among the 512 bags of one device (aligned blocks of rows), no table device is named by more than 512 bags, and in some blocks one is named by exactly 512. `parity_slot`: within the 4096 rows of one table device the values are distinct, and each device's rows include the value 8192 - 1. Parity row v is held by the table device v // 512.
All inputs are finite; a program needn't handle non-finite values.
Results may differ from a plain program's by a relative error of at most 0.0085.
Values may be sent and summed in bfloat16 or wider, within the bound.
No kernel may reach another device: no remote copies, remote signals or barrier semaphores. Data moves between devices by JAX's collectives and lax.ppermute only.
A program may use at most 64 MiB of HBM per device.

v0:
```python
import jax
import jax.numpy as jnp
from jax import lax
from jax.sharding import PartitionSpec as P

LEARN = 0.5
EPSILON = 1e-06


def adagrad(old_rows, old_accum, row_grads):
    fresh_accum = old_accum + jnp.mean(row_grads * row_grads, axis=1)
    fresh_rows = old_rows - LEARN * row_grads / jnp.sqrt(fresh_accum + EPSILON)[:, None]
    return (fresh_rows, fresh_accum)


def fold_sources(received):
    return jnp.sum(received, axis=0)


def on_device(owners, local_rows, grad_pooled, table, accum, parity, parity_slot):
    table_count = lax.axis_size("table")
    bag_count, per_bag = owners.shape
    row_count, row_width = table.shape
    lookup_count = bag_count * per_bag
    capacity = min(bag_count, 2 * lookup_count // table_count)
    slot_count = table_count * capacity
    owner_flat = owners.reshape(lookup_count)
    local_flat = local_rows.reshape(lookup_count)
    owner_hits = (owner_flat[:, None] == jnp.arange(table_count, dtype=jnp.int32)[None, :]).astype(
        jnp.int32
    )
    slot_rank = jnp.sum((jnp.cumsum(owner_hits, axis=0) - 1) * owner_hits, axis=1)
    position = owner_flat * capacity + slot_rank
    requests = jnp.full((slot_count,), row_count, jnp.int32).at[position].set(local_flat)
    requests = requests.reshape(table_count, capacity)
    table_half = table.astype(jnp.bfloat16)
    asked_rows = lax.all_to_all(requests, "table", split_axis=0, concat_axis=0, tiled=True)
    fetched = jnp.take(table_half, jnp.minimum(asked_rows, row_count - 1), axis=0)
    returned = lax.all_to_all(fetched, "table", split_axis=0, concat_axis=0, tiled=True)
    returned_rows, asked_rows = (returned, asked_rows)
    gathered = returned_rows.reshape(slot_count, row_width)[position]
    pooled = jnp.sum(
        gathered.reshape(bag_count, per_bag, row_width).astype(jnp.float32), axis=1
    ).astype(jnp.bfloat16)
    spread = jnp.repeat(grad_pooled, per_bag, axis=0)
    outgoing = jnp.zeros((slot_count, row_width), jnp.bfloat16).at[position].set(spread)
    incoming = lax.all_to_all(
        outgoing.reshape(table_count, capacity, row_width),
        "table",
        split_axis=0,
        concat_axis=0,
        tiled=True,
    )
    row_ids = jnp.minimum(asked_rows, row_count - 1).reshape(slot_count)
    partial_grads = jax.ops.segment_sum(
        incoming.reshape(slot_count, row_width).astype(jnp.float32), row_ids, num_segments=row_count
    )
    grad_share = lax.psum_scatter(
        partial_grads.astype(jnp.bfloat16), "dp", scatter_dimension=0, tiled=True
    ).astype(jnp.float32)
    share_rows = grad_share.shape[0]
    first_row = lax.axis_index("dp") * share_rows
    rows_part = lax.dynamic_slice_in_dim(table, first_row, share_rows, 0)
    accum_part = lax.dynamic_slice_in_dim(accum, first_row, share_rows, 0)
    fresh_rows, fresh_accum = adagrad(rows_part, accum_part, grad_share)
    new_table, new_accum = (
        lax.all_gather(fresh_rows, "dp", axis=0, tiled=True),
        lax.all_gather(fresh_accum, "dp", axis=0, tiled=True),
    )
    row_delta = new_table - table
    parity_count = parity.shape[0]
    buffer = (
        jnp.zeros((table_count * parity_count, row_width), jnp.float32)
        .at[parity_slot]
        .set(row_delta)
    )
    buffer = buffer.reshape(table_count, parity_count, row_width)
    parity_sum = fold_sources(
        lax.all_to_all(
            buffer.astype(jnp.bfloat16), "table", split_axis=0, concat_axis=0, tiled=True
        ).astype(buffer.dtype)
    )
    new_parity = parity + parity_sum
    return (pooled, new_table, new_accum, new_parity)


def solution(mesh):
    in_specs = (
        P(("table", "dp"), None),
        P(("table", "dp"), None),
        P(("table", "dp"), None),
        P("table", None),
        P("table"),
        P("table", None),
        P("table"),
    )
    out_specs = (P(("table", "dp"), None), P("table", None), P("table"), P("table", None))
    return jax.shard_map(
        on_device, mesh=mesh, in_specs=in_specs, out_specs=out_specs, check_vma=False
    )
```

profile of v0, /device:TPU:0, one launch (start us, length us, event | category | flops | bytes accessed | tf_op | source)
XLA Modules:
  0.0 308.0 jit_solution(15081148376140345214)
XLA Ops:
  7.2 0.9 copy.16
  9.1 4.6 %reduce-window.6 = s32[16,32,128]{2,1,0:T(8,128)S(1)} reduce-window(s32[16,32,128]{2,1,0:T(8,128)S(1)} %fusion.15, s32[]{:T(128)} %constant.16.clone.1), window={size=1x1x128 pad=0_0x0_0x127_0}, to_apply=%region_0.0 | reduce-window | flops 8323072 | bytes 524292 | tf_op jit(solution)/shard_map/reduce-window
  15.4 16.1 %scatter_custom_fusion = s32[8192]{0:T(1024)} fusion(s32[4096]{0:T(1024)S(1)} %bitcast.44, s32[4096]{0:T(1024)S(1)} %reshape.149, s32[]{:T(128)} %constant.14.clone.1), kind=kCustom, calls=%fused_computation.39 | custom fusion | bytes 32772 | tf_op jit(solution)/shard_map/scatter | solution.py:34
  31.5 7.4 %all-to-all-start = ((s32[16,1,512]{2,1,0:T(1,128)}), s32[16,1,512]{2,1,0:T(1,128)S(1)}, u32[]{:S(2)}, u32[]{:S(2)}) async-start(s32[16,1,512]{2,1,0:T(1,128)} %bitcast.3), calls=%async_computation | async-start | bytes 65536 | tf_op jit(solution)/shard_map/all_to_all | solution.py:37
  38.9 12.4 %scatter_custom_fusion.1 = bf16[8192,128]{1,0:T(8,128)(2,1)} fusion(s32[4096]{0:T(1024)S(1)} %bitcast.45, bf16[]{:T(256)} %constant.21.clone.1, bf16[512,128]{1,0:T(8,128)(2,1)S(1)} %copy-done), kind=kCustom, calls=%fused_computation.18 | custom fusion | bytes 2228226 | tf_op jit(solution)/shard_map/scatter | solution.py:46
  51.3 6.0 %all-to-all-start.2 = ((bf16[16,512,128]{2,1,0:T(8,128)(2,1)}), bf16[16,512,128]{2,1,0:T(8,128)(2,1)S(1)}, u32[]{:S(2)}, u32[]{:S(2)}) async-start(bf16[16,512,128]{2,1,0:T(8,128)(2,1)} %bitcast.11), calls=%async_computation.2 | async-start | bytes 4194304 | tf_op jit(solution)/shard_map/all_to_all | solution.py:47
  57.4 40.9 %all-to-all-done.2 = bf16[16,512,128]{2,1,0:T(8,128)(2,1)S(1)} async-done(((bf16[16,512,128]{2,1,0:T(8,128)(2,1)}), bf16[16,512,128]{2,1,0:T(8,128)(2,1)S(1)}, u32[]{:S(2)}, u32[]{:S(2)}) %all-to-all-start.2) | async-done | bytes 2097184 | tf_op jit(solution)/shard_map/all_to_all | solution.py:47
  98.3 45.7 %scatter_custom_fusion.2 = f32[4096,128]{1,0:T(8,128)} fusion(s32[8192]{0:T(1024)S(1)} %bitcast.41, bf16[8192,128]{1,0:T(8,128)(2,1)S(1)} %bitcast.39, f32[]{:T(128)} %constant.24.clone.1), kind=kCustom, calls=%fused_computation.6 | custom fusion | flops 2097152 | bytes 4194308 | tf_op jit(solution)/shard_map/scatter-add | solution.py:55
  144.0 2.8 convert_element_type.35
  147.1 24.0 %gather_fusion = bf16[8192,128]{1,0:T(8,128)(2,1)S(1)} fusion(bf16[4096,128]{1,0:T(8,128)(2,1)S(1)} %convert_element_type.32, s32[8192]{0:T(1024)S(1)} %broadcast_clamp_fusion), kind=kCustom, calls=%fused_computation | custom fusion | bytes 4227072 | tf_op jit(solution)/shard_map/jit(_take)/gather | solution.py:38
  171.1 2.6 broadcast_select_fusion
  173.8 20.1 %all-to-all-start.1 = ((bf16[16,512,128]{2,1,0:T(8,128)(2,1)}), bf16[16,512,128]{2,1,0:T(8,128)(2,1)S(1)}, u32[]{:S(2)}, u32[]{:S(2)}) async-start(bf16[16,512,128]{2,1,0:T(8,128)(2,1)} %broadcast_select_fusion), calls=%async_computation.1 | async-start | bytes 4194304 | tf_op jit(solution)/shard_map/all_to_all | solution.py:39
  194.0 1.4 fusion.7
  195.4 2.7 fusion.6
  198.2 34.7 %all-gather.2.cloned.1.call-done = f32[4096,128]{1,0:T(8,128)} async-done(((f32[2048,128]{1,0:T(8,128)}), f32[4096,128]{1,0:T(8,128)}) %all-gather.2.cloned.1.call-update) | async-done | bytes 2097168 | tf_op jit(solution)/shard_map/all_gather | solution.py:67
  232.8 13.4 %scatter_custom_fusion.3 = f32[8192,128]{1,0:T(8,128)} fusion(s32[4096]{0:T(1024)S(1)} %compare_select_fusion.3, f32[4096,128]{1,0:T(8,128)} %all-gather.2.cloned.1.call-done, f32[4096,128]{1,0:T(8,128)} %param.10, f32[]{:T(128)} %constant.24.clone.1), kind=kCustom, calls=%fused_computation.9 | custom fusion | flops 524288 | bytes 8388612 | tf_op jit(solution)/shard_map/scatter | solution.py:75
  246.2 3.7 %convert_element_type.37 = bf16[8192,128]{1,0:T(8,128)(2,1)} convert(f32[8192,128]{1,0:T(8,128)} %scatter_custom_fusion.3) | non-fusion elementwise | flops 1048576 | bytes 6291456 | tf_op jit(solution)/shard_map/convert_element_type | solution.py:80
  249.9 5.7 %all-to-all-start.3 = ((bf16[16,512,128]{2,1,0:T(8,128)(2,1)}), bf16[16,512,128]{2,1,0:T(8,128)(2,1)}, u32[]{:S(2)}, u32[]{:S(2)}) async-start(bf16[16,512,128]{2,1,0:T(8,128)(2,1)} %bitcast.37), calls=%async_computation.4 | async-start | bytes 4194304 | tf_op jit(solution)/shard_map/all_to_all | solution.py:79
  255.6 12.1 %gather_fusion.1 = bf16[4096,128]{1,0:T(8,128)(2,1)S(1)} fusion(bf16[8192,128]{1,0:T(8,128)(2,1)S(1)} %bitcast.36, s32[4096]{0:T(1024)S(1)} %broadcast_clamp_fusion.1), kind=kCustom, calls=%fused_computation.1 | custom fusion | bytes 2113536 | tf_op jit(solution)/shard_map/gather | solution.py:41
  267.8 1.3 bitcast_reduce_fusion
  269.1 4.3 %all_gather.7 = f32[4096]{0:T(1024)S(1)} all-gather(f32[2048]{0:T(1024)S(1)} %get-tuple-element.5), channel_id=1, replica_groups=mesh['table'=16,'dp'=2] {'dp'}, dimensions={0}, use_global_device_ids=true | all-gather | bytes 24576 | tf_op jit(solution)/shard_map/all_gather | solution.py:68
  273.5 23.2 %all-to-all-done.3 = bf16[16,512,128]{2,1,0:T(8,128)(2,1)} async-done(((bf16[16,512,128]{2,1,0:T(8,128)(2,1)}), bf16[16,512,128]{2,1,0:T(8,128)(2,1)}, u32[]{:S(2)}, u32[]{:S(2)}) %all-to-all-start.3) | async-done | bytes 2097184 | tf_op jit(solution)/shard_map/all_to_all | solution.py:79
  296.6 1.9 convert_reduce_fusion
  299.3 1.3 copy.27
  (44 shorter events, 4.4 us)
Async XLA Ops:
  7.2 31.7 %copy-start = (bf16[512,128]{1,0:T(8,128)(2,1)S(1)}, bf16[512,128]{1,0:T(8,128)(2,1)}, u32[]{:S(2)}) copy-start(bf16[512,128]{1,0:T(8,128)(2,1)} %param.9) | copy-start | bytes 393220
  7.2 7.7 %copy-start.4 = (s32[512,8]{0,1:T(8,128)S(1)}, s32[512,8]{0,1:T(8,128)}, u32[]{:S(2)}) copy-start(s32[512,8]{0,1:T(8,128)} %param.8) | copy-start | bytes 49156
  31.5 19.8 %all-to-all-start = ((s32[16,1,512]{2,1,0:T(1,128)}), s32[16,1,512]{2,1,0:T(1,128)S(1)}, u32[]{:S(2)}, u32[]{:S(2)}) async-start(s32[16,1,512]{2,1,0:T(1,128)} %bitcast.3), calls=%async_computation | async-start | bytes 65536 | tf_op jit(solution)/shard_map/all_to_all | solution.py:37
  51.3 47.0 %all-to-all-start.2 = ((bf16[16,512,128]{2,1,0:T(8,128)(2,1)}), bf16[16,512,128]{2,1,0:T(8,128)(2,1)S(1)}, u32[]{:S(2)}, u32[]{:S(2)}) async-start(bf16[16,512,128]{2,1,0:T(8,128)(2,1)} %bitcast.11), calls=%async_computation.2 | async-start | bytes 4194304 | tf_op jit(solution)/shard_map/all_to_all | solution.py:47
  57.3 136.6 %reduce-scatter.2.cloned.1.call-start = ((), (), s32[]{:S(2)}) async-start(), calls=%async_computation.5 | async-start | bytes 1572864 | tf_op jit(solution)/shard_map/reduce_scatter | solution.py:58
  144.0 2.9 copy-start.1
  173.8 21.6 %copy-start.6 = (f32[4096]{0:T(1024)S(1)}, f32[4096]{0:T(1024)}, u32[]{:S(2)}) copy-start(f32[4096]{0:T(1024)} %param.11) | copy-start | bytes 49156
  173.8 76.1 %all-to-all-start.1 = ((bf16[16,512,128]{2,1,0:T(8,128)(2,1)}), bf16[16,512,128]{2,1,0:T(8,128)(2,1)S(1)}, u32[]{:S(2)}, u32[]{:S(2)}) async-start(bf16[16,512,128]{2,1,0:T(8,128)(2,1)} %broadcast_select_fusion), calls=%async_computation.1 | async-start | bytes 4194304 | tf_op jit(solution)/shard_map/all_to_all | solution.py:39
  193.9 39.0 %all-gather.2.cloned.1.call-start = ((), (), s32[]{:S(2)}) async-start(), calls=%async_computation.6 | async-start | bytes 3145728 | tf_op jit(solution)/shard_map/all_gather | solution.py:67
  193.9 4.2 %copy-start.5 = (s32[4096]{0:T(1024)S(1)}, s32[4096]{0:T(1024)}, u32[]{:S(2)}) copy-start(s32[4096]{0:T(1024)} %param.13) | copy-start | bytes 49156
  249.9 46.7 %all-to-all-start.3 = ((bf16[16,512,128]{2,1,0:T(8,128)(2,1)}), bf16[16,512,128]{2,1,0:T(8,128)(2,1)}, u32[]{:S(2)}, u32[]{:S(2)}) async-start(bf16[16,512,128]{2,1,0:T(8,128)(2,1)} %bitcast.37), calls=%async_computation.4 | async-start | bytes 4194304 | tf_op jit(solution)/shard_map/all_to_all | solution.py:79
  267.8 30.8 %copy-start.3 = (f32[512,128]{1,0:T(8,128)S(1)}, f32[512,128]{1,0:T(8,128)}, u32[]{:S(2)}) copy-start(f32[512,128]{1,0:T(8,128)} %param.12) | copy-start | bytes 786436
  267.8 31.5 %copy-start.2 = (f32[4096,128]{1,0:T(8,128)S(1)}, f32[4096,128]{1,0:T(8,128)}, u32[]{:S(2)}) copy-start(f32[4096,128]{1,0:T(8,128)} %all-gather.2.cloned.1.call-done) | copy-start | bytes 6291460
Sparse Core Ops, SparseCore 0:
  147.0 35.7 reduce-scatter.1
  198.3 34.5 all-gather.1
where the time goes:
time: 314 us; the launch traced here: 308 us
  waiting for transfers between devices  98.8 us (31%)
  other arithmetic  82.5 us (26%)
  local copies, waits for them, and re-layouts  68.8 us (22%)
  starting transfers between devices  39.2 us (12%)
  between operations  14.3 us (5%)
  blocking collectives  4.35 us (1%)
    scatter-add x1, other arithmetic, on_device(): jax.ops.segment_sum(incoming.reshape(slot_count, row_width).astype(jnp.fl...  45.7 us
    all_to_all x1, waiting for transfers between devices, on_device(): lax.all_to_all(outgoing.reshape(table_count, capacity, row_width), 'table...  40.9 us
    all_gather x1, waiting for transfers between devices, on_device(): lax.all_gather(fresh_rows, 'dp', axis=0, tiled=True)  34.7 us
    gather x1, local copies, waits for them, and re-layouts, on_device(): jnp.take(table_half, jnp.minimum(asked_rows, row_count - 1), axis=0)  24 us
    all_to_all x1, waiting for transfers between devices, on_device(): lax.all_to_all(buffer.astype(jnp.bfloat16), 'table', split_axis=0, concat...  23.2 us
    all_to_all x1, starting transfers between devices, on_device(): lax.all_to_all(fetched, 'table', split_axis=0, concat_axis=0, tiled=True)  20.1 us
    scatter x1, local copies, waits for them, and re-layouts, on_device(): jnp.full((slot_count,), row_count, jnp.int32).at[position].set(local_flat)  16.1 us
    scatter x1, other arithmetic, on_device(): buffer = jnp.zeros((table_count * parity_count, row_width), jnp.float32)....  13.4 us
  transfers between devices with their start and end apart: 6, of which 3 were waited for; matrix products, arithmetic and copies ran while one was open for 24% of the time, Pallas kernels for 0%

commit v1 on v0

v1 whole, which is shorter than its diff:
```python
import functools
import jax
import jax.numpy as jnp
from jax import lax
from jax.experimental import pallas as pl
from jax.experimental.pallas import tpu as pltpu
from jax.sharding import PartitionSpec as P

LEARN = 0.5
EPSILON = 1e-06
SPLIT = 4


def column_of(row, lanes):
    return jnp.broadcast_to(row, (lanes, row.shape[1])).T


def split_index(index, low_count):
    bits = low_count.bit_length() - 1
    return lax.shift_right_arithmetic(index, bits), lax.bitwise_and(index, low_count - 1)


def tile_of(count, most):
    tile = most
    while count % tile:
        tile //= 2
    return tile


def segment_kernel(index_ref, rows_ref, out_ref, total_ref, *, low_count):
    step = pl.program_id(0)
    index = index_ref[0]
    width = rows_ref.shape[1]
    block, low = split_index(index, low_count)
    low = jnp.where(index < 0, -1, low)
    hits = (
        (lax.broadcasted_iota(jnp.int32, (low_count, index.shape[1]), 0) == low)
        .astype(jnp.float32)
        .astype(jnp.bfloat16)
    )
    block_column = column_of(block, width)
    rows = rows_ref[...].astype(jnp.float32)
    spread = jnp.concatenate(
        [jnp.where(block_column == i, rows, 0.0).astype(jnp.bfloat16) for i in range(SPLIT)], axis=1
    )
    part = jnp.dot(hits, spread, preferred_element_type=jnp.float32)

    @pl.when(step == 0)
    def _():
        total_ref[...] = part

    @pl.when(step > 0)
    def _():
        total_ref[...] += part

    @pl.when(step == pl.num_programs(0) - 1)
    def _():
        for i in range(SPLIT):
            out_ref[i] = total_ref[:, i * width : (i + 1) * width].astype(out_ref.dtype)


def segment_sums(index, rows, segment_count):
    count, width = rows.shape
    tile = tile_of(count, 2048)
    low_count = segment_count // SPLIT
    out = pl.pallas_call(
        functools.partial(segment_kernel, low_count=low_count),
        grid=(count // tile,),
        in_specs=[
            pl.BlockSpec((1, 1, tile), lambda k: (k, 0, 0)),
            pl.BlockSpec((tile, width), lambda k: (k, 0)),
        ],
        out_specs=pl.BlockSpec((SPLIT, low_count, width), lambda k: (0, 0, 0)),
        out_shape=jax.ShapeDtypeStruct((SPLIT, low_count, width), jnp.bfloat16),
        scratch_shapes=[pltpu.VMEM((low_count, SPLIT * width), jnp.float32)],
    )(index.reshape(count // tile, 1, tile), rows)
    return out.reshape(segment_count, width)


def gather_kernel(own_index_ref, peer_index_ref, own_ref, peer_ref, out_ref, held_ref, *, low_count):
    width = out_ref.shape[1]

    @pl.when(pl.program_id(0) == 0)
    def _():
        for i in range(SPLIT):
            held_ref[0, :, i * width : (i + 1) * width] = own_ref[i]
            held_ref[1, :, i * width : (i + 1) * width] = peer_ref[i]

    total = jnp.zeros(out_ref.shape, jnp.float32)
    lane = lax.broadcasted_iota(jnp.int32, out_ref.shape, 1)
    for side, index_ref in enumerate((own_index_ref, peer_index_ref)):
        block, low = split_index(column_of(index_ref[0], width), low_count)
        hits = jnp.concatenate(
            [
                (lane == low - first).astype(jnp.float32).astype(jnp.bfloat16)
                for first in range(0, low_count, width)
            ],
            axis=1,
        )
        found = jnp.dot(hits, held_ref[side], preferred_element_type=jnp.float32)
        for i in range(SPLIT):
            total += jnp.where(block == i, found[:, i * width : (i + 1) * width], 0.0)
    out_ref[...] = total.astype(out_ref.dtype)


def gather_pair_sums(own_index, peer_index, own_rows, peer_rows):
    count = own_index.size
    row_count, width = own_rows.shape
    tile = tile_of(count, 1024)
    low_count = row_count // SPLIT
    index_spec = pl.BlockSpec((1, 1, tile), lambda k: (k, 0, 0))
    rows_spec = pl.BlockSpec((SPLIT, low_count, width), lambda k: (0, 0, 0))
    return pl.pallas_call(
        functools.partial(gather_kernel, low_count=low_count),
        grid=(count // tile,),
        in_specs=[index_spec, index_spec, rows_spec, rows_spec],
        out_specs=pl.BlockSpec((tile, width), lambda k: (k, 0)),
        out_shape=jax.ShapeDtypeStruct((count, width), jnp.bfloat16),
        scratch_shapes=[pltpu.VMEM((2, low_count, SPLIT * width), jnp.bfloat16)],
    )(
        own_index.reshape(count // tile, 1, tile),
        peer_index.reshape(count // tile, 1, tile),
        own_rows.reshape(SPLIT, low_count, width),
        peer_rows.reshape(SPLIT, low_count, width),
    )


def on_device(owners, local_rows, grad_pooled, table, accum, parity, parity_slot):
    table_count = lax.axis_size("table")
    dp_count = lax.axis_size("dp")
    chip_count = table_count // 2
    bag_count = owners.shape[0]
    row_count, row_width = table.shape
    parity_count = parity.shape[0]
    core = lax.axis_index("table") % 2
    dp_index = lax.axis_index("dp")
    pairs = [(i, i ^ 1) for i in range(table_count)]
    same_core = [list(range(c, table_count, 2)) for c in range(2)]

    def swap_cores(values):
        return lax.ppermute(values, "table", pairs)

    def exchange(values):
        return lax.all_to_all(
            values, "table", split_axis=0, concat_axis=0, axis_index_groups=same_core, tiled=True
        )

    sent_grads = jnp.broadcast_to(grad_pooled[None], (chip_count, bag_count, row_width))
    own_grads = exchange(sent_grads)
    devices = jnp.arange(table_count, dtype=jnp.int32)[:, None, None]
    named = owners.T[None] == devices.reshape(table_count, 1, 1)
    requests = jnp.max(jnp.where(named, local_rows.T[None], -1), axis=1)
    asked = exchange(requests.reshape(chip_count, 2, bag_count))
    asked_own = jnp.where(core == 0, asked[:, 0], asked[:, 1])
    asked_other = jnp.where(core == 0, asked[:, 1], asked[:, 0])
    asked_by_peer = swap_cores(asked_other)
    table_half = table.astype(jnp.bfloat16)
    peer_half = swap_cores(table_half)
    peer_slot = swap_cores(parity_slot)

    fetched = gather_pair_sums(asked_own, asked_other, table_half, peer_half)

    peer_grads = swap_cores(own_grads)
    all_grads = jnp.concatenate([own_grads, peer_grads], axis=0).reshape(-1, row_width)
    all_asked = jnp.concatenate([asked_own, asked_by_peer], axis=0).reshape(-1)
    total = segment_sums(all_asked, all_grads, row_count)
    distance = 1
    while distance < dp_count:
        step_pairs = [(i, i ^ distance) for i in range(dp_count)]
        total = total.astype(jnp.bfloat16)
        total = total.astype(jnp.float32) + lax.ppermute(total, "dp", step_pairs).astype(jnp.float32)
        distance *= 2
    row_grads = total.astype(jnp.float32)

    returned = exchange(fetched.reshape(chip_count, bag_count, row_width))
    pooled = jnp.sum(returned.astype(jnp.float32), axis=0).astype(jnp.bfloat16)

    new_accum = accum + jnp.mean(row_grads * row_grads, axis=1)
    new_table = table - LEARN * row_grads / jnp.sqrt(new_accum + EPSILON)[:, None]
    row_delta = (new_table - table).astype(jnp.bfloat16)

    part_count = parity_count // dp_count
    slots = jnp.concatenate([parity_slot, peer_slot])
    holder, offset = slots // parity_count, slots % parity_count
    mine = (holder % 2 == core) & (offset // part_count == dp_index)
    target = jnp.where(mine, holder // 2 * part_count + offset % part_count, -1)
    deltas = jnp.concatenate([row_delta, swap_cores(row_delta)], axis=0)
    changes = segment_sums(target, deltas, chip_count * part_count)
    arrived = exchange(changes.reshape(chip_count, part_count, row_width))
    part = jnp.sum(arrived.astype(jnp.float32), axis=0).astype(jnp.bfloat16)
    if dp_count == 2:
        other = lax.ppermute(part, "dp", [(0, 1), (1, 0)])
        parts = jnp.where(dp_index == 0, jnp.stack([part, other]), jnp.stack([other, part]))
    else:
        parts = lax.all_gather(part, "dp", axis=0)
    new_parity = parity + parts.reshape(parity_count, row_width).astype(jnp.float32)
    return (pooled, new_table, new_accum, new_parity)


def solution(mesh):
    in_specs = (
        P(("table", "dp"), None),
        P(("table", "dp"), None),
        P(("table", "dp"), None),
        P("table", None),
        P("table"),
        P("table", None),
        P("table"),
    )
    out_specs = (P(("table", "dp"), None), P("table", None), P("table"), P("table", None))
    return jax.shard_map(
        on_device, mesh=mesh, in_specs=in_specs, out_specs=out_specs, check_vma=False
    )
```

time: 314 us -> 160 us (0.51); the launches traced: 308 us -> 159 us
  other arithmetic: 82.5 us -> 13.8 us
  local copies, waits for them, and re-layouts: 68.8 us -> 4.01 us
  waiting for transfers between devices: 98.8 us -> 58.9 us
  Pallas kernels: 0 us -> 33.2 us
  blocking collectives: 4.35 us -> 32.9 us
  starting transfers between devices: 39.2 us -> 15.8 us
  between operations: 14.3 us -> 0.76 us
    scatter-add x1 -> x0, other arithmetic: 45.7 us -> none  [on_device(): jax.ops.segment_sum(incoming.reshape(slot_count, row_width).astype(jnp.fl...]
    gather x2 -> x0, local copies, waits for them, and re-layouts: 36.2 us -> none  [the longest x1 24 us: on_device(): jnp.take(table_half, jnp.minimum(asked_rows, row_count - 1), axis=0)]
    all_to_all x4 -> x3, waiting for transfers between devices: 64 us -> 28.7 us  [exchange(): lax.all_to_all(values, 'table', split_axis=0, concat_axis=0, axis_index_g...]
    all_gather x1 -> x0, waiting for transfers between devices: 34.7 us -> none  [on_device(): lax.all_gather(fresh_rows, 'dp', axis=0, tiled=True)]
    pallas_call x0 -> x3, Pallas kernels: none -> 33.2 us  [the longest x2 20.7 us: segment_sums(): pl.pallas_call(functools.partial(segment_kernel, low_count=low_count), gr...]
    all_to_all x0 -> x1, blocking collectives: none -> 32.9 us  [exchange(): lax.all_to_all(values, 'table', split_axis=0, concat_axis=0, axis_index_g...]
    ppermute x0 -> x7, waiting for transfers between devices: none -> 30.2 us  [the longest x1 23.9 us: on_device(): lax.ppermute(total, 'dp', step_pairs).astype(jnp.float32)]
    scatter x2 -> x0, local copies, waits for them, and re-layouts: 28.5 us -> none  [the longest x1 16.1 us: on_device(): jnp.full((slot_count,), row_count, jnp.int32).at[position].set(local_flat)]
  transfers between devices with their start and end apart: 6 -> 10, of which waited for: 3 -> 7; matrix products, arithmetic and copies ran while one was open for 24% -> 4% of each run, Pallas kernels for 0% -> 13%
where the time goes in v1:
time: 160 us; the launch traced here: 159 us
  waiting for transfers between devices  58.9 us (37%)
  Pallas kernels  33.2 us (21%)
  blocking collectives  32.9 us (21%)
  starting transfers between devices  15.8 us (10%)
  other arithmetic  13.8 us (9%)
  local copies, waits for them, and re-layouts  4.01 us (3%)
    all_to_all x1, blocking collectives, exchange(): lax.all_to_all(values, 'table', split_axis=0, concat_axis=0, axis_index_g...  32.9 us
    all_to_all x3, waiting for transfers between devices, exchange(): lax.all_to_all(values, 'table', split_axis=0, concat_axis=0, axis_index_g...  28.7 us
    ppermute x1, waiting for transfers between devices, on_device(): lax.ppermute(total, 'dp', step_pairs).astype(jnp.float32)  23.9 us
    pallas_call x2, Pallas kernels, segment_sums(): pl.pallas_call(functools.partial(segment_kernel, low_count=low_count), gr...  20.7 us
    pallas_call x1, Pallas kernels, gather_pair_sums(): pl.pallas_call(functools.partial(gather_kernel, low_count=low_count), gri...  12.4 us
    all_to_all x3, starting transfers between devices, exchange(): lax.all_to_all(values, 'table', split_axis=0, concat_axis=0, axis_index_g...  12 us
    convert_element_type x1, other arithmetic, on_device(): row_delta = (new_table - table).astype(jnp.bfloat16)  3.99 us
    ppermute x5, waiting for transfers between devices, swap_cores(): return lax.ppermute(values, 'table', pairs)  3.44 us
  transfers between devices with their start and end apart: 10, of which 7 were waited for; matrix products, arithmetic and copies ran while one was open for 4% of the time, Pallas kernels for 13%

profile of v1, /device:TPU:0, one launch (start us, length us, event | category | flops | bytes accessed | tf_op | source)
XLA Modules:
  0.0 159.2 jit_solution(16636499140422088578)
XLA Ops:
  0.7 1.1 broadcast_in_dim.26
  1.7 32.9 %all_to_all.20 = bf16[8,512,128]{2,1,0:T(8,128)(2,1)S(1)} all-to-all(bf16[8,512,128]{2,1,0:T(8,128)(2,1)S(1)} %broadcast_in_dim.26), channel_id=1, replica_groups={{0,4,8,12,16,20,24,28},{2,6,10,14,18,22,26,30},{1,5,9,13,17,21,25,29},{..., dimensions={0} | all-to-all | bytes 2097152 | tf_op jit(solution)/shard_map/all_to_all | solution.py:144
  35.3 3.6 %all-to-all-start = ((s32[8,2,512]{2,1,0:T(2,128)}), s32[8,2,512]{2,1,0:T(2,128)S(1)}, u32[]{:S(2)}, u32[]{:S(2)}) async-start(s32[8,2,512]{2,1,0:T(2,128)} %reshape.414), calls=%async_computation | async-start | bytes 65536 | tf_op jit(solution)/shard_map/all_to_all | solution.py:144
  38.9 6.7 %all-to-all-done = s32[8,2,512]{2,1,0:T(2,128)S(1)} async-done(((s32[8,2,512]{2,1,0:T(2,128)}), s32[8,2,512]{2,1,0:T(2,128)S(1)}, u32[]{:S(2)}, u32[]{:S(2)}) %all-to-all-start) | async-done | bytes 32800 | tf_op jit(solution)/shard_map/all_to_all | solution.py:144
  45.8 1.2 collective-permute-done.1
  47.6 1.5 pad_maximum_fusion
  49.1 12.7 %shard_map.103 = bf16[4,1024,128]{2,1,0:T(8,128)(2,1)} custom-call(s32[4,1,2048]{2,1,0:T(1,128)} %reshape_reshape.6.index_ref, bf16[8192,128]{1,0:T(8,128)(2,1)} %bitcast.26), custom_call_target="tpu_custom_call" | custom-call | tf_op jit(solution)/shard_map/pallas_call | solution.py:66
  61.8 1.5 collective-permute-start.3
  63.3 23.9 %collective-permute-done.3 = bf16[4096,128]{1,0:T(8,128)(2,1)S(1)} collective-permute-done((bf16[4096,128]{1,0:T(8,128)(2,1)}, bf16[4096,128]{1,0:T(8,128)(2,1)S(1)}, u32[]{:S(2)}, u32[]{:S(2)}) %collective-permute-start.3) | collective-permute-done | bytes 1048608 | tf_op jit(solution)/shard_map/ppermute | solution.py:171
  87.3 1.8 %multiply_reduce_fusion = f32[4096]{0:T(1024)S(1)} fusion(bf16[4096,128]{1,0:T(8,128)(2,1)S(1)} %collective-permute-done.3, bf16[4,1024,128]{2,1,0:T(8,128)(2,1)} %shard_map.103), kind=kLoop, calls=%fused_computation.4 | loop fusion | flops 2617344 | bytes 2113536 | tf_op jit(solution)/shard_map/reduce_sum | solution.py:178
  89.7 4.0 %subtract_convert_fusion = (bf16[4096,128]{1,0:T(8,128)(2,1)S(1)}, f32[4096,128]{1,0:T(8,128)}, bf16[4096,128]{1,0:T(8,128)(2,1)S(1)}) fusion(f32[4096,128]{1,0:T(8,128)} %param.10, f32[4096]{0:T(1024)S(1)} %get-tuple-element.6, bf16[4096,128]{1,0:T(8,128)(2,1)S(1)} %collective-permute-done.3, bf16[4,1024,128]{2,1,0:T(8,128)(2,1)S(1)} %copy-done), kind=kLoop, calls=%fused_computation.2 | loop fusion | flops 4718592 | bytes 8404992 | tf_op jit(solution)/shard_map/convert_element_type | solution.py:180
  94.2 2.3 %collective-permute-done.4 = s32[4096]{0:T(1024)S(1)} collective-permute-done((s32[4096]{0:T(1024)S(1)}, s32[4096]{0:T(1024)S(1)}, u32[]{:S(2)}, u32[]{:S(2)}) %collective-permute-start.4) | collective-permute-done | bytes 16416 | tf_op jit(solution)/shard_map/ppermute | solution.py:141
  96.5 1.3 and_select_fusion.2.index_ref
  98.0 2.7 %pad_maximum_fusion.1.rows_ref = bf16[8192,128]{1,0:T(8,128)(2,1)} fusion(bf16[4096,128]{1,0:T(8,128)(2,1)} %collective-permute-done.5, bf16[4096,128]{1,0:T(8,128)(2,1)S(1)} %get-tuple-element.4), kind=kLoop, calls=%fused_computation.1 | loop fusion | flops 4194304 | bytes 4194304 | tf_op jit(solution)/shard_map/concatenate | solution.py:187
  100.7 8.0 %shard_map.104 = bf16[4,512,128]{2,1,0:T(8,128)(2,1)} custom-call(s32[4,1,2048]{2,1,0:T(1,128)} %and_select_fusion.2.index_ref, bf16[8192,128]{1,0:T(8,128)(2,1)} %pad_maximum_fusion.1.rows_ref), custom_call_target="tpu_custom_call" | custom-call | tf_op jit(solution)/shard_map/pallas_call | solution.py:66
  108.7 3.5 %all-to-all-start.3 = ((bf16[8,256,128]{2,1,0:T(8,128)(2,1)}), bf16[8,256,128]{2,1,0:T(8,128)(2,1)S(1)}, u32[]{:S(2)}, u32[]{:S(2)}) async-start(bf16[8,256,128]{2,1,0:T(8,128)(2,1)} %bitcast.29), calls=%async_computation.3 | async-start | bytes 1048576 | tf_op jit(solution)/shard_map/all_to_all | solution.py:144
  112.8 1.0 copy-done.2
  113.8 12.4 %shard_map.102 = bf16[4096,128]{1,0:T(8,128)(2,1)} custom-call(s32[4,1,1024]{2,1,0:T(1,128)} %select_n.141.own_index_ref, s32[4,1,1024]{2,1,0:T(1,128)} %bitcast.32, bf16[4,1024,128]{2,1,0:T(8,128)(2,1)} %bitcast.28, bf16[4,1024,128]{2,1,0:T(8,128)(2,1)} %bitcast.30), custom_call_target="tpu_custom_call" | custom-call | tf_op jit(solution)/shard_map/pallas_call | solution.py:113
  126.3 1.1 all-to-all-done.3
  127.4 4.9 %all-to-all-start.1 = ((bf16[8,512,128]{2,1,0:T(8,128)(2,1)}), bf16[8,512,128]{2,1,0:T(8,128)(2,1)S(1)}, u32[]{:S(2)}, u32[]{:S(2)}) async-start(bf16[8,512,128]{2,1,0:T(8,128)(2,1)} %bitcast.27), calls=%async_computation.1 | async-start | bytes 2097152 | tf_op jit(solution)/shard_map/all_to_all | solution.py:144
  132.4 1.6 collective-permute-start.6
  134.0 2.8 %collective-permute-done.6 = bf16[256,128]{1,0:T(8,128)(2,1)S(1)} collective-permute-done((bf16[256,128]{1,0:T(8,128)(2,1)S(1)}, bf16[256,128]{1,0:T(8,128)(2,1)S(1)}, u32[]{:S(2)}, u32[]{:S(2)}) %collective-permute-start.6) | collective-permute-done | bytes 65568 | tf_op jit(solution)/shard_map/ppermute | solution.py:192
  137.5 20.9 %all-to-all-done.1 = bf16[8,512,128]{2,1,0:T(8,128)(2,1)S(1)} async-done(((bf16[8,512,128]{2,1,0:T(8,128)(2,1)}), bf16[8,512,128]{2,1,0:T(8,128)(2,1)S(1)}, u32[]{:S(2)}, u32[]{:S(2)}) %all-to-all-start.1) | async-done | bytes 1048608 | tf_op jit(solution)/shard_map/all_to_all | solution.py:144
  158.4 0.8 reduce_sum.33
  (37 shorter events, 4.3 us)
Async XLA Ops:
  0.6 34.0 %copy-start.5 = (s32[512,8]{0,1:T(8,128)S(1)}, s32[512,8]{0,1:T(8,128)}, u32[]{:S(2)}) copy-start(s32[512,8]{0,1:T(8,128)} %param.8) | copy-start | bytes 49156
  0.6 33.9 %copy-start.6 = (s32[512,8]{0,1:T(8,128)S(1)}, s32[512,8]{0,1:T(8,128)}, u32[]{:S(2)}) copy-start(s32[512,8]{0,1:T(8,128)} %param.7) | copy-start | bytes 49156
  34.6 13.0 %collective-permute-start.2 = (bf16[8,512,128]{2,1,0:T(8,128)(2,1)S(1)}, bf16[8,512,128]{2,1,0:T(8,128)(2,1)S(1)}, u32[]{:S(2)}, u32[]{:S(2)}) collective-permute-start(bf16[8,512,128]{2,1,0:T(8,128)(2,1)S(1)} %all_to_all.20), channel_id=1, source_target_pairs={{0,2},{2,0},{4,6},{6,4},{8,10},{10,8},{12,14},{14,12},{16,18},{18,... | collective-permute-start | bytes 3145736 | tf_op jit(solution)/shard_map/ppermute | solution.py:141
  35.3 10.3 %all-to-all-start = ((s32[8,2,512]{2,1,0:T(2,128)}), s32[8,2,512]{2,1,0:T(2,128)S(1)}, u32[]{:S(2)}, u32[]{:S(2)}) async-start(s32[8,2,512]{2,1,0:T(2,128)} %reshape.414), calls=%async_computation | async-start | bytes 65536 | tf_op jit(solution)/shard_map/all_to_all | solution.py:144
  45.7 3.4 %copy-start.4 = (s32[8,1,512]{2,1,0:T(1,128)}, s32[8,1,512]{2,1,0:T(1,128)S(1)}, u32[]{:S(2)}) copy-start(s32[8,1,512]{2,1,0:T(1,128)S(1)} %get-tuple-element.9) | copy-start | bytes 49156
  45.7 1.2 collective-permute-start.1
  49.1 40.0 %copy-start.7 = (f32[4096]{0:T(1024)S(1)}, f32[4096]{0:T(1024)}, u32[]{:S(2)}) copy-start(f32[4096]{0:T(1024)} %param.11) | copy-start | bytes 49156
  61.8 27.9 %copy-start = (bf16[4,1024,128]{2,1,0:T(8,128)(2,1)S(1)}, bf16[4,1024,128]{2,1,0:T(8,128)(2,1)}, u32[]{:S(2)}) copy-start(bf16[4,1024,128]{2,1,0:T(8,128)(2,1)} %shard_map.103) | copy-start | bytes 3145732
  61.8 25.4 %collective-permute-start.3 = (bf16[4096,128]{1,0:T(8,128)(2,1)}, bf16[4096,128]{1,0:T(8,128)(2,1)S(1)}, u32[]{:S(2)}, u32[]{:S(2)}) collective-permute-start(bf16[4096,128]{1,0:T(8,128)(2,1)} %bitcast.25), channel_id=1, source_target_pairs={{0,1},{1,0},{2,3},{3,2},{4,5},{5,4},{6,7},{7,6},{8,9},{9,8},{10,11... | collective-permute-start | bytes 3145736 | tf_op jit(solution)/shard_map/ppermute | solution.py:171
  89.7 4.0 %copy-start.8 = (s32[4096]{0:T(1024)S(1)}, s32[4096]{0:T(1024)}, u32[]{:S(2)}) copy-start(s32[4096]{0:T(1024)} %param.13) | copy-start | bytes 49156
  93.7 7.0 %copy-start.1 = (bf16[4096,128]{1,0:T(8,128)(2,1)}, bf16[4096,128]{1,0:T(8,128)(2,1)S(1)}, u32[]{:S(2)}) copy-start(bf16[4096,128]{1,0:T(8,128)(2,1)S(1)} %get-tuple-element.8) | copy-start | bytes 3145732
  93.7 4.3 %collective-permute-start.5 = (bf16[4096,128]{1,0:T(8,128)(2,1)S(1)}, bf16[4096,128]{1,0:T(8,128)(2,1)}, u32[]{:S(2)}, u32[]{:S(2)}) collective-permute-start(bf16[4096,128]{1,0:T(8,128)(2,1)S(1)} %get-tuple-element.4), channel_id=1, source_target_pairs={{0,2},{2,0},{4,6},{6,4},{8,10},{10,8},{12,14},{14,12},{16,18},{18,... | collective-permute-start | bytes 3145736 | tf_op jit(solution)/shard_map/ppermute | solution.py:141
  93.7 2.8 %collective-permute-start.4 = (s32[4096]{0:T(1024)S(1)}, s32[4096]{0:T(1024)S(1)}, u32[]{:S(2)}, u32[]{:S(2)}) collective-permute-start(s32[4096]{0:T(1024)S(1)} %copy-done.8), channel_id=1, source_target_pairs={{0,2},{2,0},{4,6},{6,4},{8,10},{10,8},{12,14},{14,12},{16,18},{18,... | collective-permute-start | bytes 49160 | tf_op jit(solution)/shard_map/ppermute | solution.py:141
  97.8 15.0 %collective-permute-start = (bf16[4096,128]{1,0:T(8,128)(2,1)S(1)}, bf16[4096,128]{1,0:T(8,128)(2,1)S(1)}, u32[]{:S(2)}, u32[]{:S(2)}) collective-permute-start(bf16[4096,128]{1,0:T(8,128)(2,1)S(1)} %get-tuple-element.8), channel_id=1, source_target_pairs={{0,2},{2,0},{4,6},{6,4},{8,10},{10,8},{12,14},{14,12},{16,18},{18,... | collective-permute-start | bytes 3145736 | tf_op jit(solution)/shard_map/ppermute | solution.py:141
  108.7 18.7 %all-to-all-start.3 = ((bf16[8,256,128]{2,1,0:T(8,128)(2,1)}), bf16[8,256,128]{2,1,0:T(8,128)(2,1)S(1)}, u32[]{:S(2)}, u32[]{:S(2)}) async-start(bf16[8,256,128]{2,1,0:T(8,128)(2,1)} %bitcast.29), calls=%async_computation.3 | async-start | bytes 1048576 | tf_op jit(solution)/shard_map/all_to_all | solution.py:144
  112.8 1.0 copy-start.2
  126.3 10.5 %copy-start.3 = (f32[512,128]{1,0:T(8,128)S(1)}, f32[512,128]{1,0:T(8,128)}, u32[]{:S(2)}) copy-start(f32[512,128]{1,0:T(8,128)} %param.12) | copy-start | bytes 786436
  127.4 31.0 %all-to-all-start.1 = ((bf16[8,512,128]{2,1,0:T(8,128)(2,1)}), bf16[8,512,128]{2,1,0:T(8,128)(2,1)S(1)}, u32[]{:S(2)}, u32[]{:S(2)}) async-start(bf16[8,512,128]{2,1,0:T(8,128)(2,1)} %bitcast.27), calls=%async_computation.1 | async-start | bytes 2097152 | tf_op jit(solution)/shard_map/all_to_all | solution.py:144
  132.4 4.3 %collective-permute-start.6 = (bf16[256,128]{1,0:T(8,128)(2,1)S(1)}, bf16[256,128]{1,0:T(8,128)(2,1)S(1)}, u32[]{:S(2)}, u32[]{:S(2)}) collective-permute-start(bf16[256,128]{1,0:T(8,128)(2,1)S(1)} %reduce_sum.35), channel_id=1, source_target_pairs={{0,1},{1,0},{2,3},{3,2},{4,5},{5,4},{6,7},{7,6},{8,9},{9,8},{10,11... | collective-permute-start | bytes 196616 | tf_op jit(solution)/shard_map/ppermute | solution.py:192

commit v2 on v1

v2 whole, which is shorter than its diff:
```python
import functools
import jax
import jax.numpy as jnp
from jax import lax
from jax.experimental import pallas as pl
from jax.experimental.pallas import tpu as pltpu
from jax.sharding import PartitionSpec as P

LEARN = 0.5
EPSILON = 1e-06
SPLIT = 4
PARTS = 2


def column_of(row, lanes):
    return jnp.broadcast_to(row, (lanes, row.shape[1])).T


def split_index(index, low_count):
    bits = low_count.bit_length() - 1
    return lax.shift_right_arithmetic(index, bits), lax.bitwise_and(index, low_count - 1)


def tile_of(count, most):
    tile = most
    while count % tile:
        tile //= 2
    return tile


def lane_row(ref, first, count):
    return jnp.concatenate([ref[pl.ds(first + i, 1), :] for i in range(count)], axis=1)


def segment_kernel(*refs, low_count, index_rows, base, sides, start_given):
    index_refs, refs = refs[:sides], refs[sides:]
    row_refs, refs = refs[:sides], refs[sides:]
    out_ref, total_ref = refs[-2:]
    step = pl.program_id(0)
    width = row_refs[0].shape[1]
    index = jnp.concatenate(
        [lane_row(ref, step * index_rows, index_rows) for ref in index_refs], axis=1
    )
    block, low = split_index(index - base, low_count)
    low = jnp.where((block < 0) | (block >= SPLIT), -1, low)
    hits = (
        (lax.broadcasted_iota(jnp.int32, (low_count, index.shape[1]), 0) == low)
        .astype(jnp.float32)
        .astype(jnp.bfloat16)
    )
    block_column = column_of(block, width)
    rows = jnp.concatenate([ref[...] for ref in row_refs], axis=0).astype(jnp.float32)
    spread = jnp.concatenate(
        [jnp.where(block_column == i, rows, 0.0).astype(jnp.bfloat16) for i in range(SPLIT)], axis=1
    )
    part = jnp.dot(hits, spread, preferred_element_type=jnp.float32)

    @pl.when(step == 0)
    def _():
        if start_given:
            for i in range(SPLIT):
                lanes = slice(i * width, (i + 1) * width)
                total_ref[:, lanes] = part[:, lanes] + refs[0][i]
        else:
            total_ref[...] = part

    @pl.when(step > 0)
    def _():
        total_ref[...] += part

    @pl.when(step == pl.num_programs(0) - 1)
    def _():
        for i in range(SPLIT):
            out_ref[i] = total_ref[:, i * width : (i + 1) * width].astype(out_ref.dtype)


def segment_sums(indices, rows, base, segment_count, dtype, start=None):
    sides = len(indices)
    index_shape = indices[0].shape
    width = rows[0].shape[1]
    low_count = segment_count // SPLIT
    index_rows = tile_of(index_shape[0], max(1, 2048 // sides // index_shape[1]))
    tile = index_rows * index_shape[1]
    block = pl.BlockSpec((SPLIT, low_count, width), lambda k: (0, 0, 0))
    given = [] if start is None else [start]
    return pl.pallas_call(
        functools.partial(
            segment_kernel,
            low_count=low_count,
            index_rows=index_rows,
            base=base,
            sides=sides,
            start_given=bool(given),
        ),
        grid=(index_shape[0] // index_rows,),
        in_specs=[pl.BlockSpec(index_shape, lambda k: (0, 0))] * sides
        + [pl.BlockSpec((tile, width), lambda k: (k, 0))] * sides
        + [block] * len(given),
        out_specs=block,
        out_shape=jax.ShapeDtypeStruct((SPLIT, low_count, width), dtype),
        scratch_shapes=[pltpu.VMEM((low_count, SPLIT * width), jnp.float32)],
    )(*indices, *rows, *given)


def gather_kernel(own_index_ref, peer_index_ref, own_ref, peer_ref, out_ref, held_ref, *, low_count, index_rows):
    width = out_ref.shape[1]
    step = pl.program_id(0)

    @pl.when(step == 0)
    def _():
        for i in range(SPLIT):
            held_ref[0, :, i * width : (i + 1) * width] = own_ref[i]
            held_ref[1, :, i * width : (i + 1) * width] = peer_ref[i]

    total = jnp.zeros(out_ref.shape, jnp.float32)
    lane = lax.broadcasted_iota(jnp.int32, out_ref.shape, 1)
    for side, index_ref in enumerate((own_index_ref, peer_index_ref)):
        index = lane_row(index_ref, step * index_rows, index_rows)
        block, low = split_index(column_of(index, width), low_count)
        hits = jnp.concatenate(
            [
                (lane == low - first).astype(jnp.float32).astype(jnp.bfloat16)
                for first in range(0, low_count, width)
            ],
            axis=1,
        )
        found = jnp.dot(hits, held_ref[side], preferred_element_type=jnp.float32)
        for i in range(SPLIT):
            total += jnp.where(block == i, found[:, i * width : (i + 1) * width], 0.0)
    out_ref[...] = total.astype(out_ref.dtype)


def gather_pair_sums(own_index, peer_index, own_rows, peer_rows):
    row_count, width = own_rows.shape
    low_count = row_count // SPLIT
    index_rows = tile_of(own_index.shape[0], max(1, 1024 // own_index.shape[1]))
    tile = index_rows * own_index.shape[1]
    index_spec = pl.BlockSpec(own_index.shape, lambda k: (0, 0))
    rows_spec = pl.BlockSpec((SPLIT, low_count, width), lambda k: (0, 0, 0))
    return pl.pallas_call(
        functools.partial(gather_kernel, low_count=low_count, index_rows=index_rows),
        grid=(own_index.shape[0] // index_rows,),
        in_specs=[index_spec, index_spec, rows_spec, rows_spec],
        out_specs=pl.BlockSpec((tile, width), lambda k: (k, 0)),
        out_shape=jax.ShapeDtypeStruct((own_index.size, width), jnp.bfloat16),
        scratch_shapes=[pltpu.VMEM((2, low_count, SPLIT * width), jnp.bfloat16)],
    )(
        own_index,
        peer_index,
        own_rows.reshape(SPLIT, low_count, width),
        peer_rows.reshape(SPLIT, low_count, width),
    )


def update_kernel(own_ref, other_ref, table_ref, accum_ref, *refs, first_line):
    new_table_ref, new_accum_ref, delta_ref = refs[-3:]
    rows, width = table_ref.shape
    lines = rows // width
    step = pl.program_id(0)
    for j in range(lines):
        at = slice(j * width, (j + 1) * width)
        grads = own_ref[at, :].astype(jnp.float32) + other_ref[at, :].astype(jnp.float32)
        old_accum = column_of(accum_ref[pl.ds(first_line + step * lines + j, 1), :], width)
        fresh_accum = old_accum + jnp.mean(grads * grads, axis=1, keepdims=True)
        old_rows = table_ref[at, :]
        fresh_rows = old_rows - LEARN * grads / jnp.sqrt(fresh_accum + EPSILON)
        new_table_ref[at, :] = fresh_rows
        delta_ref[at, :] = (fresh_rows - old_rows).astype(jnp.bfloat16)
        new_accum_ref[pl.ds(step * lines + j, 1), :] = fresh_accum.T[0:1, :]


def update(own, other, table, accum, part, unfinished):
    _, width = table.shape
    part_rows = own.shape[0]
    tile = tile_of(part_rows, 512)
    steps = part_rows // tile
    rows_spec = pl.BlockSpec((tile, width), lambda k: (k, 0))
    table_spec = pl.BlockSpec((tile, width), lambda k: (part * steps + k, 0))
    part_lines = part_rows // width
    given = [] if unfinished is None else [unfinished]
    return pl.pallas_call(
        functools.partial(update_kernel, first_line=part * part_lines),
        grid=(steps,),
        in_specs=[rows_spec, rows_spec, table_spec, pl.BlockSpec(accum.shape, lambda k: (0, 0))]
        + [pl.BlockSpec(memory_space=pl.ANY)] * len(given),
        out_specs=[table_spec, pl.BlockSpec((part_lines, width), lambda k: (0, 0)), rows_spec],
        out_shape=[
            jax.ShapeDtypeStruct(table.shape, jnp.float32),
            jax.ShapeDtypeStruct((part_lines, width), jnp.float32),
            jax.ShapeDtypeStruct((part_rows, width), jnp.bfloat16),
        ],
        input_output_aliases={4: 0} if given else {},
    )(own, other, table, accum, *given)


def on_device(owners, local_rows, grad_pooled, table, accum, parity, parity_slot):
    table_count = lax.axis_size("table")
    dp_count = lax.axis_size("dp")
    chip_count = table_count // 2
    bag_count = owners.shape[0]
    row_count, row_width = table.shape
    parity_count = parity.shape[0]
    core = lax.axis_index("table") % 2
    dp_index = lax.axis_index("dp")
    pairs = [(i, i ^ 1) for i in range(table_count)]
    same_core = [list(range(c, table_count, 2)) for c in range(2)]

    def swap_cores(values):
        return lax.ppermute(values, "table", pairs)

    def exchange(values):
        return lax.all_to_all(
            values, "table", split_axis=0, concat_axis=0, axis_index_groups=same_core, tiled=True
        )

    half = table_count // 2
    far_grads = lax.ppermute(grad_pooled, "table", [(i, (i + half) % table_count) for i in range(table_count)])
    devices = jnp.arange(table_count, dtype=jnp.int32)[:, None, None]
    requests = jnp.max(jnp.where(owners.T[None] == devices, local_rows.T[None], -1), axis=1)
    asked = exchange(requests.reshape(chip_count, 2, bag_count))
    asked_own = jnp.where(core == 0, asked[:, 0], asked[:, 1])
    asked_other = jnp.where(core == 0, asked[:, 1], asked[:, 0])
    asked_by_peer = swap_cores(asked_other)
    table_half = table.astype(jnp.bfloat16)
    peer_half = swap_cores(table_half)

    part_count = parity_count // dp_count

    def target_of(slot):
        holder, offset = slot // parity_count, slot % parity_count
        mine = (holder % 2 == core) & (offset // part_count == dp_index)
        target = jnp.where(mine, holder // 2 * part_count + offset % part_count, -1)
        return target.reshape(PARTS, -1, 4 * row_width)

    own_target = target_of(parity_slot)
    peer_target = target_of(swap_cores(parity_slot))

    fetched = gather_pair_sums(asked_own, asked_other, table_half, peer_half)

    upper = lax.axis_index("table") >= half
    two_grads = jnp.where(
        upper, jnp.stack([far_grads, grad_pooled]), jnp.stack([grad_pooled, far_grads])
    )
    near = [list(range(h + c, h + half, 2)) for h in (0, half) for c in range(2)]
    own_grads = lax.all_to_all(
        jnp.broadcast_to(two_grads[None], (chip_count // 2,) + two_grads.shape),
        "table", split_axis=0, concat_axis=0, axis_index_groups=near, tiled=True,
    )

    def in_source_order(index):
        index = index.reshape(2, chip_count // 2, bag_count)
        return jnp.swapaxes(index, 0, 1).reshape(chip_count, bag_count)

    named_own, named_by_peer = in_source_order(asked_own), in_source_order(asked_by_peer)
    peer_grads = swap_cores(own_grads)
    grads = [own_grads.reshape(-1, row_width), peer_grads.reshape(-1, row_width)]
    part_rows = row_count // PARTS
    halves = []
    for part in range(PARTS):
        mine = segment_sums(
            [named_own, named_by_peer], grads, part * part_rows, part_rows, jnp.bfloat16
        ).reshape(part_rows, row_width)
        distance = 1
        other = lax.ppermute(mine, "dp", [(i, i ^ 1) for i in range(dp_count)])
        while 2 * distance < dp_count:
            distance *= 2
            mine = (mine.astype(jnp.float32) + other.astype(jnp.float32)).astype(jnp.bfloat16)
            other = lax.ppermute(mine, "dp", [(i, i ^ distance) for i in range(dp_count)])
        halves.append((mine, other))

    returned = exchange(fetched.reshape(chip_count, bag_count, row_width))

    new_table, accums, changes = None, [], None
    accum_lines = accum.reshape(-1, row_width)
    for part, (mine, other) in enumerate(halves):
        new_table, part_accum, delta = update(mine, other, table, accum_lines, part, new_table)
        accums.append(part_accum)
        peer_delta = swap_cores(delta)
        changes = segment_sums(
            [own_target[part], peer_target[part]],
            [delta, peer_delta],
            0,
            chip_count * part_count,
            jnp.bfloat16 if part == PARTS - 1 else jnp.float32,
            changes,
        )
    new_accum = jnp.concatenate(accums, axis=0).reshape(row_count)

    arrived = exchange(changes.reshape(chip_count, part_count, row_width))
    pooled = jnp.sum(returned.astype(jnp.float32), axis=0).astype(jnp.bfloat16)
    part = jnp.sum(arrived.astype(jnp.float32), axis=0).astype(jnp.bfloat16)
    if dp_count == 2:
        other = lax.ppermute(part, "dp", [(0, 1), (1, 0)])
        parts = jnp.where(dp_index == 0, jnp.stack([part, other]), jnp.stack([other, part]))
    else:
        parts = lax.all_gather(part, "dp", axis=0)
    new_parity = parity + parts.reshape(parity_count, row_width).astype(jnp.float32)
    return (pooled, new_table, new_accum, new_parity)


def solution(mesh):
    in_specs = (
        P(("table", "dp"), None),
        P(("table", "dp"), None),
        P(("table", "dp"), None),
        P("table", None),
        P("table"),
        P("table", None),
        P("table"),
    )
    out_specs = (P(("table", "dp"), None), P("table", None), P("table"), P("table", None))

    return jax.shard_map(on_device, mesh=mesh, in_specs=in_specs, out_specs=out_specs, check_vma=False)
```

time: 160 us -> 143 us (0.89)
  blocking collectives: 32.9 us -> 0 us
  Pallas kernels: 33.2 us -> 47.7 us
  starting transfers between devices: 15.8 us -> 26.9 us
  other arithmetic: 13.8 us -> 5.17 us
  waiting for transfers between devices: 58.9 us -> 51.5 us
  local copies, waits for them, and re-layouts: 4.01 us -> 10.7 us
    all_to_all x1 -> x0, blocking collectives: 32.9 us -> none  [exchange(): lax.all_to_all(values, 'table', split_axis=0, concat_axis=0, axis_index_g...]
    pallas_call x3 -> x7, Pallas kernels: 33.2 us -> 47.7 us  [the longest x4 26.5 us: segment_sums(): pl.pallas_call(functools.partial(segment_kernel, low_count=low_count, ind...]
    all_to_all x0 -> x1, waiting for transfers between devices: none -> 11.5 us  [on_device(): lax.all_to_all(jnp.broadcast_to(two_grads[None], (chip_count // 2,) + two...]
    all_to_all x3, waiting for transfers between devices: 28.7 us -> 20.6 us  [exchange(): lax.all_to_all(values, 'table', split_axis=0, concat_axis=0, axis_index_g...]
    ppermute x1 -> x3, waiting for transfers between devices: 23.9 us -> 16.8 us  [the longest x2 10.2 us: on_device(): other = lax.ppermute(mine, 'dp', [(i, i ^ 1) for i in range(dp_count)])]
    ppermute x1 -> x3, starting transfers between devices: 1.49 us -> 6.16 us  [the longest x1 4.13 us: on_device(): lax.ppermute(grad_pooled, 'table', [(i, (i + half) % table_count) for i i...]
    unnamed x19 -> x34, local copies, waits for them, and re-layouts: 1.04 us -> 5.23 us
    concatenate x3 -> x0, other arithmetic: 4.19 us -> none  [the longest x1 2.69 us: on_device(): deltas = jnp.concatenate([row_delta, swap_cores(row_delta)], axis=0)]
  transfers between devices with their start and end apart: 10 -> 14, of which waited for: 7 -> 8; matrix products, arithmetic and copies ran while one was open for 4% -> 5% of each run, Pallas kernels for 13% -> 33%
where the time goes in v2:
time: 143 us
  waiting for transfers between devices  51.5 us (36%)
  Pallas kernels  47.7 us (33%)
  starting transfers between devices  26.9 us (19%)
  local copies, waits for them, and re-layouts  10.7 us (7%)
  other arithmetic  5.17 us (4%)
    pallas_call x4, Pallas kernels, segment_sums(): pl.pallas_call(functools.partial(segment_kernel, low_count=low_count, ind...  26.5 us
    all_to_all x3, waiting for transfers between devices, exchange(): lax.all_to_all(values, 'table', split_axis=0, concat_axis=0, axis_index_g...  20.6 us
    all_to_all x3, starting transfers between devices, exchange(): lax.all_to_all(values, 'table', split_axis=0, concat_axis=0, axis_index_g...  15 us
    pallas_call x1, Pallas kernels, gather_pair_sums(): pl.pallas_call(functools.partial(gather_kernel, low_count=low_count, inde...  12.5 us
    all_to_all x1, waiting for transfers between devices, on_device(): lax.all_to_all(jnp.broadcast_to(two_grads[None], (chip_count // 2,) + two...  11.5 us
    ppermute x2, waiting for transfers between devices, on_device(): other = lax.ppermute(mine, 'dp', [(i, i ^ 1) for i in range(dp_count)])  10.2 us
    pallas_call x2, Pallas kernels, update(): pl.pallas_call(functools.partial(update_kernel, first_line=part * part_li...  8.64 us
    ppermute x1, waiting for transfers between devices, on_device(): lax.ppermute(grad_pooled, 'table', [(i, (i + half) % table_count) for i i...  6.52 us
  transfers between devices with their start and end apart: 14, of which 8 were waited for; matrix products, arithmetic and copies ran while one was open for 5% of the time, Pallas kernels for 33%

profile of v2, /device:TPU:0, one launch (start us, length us, event | category | flops | bytes accessed | tf_op | source)
XLA Modules:
  0.0 142.7 jit_solution(16464844091078210804)
XLA Ops:
  0.6 4.1 %collective-permute-start.2 = (bf16[512,128]{1,0:T(8,128)(2,1)}, bf16[512,128]{1,0:T(8,128)(2,1)S(1)}, u32[]{:S(2)}, u32[]{:S(2)}) collective-permute-start(bf16[512,128]{1,0:T(8,128)(2,1)} %param.9), channel_id=1, source_target_pairs={{0,16},{2,18},{4,20},{6,22},{8,24},{10,26},{12,28},{14,30},{16,0},... | collective-permute-start | bytes 393224 | tf_op jit(solution)/shard_map/ppermute | solution.py:217
  4.8 6.5 %collective-permute-done.2 = bf16[512,128]{1,0:T(8,128)(2,1)S(1)} collective-permute-done((bf16[512,128]{1,0:T(8,128)(2,1)}, bf16[512,128]{1,0:T(8,128)(2,1)S(1)}, u32[]{:S(2)}, u32[]{:S(2)}) %collective-permute-start.2) | collective-permute-done | bytes 131104 | tf_op jit(solution)/shard_map/ppermute | solution.py:217
  11.3 1.0 maximum_select_fusion
  12.3 1.1 broadcast_in_dim.26
  13.4 3.5 %all-to-all-start.2 = ((bf16[4,2,512,128]{3,2,1,0:T(8,128)(2,1)}), bf16[4,2,512,128]{3,2,1,0:T(8,128)(2,1)S(1)}, u32[]{:S(2)}, u32[]{:S(2)}) async-start(bf16[4,2,512,128]{3,2,1,0:T(8,128)(2,1)} %broadcast_in_dim.26), calls=%async_computation.2 | async-start | bytes 2097152 | tf_op jit(solution)/shard_map/all_to_all | solution.py:245
  17.0 1.1 convert_element_type.13
  18.8 11.5 %all-to-all-done.2 = bf16[4,2,512,128]{3,2,1,0:T(8,128)(2,1)S(1)} async-done(((bf16[4,2,512,128]{3,2,1,0:T(8,128)(2,1)}), bf16[4,2,512,128]{3,2,1,0:T(8,128)(2,1)S(1)}, u32[]{:S(2)}, u32[]{:S(2)}) %all-to-all-start.2) | async-done | bytes 1048608 | tf_op jit(solution)/shard_map/all_to_all | solution.py:245
  30.3 5.4 %all-to-all-start = ((s32[8,2,512]{2,1,0:T(2,128)}), s32[8,2,512]{2,1,0:T(2,128)S(1)}, u32[]{:S(2)}, u32[]{:S(2)}) async-start(s32[8,2,512]{2,1,0:T(2,128)} %reshape.143), calls=%async_computation | async-start | bytes 65536 | tf_op jit(solution)/shard_map/all_to_all | solution.py:212
  35.8 6.7 %all-to-all-done = s32[8,2,512]{2,1,0:T(2,128)S(1)} async-done(((s32[8,2,512]{2,1,0:T(2,128)}), s32[8,2,512]{2,1,0:T(2,128)S(1)}, u32[]{:S(2)}, u32[]{:S(2)}) %all-to-all-start) | async-done | bytes 32800 | tf_op jit(solution)/shard_map/all_to_all | solution.py:212
  44.1 12.5 %shard_map.102 = bf16[4096,128]{1,0:T(8,128)(2,1)} custom-call(s32[8,512]{1,0:T(8,128)} %bitcast.43, s32[8,512]{1,0:T(8,128)} %get-tuple-element.16.peer_index_ref, bf16[4,1024,128]{2,1,0:T(8,128)(2,1)} %bitcast.4.own_ref, bf16[4,1024,128]{2,1,0:T(8,128)(2,1)} %bitcast.41), custom_call_target="tpu_custom_call" | custom-call | tf_op jit(solution)/shard_map/pallas_call | solution.py:140
  56.6 3.6 %all-to-all-start.1 = ((bf16[8,512,128]{2,1,0:T(8,128)(2,1)}), bf16[8,512,128]{2,1,0:T(8,128)(2,1)S(1)}, u32[]{:S(2)}, u32[]{:S(2)}) async-start(bf16[8,512,128]{2,1,0:T(8,128)(2,1)} %bitcast.33), calls=%async_computation.1 | async-start | bytes 2097152 | tf_op jit(solution)/shard_map/all_to_all | solution.py:212
  63.0 8.0 %shard_map.104 = bf16[4,512,128]{2,1,0:T(8,128)(2,1)} custom-call(s32[8,512]{1,0:T(8,128)} %reshape.147.refs_0_, s32[8,512]{1,0:T(8,128)} %reshape.149.refs_1_, bf16[4096,128]{1,0:T(8,128)(2,1)} %bitcast.31, bf16[4096,128]{1,0:T(8,128)(2,1)} %bitcast.34), custom_call_target="tpu_custom_call" | custom-call | tf_op jit(solution)/shard_map/pallas_call | solution.py:86
  71.0 1.5 %collective-permute-start.5 = (bf16[2048,128]{1,0:T(8,128)(2,1)}, bf16[2048,128]{1,0:T(8,128)(2,1)S(1)}, u32[]{:S(2)}, u32[]{:S(2)}) collective-permute-start(bf16[2048,128]{1,0:T(8,128)(2,1)} %bitcast.39), channel_id=1, source_target_pairs={{0,1},{1,0},{2,3},{3,2},{4,5},{5,4},{6,7},{7,6},{8,9},{9,8},{10,11... | collective-permute-start | bytes 1572872 | tf_op jit(solution)/shard_map/ppermute | solution.py:264
  72.5 8.0 %shard_map.103 = bf16[4,512,128]{2,1,0:T(8,128)(2,1)} custom-call(s32[8,512]{1,0:T(8,128)} %reshape.147.refs_0_, s32[8,512]{1,0:T(8,128)} %reshape.149.refs_1_, bf16[4096,128]{1,0:T(8,128)(2,1)} %bitcast.32, bf16[4096,128]{1,0:T(8,128)(2,1)} %bitcast.35), custom_call_target="tpu_custom_call" | custom-call | tf_op jit(solution)/shard_map/pallas_call | solution.py:86
  81.1 4.9 %collective-permute-done.5.other_ref = bf16[2048,128]{1,0:T(8,128)(2,1)S(1)} collective-permute-done((bf16[2048,128]{1,0:T(8,128)(2,1)}, bf16[2048,128]{1,0:T(8,128)(2,1)S(1)}, u32[]{:S(2)}, u32[]{:S(2)}) %collective-permute-start.5) | collective-permute-done | bytes 524320 | tf_op jit(solution)/shard_map/ppermute | solution.py:264
  86.8 4.3 %shard_map.105 = (f32[4096,128]{1,0:T(8,128)}, f32[16,128]{1,0:T(8,128)}, bf16[2048,128]{1,0:T(8,128)(2,1)}) custom-call(bf16[2048,128]{1,0:T(8,128)(2,1)} %bitcast.40, bf16[2048,128]{1,0:T(8,128)(2,1)} %copy-done.8, f32[4096,128]{1,0:T(8,128)} %table_ref.3, f32[32,128]{1,0:T(8,128)} %bitcast.46), custom_call_target="tpu_custom_call" | custom-call | tf_op jit(solution)/shard_map/pallas_call | solution.py:181
  91.1 5.3 %collective-permute-done.4.other_ref = bf16[2048,128]{1,0:T(8,128)(2,1)S(1)} collective-permute-done((bf16[2048,128]{1,0:T(8,128)(2,1)}, bf16[2048,128]{1,0:T(8,128)(2,1)S(1)}, u32[]{:S(2)}, u32[]{:S(2)}) %collective-permute-start.4) | collective-permute-done | bytes 524320 | tf_op jit(solution)/shard_map/ppermute | solution.py:264
  97.3 4.4 %shard_map.106 = (f32[4096,128]{1,0:T(8,128)}, f32[16,128]{1,0:T(8,128)}, bf16[2048,128]{1,0:T(8,128)(2,1)}) custom-call(bf16[2048,128]{1,0:T(8,128)(2,1)} %bitcast.38, bf16[2048,128]{1,0:T(8,128)(2,1)} %copy-done.5, f32[4096,128]{1,0:T(8,128)} %table_ref.3, f32[32,128]{1,0:T(8,128)} %bitcast.47, ...), custom_call_target="tpu_custom_call", output_to_operand_aliasing={{0}: (4, {})} | custom-call | tf_op jit(solution)/shard_map/pallas_call | solution.py:181
  105.5 5.1 %shard_map.107.refs_4_ = f32[4,512,128]{2,1,0:T(8,128)} custom-call(s32[4,512]{1,0:T(4,128)} %slice.71.refs_0_, s32[4,512]{1,0:T(4,128)} %slice.73.refs_1_, bf16[2048,128]{1,0:T(8,128)(2,1)} %get-tuple-element.15.refs_2_, bf16[2048,128]{1,0:T(8,128)(2,1)} %copy-done.7), custom_call_target="tpu_custom_call" | custom-call | tf_op jit(solution)/shard_map/pallas_call | solution.py:86
  111.4 5.4 %shard_map.108 = bf16[4,512,128]{2,1,0:T(8,128)(2,1)} custom-call(s32[4,512]{1,0:T(4,128)} %slice.67.refs_0_, s32[4,512]{1,0:T(4,128)} %slice.69.refs_1_, bf16[2048,128]{1,0:T(8,128)(2,1)} %get-tuple-element.14.refs_2_, bf16[2048,128]{1,0:T(8,128)(2,1)} %copy-done.4, f32[4,512,128]{2,1,0:T(8,128)} %shard_map.107.refs_4_), custom_call_target="tpu_custom_call" | custom-call | tf_op jit(solution)/shard_map/pallas_call | solution.py:86
  116.8 6.0 %all-to-all-start.3 = ((bf16[8,256,128]{2,1,0:T(8,128)(2,1)}), bf16[8,256,128]{2,1,0:T(8,128)(2,1)S(1)}, u32[]{:S(2)}, u32[]{:S(2)}) async-start(bf16[8,256,128]{2,1,0:T(8,128)(2,1)} %bitcast.36), calls=%async_computation.3 | async-start | bytes 1048576 | tf_op jit(solution)/shard_map/all_to_all | solution.py:212
  123.6 13.9 %all-to-all-done.3 = bf16[8,256,128]{2,1,0:T(8,128)(2,1)S(1)} async-done(((bf16[8,256,128]{2,1,0:T(8,128)(2,1)}), bf16[8,256,128]{2,1,0:T(8,128)(2,1)S(1)}, u32[]{:S(2)}, u32[]{:S(2)}) %all-to-all-start.3) | async-done | bytes 524320 | tf_op jit(solution)/shard_map/all_to_all | solution.py:212
  137.6 1.5 %collective-permute-start.9 = (bf16[256,128]{1,0:T(8,128)(2,1)S(1)}, bf16[256,128]{1,0:T(8,128)(2,1)S(1)}, u32[]{:S(2)}, u32[]{:S(2)}) collective-permute-start(bf16[256,128]{1,0:T(8,128)(2,1)S(1)} %reduce_sum.25), channel_id=1, source_target_pairs={{0,1},{1,0},{2,3},{3,2},{4,5},{5,4},{6,7},{7,6},{8,9},{9,8},{10,11... | collective-permute-start | bytes 196616 | tf_op jit(solution)/shard_map/ppermute | solution.py:293
  139.8 2.2 %collective-permute-done.9 = bf16[256,128]{1,0:T(8,128)(2,1)S(1)} collective-permute-done((bf16[256,128]{1,0:T(8,128)(2,1)S(1)}, bf16[256,128]{1,0:T(8,128)(2,1)S(1)}, u32[]{:S(2)}, u32[]{:S(2)}) %collective-permute-start.9) | collective-permute-done | bytes 65568 | tf_op jit(solution)/shard_map/ppermute | solution.py:293
  (71 shorter events, 14.4 us)
Async XLA Ops:
  0.6 16.3 %copy-start = (f32[4096,128]{1,0:T(8,128)S(1)}, f32[4096,128]{1,0:T(8,128)}, u32[]{:S(2)}) copy-start(f32[4096,128]{1,0:T(8,128)} %table_ref.3) | copy-start | bytes 6291460
  0.6 10.6 %collective-permute-start.2 = (bf16[512,128]{1,0:T(8,128)(2,1)}, bf16[512,128]{1,0:T(8,128)(2,1)S(1)}, u32[]{:S(2)}, u32[]{:S(2)}) collective-permute-start(bf16[512,128]{1,0:T(8,128)(2,1)} %param.9), channel_id=1, source_target_pairs={{0,16},{2,18},{4,20},{6,22},{8,24},{10,26},{12,28},{14,30},{16,0},... | collective-permute-start | bytes 393224 | tf_op jit(solution)/shard_map/ppermute | solution.py:217
  13.4 16.9 %all-to-all-start.2 = ((bf16[4,2,512,128]{3,2,1,0:T(8,128)(2,1)}), bf16[4,2,512,128]{3,2,1,0:T(8,128)(2,1)S(1)}, u32[]{:S(2)}, u32[]{:S(2)}) async-start(bf16[4,2,512,128]{3,2,1,0:T(8,128)(2,1)} %broadcast_in_dim.26), calls=%async_computation.2 | async-start | bytes 2097152 | tf_op jit(solution)/shard_map/all_to_all | solution.py:245
  17.0 1.1 copy-start.13
  18.1 25.0 %collective-permute-start = (bf16[4096,128]{1,0:T(8,128)(2,1)}, bf16[4096,128]{1,0:T(8,128)(2,1)S(1)}, u32[]{:S(2)}, u32[]{:S(2)}) collective-permute-start(bf16[4096,128]{1,0:T(8,128)(2,1)} %convert_element_type.13), channel_id=1, source_target_pairs={{0,2},{2,0},{4,6},{6,4},{8,10},{10,8},{12,14},{14,12},{16,18},{18,... | collective-permute-start | bytes 3145736 | tf_op jit(solution)/shard_map/ppermute | solution.py:209
  30.3 26.3 %copy-start.1 = (bf16[4,2,512,128]{3,2,1,0:T(8,128)(2,1)}, bf16[4,2,512,128]{3,2,1,0:T(8,128)(2,1)S(1)}, u32[]{:S(2)}) copy-start(bf16[4,2,512,128]{3,2,1,0:T(8,128)(2,1)S(1)} %all-to-all-done.2) | copy-start | bytes 3145732
  30.3 12.1 %all-to-all-start = ((s32[8,2,512]{2,1,0:T(2,128)}), s32[8,2,512]{2,1,0:T(2,128)S(1)}, u32[]{:S(2)}, u32[]{:S(2)}) async-start(s32[8,2,512]{2,1,0:T(2,128)} %reshape.143), calls=%async_computation | async-start | bytes 65536 | tf_op jit(solution)/shard_map/all_to_all | solution.py:212
  35.7 26.3 %collective-permute-start.3 = (bf16[4,2,512,128]{3,2,1,0:T(8,128)(2,1)S(1)}, bf16[4,2,512,128]{3,2,1,0:T(8,128)(2,1)S(1)}, u32[]{:S(2)}, u32[]{:S(2)}) collective-permute-start(bf16[4,2,512,128]{3,2,1,0:T(8,128)(2,1)S(1)} %all-to-all-done.2), channel_id=1, source_target_pairs={{0,2},{2,0},{4,6},{6,4},{8,10},{10,8},{12,14},{14,12},{16,18},{18,... | collective-permute-start | bytes 3145736 | tf_op jit(solution)/shard_map/ppermute | solution.py:209
  44.1 16.0 %copy-start.11 = (s32[8,512]{1,0:T(8,128)S(1)}, s32[8,512]{1,0:T(8,128)}, u32[]{:S(2)}) copy-start(s32[8,512]{1,0:T(8,128)} %get-tuple-element.16.peer_index_ref) | copy-start | bytes 49156
  44.1 16.1 %copy-start.10 = (s32[8,1,512]{2,0,1:T(8,128)S(1)}, s32[8,1,512]{2,0,1:T(8,128)}, u32[]{:S(2)}) copy-start(s32[8,1,512]{2,0,1:T(8,128)} %get-tuple-element.17) | copy-start | bytes 49156
  56.6 60.3 %all-to-all-start.1 = ((bf16[8,512,128]{2,1,0:T(8,128)(2,1)}), bf16[8,512,128]{2,1,0:T(8,128)(2,1)S(1)}, u32[]{:S(2)}, u32[]{:S(2)}) async-start(bf16[8,512,128]{2,1,0:T(8,128)(2,1)} %bitcast.33), calls=%async_computation.1 | async-start | bytes 2097152 | tf_op jit(solution)/shard_map/all_to_all | solution.py:212
  60.1 1.2 collective-permute-start.1
  63.0 18.1 %copy-start.12 = (s32[4096]{0:T(1024)S(1)}, s32[4096]{0:T(1024)}, u32[]{:S(2)}) copy-start(s32[4096]{0:T(1024)} %param.13) | copy-start | bytes 49156
  71.0 15.0 %collective-permute-start.5 = (bf16[2048,128]{1,0:T(8,128)(2,1)}, bf16[2048,128]{1,0:T(8,128)(2,1)S(1)}, u32[]{:S(2)}, u32[]{:S(2)}) collective-permute-start(bf16[2048,128]{1,0:T(8,128)(2,1)} %bitcast.39), channel_id=1, source_target_pairs={{0,1},{1,0},{2,3},{3,2},{4,5},{5,4},{6,7},{7,6},{8,9},{9,8},{10,11... | collective-permute-start | bytes 1572872 | tf_op jit(solution)/shard_map/ppermute | solution.py:264
  80.5 15.9 %collective-permute-start.4 = (bf16[2048,128]{1,0:T(8,128)(2,1)}, bf16[2048,128]{1,0:T(8,128)(2,1)S(1)}, u32[]{:S(2)}, u32[]{:S(2)}) collective-permute-start(bf16[2048,128]{1,0:T(8,128)(2,1)} %bitcast.37), channel_id=1, source_target_pairs={{0,1},{1,0},{2,3},{3,2},{4,5},{5,4},{6,7},{7,6},{8,9},{9,8},{10,11... | collective-permute-start | bytes 1572872 | tf_op jit(solution)/shard_map/ppermute | solution.py:264
  81.1 22.3 %collective-permute-start.6 = (s32[4096]{0:T(1024)S(1)}, s32[4096]{0:T(1024)S(1)}, u32[]{:S(2)}, u32[]{:S(2)}) collective-permute-start(s32[4096]{0:T(1024)S(1)} %copy-done.12), channel_id=1, source_target_pairs={{0,2},{2,0},{4,6},{6,4},{8,10},{10,8},{12,14},{14,12},{16,18},{18,... | collective-permute-start | bytes 49160 | tf_op jit(solution)/shard_map/ppermute | solution.py:209
  97.3 4.4 %copy-start.6 = (bf16[2048,128]{1,0:T(8,128)(2,1)S(1)}, bf16[2048,128]{1,0:T(8,128)(2,1)}, u32[]{:S(2)}) copy-start(bf16[2048,128]{1,0:T(8,128)(2,1)} %get-tuple-element.15.refs_2_) | copy-start | bytes 1572868
  101.6 8.9 %collective-permute-start.7 = (bf16[2048,128]{1,0:T(8,128)(2,1)}, bf16[2048,128]{1,0:T(8,128)(2,1)S(1)}, u32[]{:S(2)}, u32[]{:S(2)}) collective-permute-start(bf16[2048,128]{1,0:T(8,128)(2,1)} %get-tuple-element.14.refs_2_), channel_id=1, source_target_pairs={{0,2},{2,0},{4,6},{6,4},{8,10},{10,8},{12,14},{14,12},{16,18},{18,... | collective-permute-start | bytes 1572872 | tf_op jit(solution)/shard_map/ppermute | solution.py:209
  101.7 3.0 %collective-permute-start.8 = (bf16[2048,128]{1,0:T(8,128)(2,1)S(1)}, bf16[2048,128]{1,0:T(8,128)(2,1)S(1)}, u32[]{:S(2)}, u32[]{:S(2)}) collective-permute-start(bf16[2048,128]{1,0:T(8,128)(2,1)S(1)} %copy-done.6), channel_id=1, source_target_pairs={{0,2},{2,0},{4,6},{6,4},{8,10},{10,8},{12,14},{14,12},{16,18},{18,... | collective-permute-start | bytes 1572872 | tf_op jit(solution)/shard_map/ppermute | solution.py:209
  110.6 28.6 %copy-start.15 = (f32[16,128]{1,0:T(8,128)S(1)}, f32[16,128]{1,0:T(8,128)}, u32[]{:S(2)}) copy-start(f32[16,128]{1,0:T(8,128)} %get-tuple-element.12) | copy-start | bytes 24580
  110.6 28.6 %copy-start.16 = (f32[16,128]{1,0:T(8,128)S(1)}, f32[16,128]{1,0:T(8,128)}, u32[]{:S(2)}) copy-start(f32[16,128]{1,0:T(8,128)} %get-tuple-element.13) | copy-start | bytes 24580
  116.8 25.2 %copy-start.9 = (f32[512,128]{1,0:T(8,128)S(1)}, f32[512,128]{1,0:T(8,128)}, u32[]{:S(2)}) copy-start(f32[512,128]{1,0:T(8,128)} %param.12) | copy-start | bytes 786436
  116.8 20.7 %all-to-all-start.3 = ((bf16[8,256,128]{2,1,0:T(8,128)(2,1)}), bf16[8,256,128]{2,1,0:T(8,128)(2,1)S(1)}, u32[]{:S(2)}, u32[]{:S(2)}) async-start(bf16[8,256,128]{2,1,0:T(8,128)(2,1)} %bitcast.36), calls=%async_computation.3 | async-start | bytes 1048576 | tf_op jit(solution)/shard_map/all_to_all | solution.py:212
  137.6 4.3 %collective-permute-start.9 = (bf16[256,128]{1,0:T(8,128)(2,1)S(1)}, bf16[256,128]{1,0:T(8,128)(2,1)S(1)}, u32[]{:S(2)}, u32[]{:S(2)}) collective-permute-start(bf16[256,128]{1,0:T(8,128)(2,1)S(1)} %reduce_sum.25), channel_id=1, source_target_pairs={{0,1},{1,0},{2,3},{3,2},{4,5},{5,4},{6,7},{7,6},{8,9},{9,8},{10,11... | collective-permute-start | bytes 196616 | tf_op jit(solution)/shard_map/ppermute | solution.py:293
  (7 other events, 6.3 us)

commit v3 on v0

v3 whole, which is shorter than its diff:
```python
import functools
import jax
import jax.numpy as jnp
from jax import lax
from jax.experimental import pallas as pl
from jax.experimental.pallas import tpu as pltpu
from jax.sharding import PartitionSpec as P

LEARN = 0.5
EPSILON = 1e-06
SPLIT = 4
PARTS = 2
TABLE_ROWS = 512
NEAR_BYTES = 1 << 21
VMEM = pl.BlockSpec(memory_space=pltpu.VMEM)
SMEM = pl.BlockSpec(memory_space=pltpu.SMEM)


def near(values, copies=1):
    if copies * values.size * values.dtype.itemsize > NEAR_BYTES:
        return values
    return pltpu.with_memory_space_constraint(values, pltpu.MemorySpace.VMEM)


def column_of(row, lanes):
    return jnp.broadcast_to(row, (lanes, row.shape[1])).T


def bits_of(count):
    assert count & (count - 1) == 0
    return count.bit_length() - 1


def split_index(index, low_count):
    return lax.shift_right_arithmetic(index, bits_of(low_count)), lax.bitwise_and(index, low_count - 1)


def side_of(line, side):
    count = line.shape[1] // 2
    return jnp.where(side == 0, line[:, :count], line[:, count:])


def add_segments(total_ref, index, rows, first):
    low_count, spread_width = total_ref.shape
    width = spread_width // SPLIT
    block, low = split_index(index, low_count)
    low = jnp.where((block < 0) | (block >= SPLIT), -1, low)
    hits = (
        (lax.broadcasted_iota(jnp.int32, (low_count, index.shape[1]), 0) == low)
        .astype(jnp.float32)
        .astype(jnp.bfloat16)
    )
    block_column = column_of(block, width)
    rows = rows.astype(jnp.float32)
    spread = jnp.concatenate(
        [jnp.where(block_column == i, rows, 0.0).astype(jnp.bfloat16) for i in range(SPLIT)], axis=1
    )
    part = jnp.dot(hits, spread, preferred_element_type=jnp.float32)
    if first:
        total_ref[...] = part
    else:
        total_ref[...] += part


def put_segments(out_ref, total_ref):
    low_count, width = total_ref.shape[0], out_ref.shape[1]
    for i in range(SPLIT):
        out_ref[i * low_count : (i + 1) * low_count, :] = total_ref[
            :, i * width : (i + 1) * width
        ].astype(out_ref.dtype)


def segment_kernel(place_ref, asked_ref, peer_asked_ref, *refs, base):
    out_ref, total_ref = refs[-2:]
    count = (len(refs) - 2) // 2
    core, chip = place_ref[0], place_ref[1]
    for k in range(count):
        lines = []
        for ref in (asked_ref, peer_asked_ref):
            for source in (chip ^ k, chip ^ k ^ count):
                lines.append(side_of(ref[source], core))
        index = jnp.concatenate(lines, axis=1) - base
        rows = jnp.concatenate([refs[k][...], refs[count + k][...]], axis=0)
        add_segments(total_ref, index, rows, k == 0)
    put_segments(out_ref, total_ref)


def row_gradients(place, asked, peer_asked, grads, peer_grads, base, row_count):
    width = grads[0].shape[1]
    return pl.pallas_call(
        functools.partial(segment_kernel, base=base),
        in_specs=[SMEM] + [VMEM] * (2 + 2 * len(grads)),
        out_specs=VMEM,
        out_shape=pltpu.VMEM((row_count, width), jnp.bfloat16),
        scratch_shapes=[pltpu.VMEM((row_count // SPLIT, SPLIT * width), jnp.float32)],
    )(place, near(asked), near(peer_asked), *[near(g, 2 * len(grads)) for g in (*grads, *peer_grads)])


def gather_kernel(place_ref, asked_ref, own_ref, peer_ref, out_ref, held_ref, *, together):
    chips = asked_ref.shape[0]
    low_count, width = held_ref.shape[1], out_ref.shape[1]
    bags = out_ref.shape[0] // chips
    core = place_ref[0]
    for i in range(SPLIT):
        at = slice(i * low_count, (i + 1) * low_count)
        held_ref[0, :, i * width : (i + 1) * width] = own_ref[at, :].astype(jnp.bfloat16)
        held_ref[1, :, i * width : (i + 1) * width] = peer_ref[at, :]
    for j in range(0, chips, together):
        total = jnp.zeros((together * bags, width), jnp.float32)
        lane = lax.broadcasted_iota(jnp.int32, total.shape, 1)
        for side in range(2):
            index = jnp.concatenate(
                [side_of(asked_ref[j + i], core ^ side) for i in range(together)], axis=1
            )
            block, low = split_index(column_of(index, width), low_count)
            hits = jnp.concatenate(
                [
                    (lane == low - first).astype(jnp.float32).astype(jnp.bfloat16)
                    for first in range(0, low_count, width)
                ],
                axis=1,
            )
            found = jnp.dot(hits, held_ref[side], preferred_element_type=jnp.float32)
            for i in range(SPLIT):
                total += jnp.where(block == i, found[:, i * width : (i + 1) * width], 0.0)
        out_ref[j * bags : (j + together) * bags, :] = total.astype(out_ref.dtype)


def chip_rows(place, asked, own_rows, peer_rows):
    row_count, width = own_rows.shape
    chips, bags = asked.shape[0], asked.shape[2] // 2
    return pl.pallas_call(
        functools.partial(gather_kernel, together=2),
        in_specs=[SMEM, VMEM, VMEM, VMEM],
        out_specs=VMEM,
        out_shape=jax.ShapeDtypeStruct((chips * bags, width), jnp.bfloat16),
        scratch_shapes=[pltpu.VMEM((2, row_count // SPLIT, SPLIT * width), jnp.bfloat16)],
    )(place, *map(near, (asked, own_rows, peer_rows)))


def update_kernel(
    own_ref, other_ref, table_ref, accum_ref, new_table_ref, new_accum_ref, delta_ref, old_ref, sems, *, base
):
    rows, width = own_ref.shape
    copies = [
        pltpu.make_async_copy(
            table_ref.at[pl.ds(base + i * TABLE_ROWS, TABLE_ROWS), :],
            old_ref.at[pl.ds(i * TABLE_ROWS, TABLE_ROWS), :],
            sems.at[i],
        )
        for i in range(rows // TABLE_ROWS)
    ]
    for copy in copies:
        copy.start()
    diagonal = lax.broadcasted_iota(jnp.int32, (width, width), 0) == lax.broadcasted_iota(
        jnp.int32, (width, width), 1
    )
    for j in range(rows // width):
        if j * width % TABLE_ROWS == 0:
            copies[j * width // TABLE_ROWS].wait()
        at = slice(j * width, (j + 1) * width)
        line = base // width + j
        grads = own_ref[at, :].astype(jnp.float32) + other_ref[at, :].astype(jnp.float32)
        scaled = jnp.where(diagonal, accum_ref[line : line + 1, :] * width, 0.0)
        fresh_accum = jnp.sum(grads * grads + scaled, axis=1, keepdims=True) * (1.0 / width)
        old_rows = old_ref[at, :]
        fresh_rows = old_rows - LEARN * grads / jnp.sqrt(fresh_accum + EPSILON)
        new_table_ref[at, :] = fresh_rows
        delta_ref[at, :] = (fresh_rows - old_rows).astype(jnp.bfloat16)
        new_accum_ref[j : j + 1, :] = jnp.sum(
            jnp.where(diagonal, fresh_accum, 0.0), axis=0, keepdims=True
        )


def update(own, other, table, accum, base):
    rows, width = own.shape
    return pl.pallas_call(
        functools.partial(update_kernel, base=base),
        in_specs=[VMEM, VMEM, pl.BlockSpec(memory_space=pl.ANY), VMEM],
        out_specs=[VMEM] * 3,
        out_shape=[
            jax.ShapeDtypeStruct((rows, width), jnp.float32),
            jax.ShapeDtypeStruct((rows // width, width), jnp.float32),
            pltpu.VMEM((rows, width), jnp.bfloat16),
        ],
        scratch_shapes=[
            pltpu.VMEM((rows, width), jnp.float32),
            pltpu.SemaphoreType.DMA((rows // TABLE_ROWS,)),
        ],
    )(near(own), near(other), table, near(accum))


def parity_kernel(place_ref, slot_ref, peer_slot_ref, delta_ref, peer_delta_ref, *refs, base, holder_rows, dp_count, tile):
    start_refs, (out_ref, total_ref) = refs[:-2], refs[-2:]
    core, dp_index = place_ref[0], place_ref[2]
    part_count = holder_rows // dp_count
    line_width = slot_ref.shape[1]
    for k in range(delta_ref.shape[0] // tile):
        first = (base + k * tile) // line_width
        slot = jnp.concatenate(
            [
                ref[first + i : first + i + 1, :]
                for ref in (slot_ref, peer_slot_ref)
                for i in range(tile // line_width)
            ],
            axis=1,
        )
        holder, offset = split_index(slot, holder_rows)
        part, offset = split_index(offset, part_count)
        mine = (lax.bitwise_and(holder, 1) == core) & (part == dp_index)
        target = lax.shift_right_arithmetic(holder, 1) * part_count + offset
        at = slice(k * tile, (k + 1) * tile)
        rows = jnp.concatenate([delta_ref[at, :], peer_delta_ref[at, :]], axis=0)
        add_segments(total_ref, jnp.where(mine, target, -1), rows, k == 0)
    for ref in start_refs:
        total_ref[...] += ref[...]
    if out_ref.shape == total_ref.shape:
        out_ref[...] = total_ref[...]
    else:
        put_segments(out_ref, total_ref)


def parity_changes(place, slot, peer_slot, delta, peer_delta, base, holder_rows, dp_count, segment_count, start, last):
    width = delta.shape[1]
    held = pltpu.VMEM((segment_count // SPLIT, SPLIT * width), jnp.float32)
    return pl.pallas_call(
        functools.partial(
            parity_kernel, base=base, holder_rows=holder_rows, dp_count=dp_count,
            tile=min(1024, delta.shape[0]),
        ),
        in_specs=[SMEM] + [VMEM] * (4 + len(start)),
        out_specs=VMEM,
        out_shape=jax.ShapeDtypeStruct((segment_count, width), jnp.bfloat16) if last else held,
        scratch_shapes=[held],
    )(place, *map(near, (slot, peer_slot, delta, peer_delta, *start)))


def on_device(owners, local_rows, grad_pooled, table, accum, parity, parity_slot):
    table_count = lax.axis_size("table")
    dp_count = lax.axis_size("dp")
    chip_count = table_count // 2
    half = table_count // 2
    bag_count, per_bag = owners.shape
    row_count, width = table.shape
    parity_count = parity.shape[0]
    device = lax.axis_index("table")
    dp_index = lax.axis_index("dp")
    place = jnp.stack([device % 2, device // 2, dp_index]).astype(jnp.int32)
    same_core = [list(range(c, table_count, 2)) for c in range(2)]

    def swap(values, distance):
        return lax.ppermute(values, "table", [(i, i ^ distance) for i in range(table_count)])

    def exchange(values):
        return lax.all_to_all(
            values, "table", split_axis=0, concat_axis=0, axis_index_groups=same_core, tiled=True
        )

    far_grads = swap(grad_pooled, half)

    lanes = jnp.arange(2 * bag_count, dtype=jnp.int32)[None, None, None, :]
    chips = jnp.arange(chip_count, dtype=jnp.int32)[:, None, None, None]
    owners_twice = jnp.tile(owners.T, (1, 2)).reshape(1, 1, per_bag, 2 * bag_count)
    rows_twice = jnp.tile(local_rows.T, (1, 2)).reshape(1, 1, per_bag, 2 * bag_count)
    named = owners_twice == 2 * chips + (lanes >= bag_count).astype(jnp.int32)
    requests = jnp.max(jnp.where(named, rows_twice, -1), axis=2)
    asked = exchange(requests)
    peer_half = swap(table.astype(jnp.bfloat16), 1)
    line_width = 4 * width
    slot_lines = parity_slot.reshape(-1, line_width)
    peer_slot_lines = swap(slot_lines, 1)

    grads = [jnp.concatenate([grad_pooled, far_grads], axis=0)]
    for k in range(1, chip_count // 2):
        grads.append(swap(grads[0], 2 * k))
    peer_asked = swap(asked, 1)
    peer_grads = []
    for values in grads:
        peer_grads.append(swap(values, 1))

    fetched = chip_rows(place, asked, table, peer_half)

    part_rows = row_count // PARTS
    halves = []
    for part in range(PARTS):
        mine = row_gradients(place, asked, peer_asked, grads, peer_grads, part * part_rows, part_rows)
        distance = 1
        other = lax.ppermute(mine, "dp", [(i, i ^ 1) for i in range(dp_count)])
        while 2 * distance < dp_count:
            distance *= 2
            mine = (mine.astype(jnp.float32) + other.astype(jnp.float32)).astype(jnp.bfloat16)
            other = lax.ppermute(mine, "dp", [(i, i ^ distance) for i in range(dp_count)])
        halves.append((mine, other))

    returned = exchange(fetched.reshape(chip_count, bag_count, width))

    part_count = parity_count // dp_count
    tables, accums, changes = [], [], []
    accum_lines = accum.reshape(-1, width)
    for part, (mine, other) in enumerate(halves):
        fresh, fresh_accum, delta = update(mine, other, table, accum_lines, part * part_rows)
        tables.append(fresh)
        accums.append(fresh_accum)
        peer_delta = swap(delta, 1)
        changes = [
            parity_changes(
                place, slot_lines, peer_slot_lines, delta, peer_delta, part * part_rows,
                parity_count, dp_count, chip_count * part_count, changes, part == PARTS - 1,
            )
        ]
    arrived = exchange(changes[0].reshape(chip_count, part_count, width))
    pooled = jnp.sum(returned.astype(jnp.float32), axis=0).astype(jnp.bfloat16)
    new_table = jnp.concatenate(tables, axis=0)
    new_accum = jnp.concatenate(accums, axis=0).reshape(row_count)
    part = jnp.sum(arrived.astype(jnp.float32), axis=0).astype(jnp.bfloat16)
    if dp_count == 2:
        other = lax.ppermute(part, "dp", [(0, 1), (1, 0)])
        parts = jnp.where(dp_index == 0, jnp.stack([part, other]), jnp.stack([other, part]))
    else:
        parts = lax.all_gather(part, "dp", axis=0)
    new_parity = parity + parts.reshape(parity_count, width).astype(jnp.float32)
    return (pooled, new_table, new_accum, new_parity)


def solution(mesh):
    in_specs = (
        P(("table", "dp"), None),
        P(("table", "dp"), None),
        P(("table", "dp"), None),
        P("table", None),
        P("table"),
        P("table", None),
        P("table"),
    )
    out_specs = (P(("table", "dp"), None), P("table", None), P("table"), P("table", None))

    return jax.shard_map(on_device, mesh=mesh, in_specs=in_specs, out_specs=out_specs, check_vma=False)
```

time: 314 us -> 145 us (0.46); the launches traced: 308 us -> 145 us
  other arithmetic: 82.5 us -> 8.26 us
  local copies, waits for them, and re-layouts: 68.8 us -> 9.73 us
  waiting for transfers between devices: 98.8 us -> 60.5 us
  Pallas kernels: 0 us -> 37 us
  between operations: 14.3 us -> 0.84 us
  starting transfers between devices: 39.2 us -> 28.2 us
  blocking collectives: 4.35 us -> 0 us
    scatter-add x1 -> x0, other arithmetic: 45.7 us -> none  [on_device(): jax.ops.segment_sum(incoming.reshape(slot_count, row_width).astype(jnp.fl...]
    all_to_all x4 -> x3, waiting for transfers between devices: 64 us -> 25.6 us  [exchange(): lax.all_to_all(values, 'table', split_axis=0, concat_axis=0, axis_index_g...]
    pallas_call x0 -> x7, Pallas kernels: none -> 37 us  [the longest x2 11.1 us: row_gradients(): pl.pallas_call(functools.partial(segment_kernel, base=base), in_specs=[SM...]
    gather x2 -> x0, local copies, waits for them, and re-layouts: 36.2 us -> none  [the longest x1 24 us: on_device(): jnp.take(table_half, jnp.minimum(asked_rows, row_count - 1), axis=0)]
    ppermute x0 -> x16, waiting for transfers between devices: none -> 34.9 us  [the longest x13 19.3 us: swap(): lax.ppermute(values, 'table', [(i, i ^ distance) for i in range(table_cou...]
    all_gather x1 -> x0, waiting for transfers between devices: 34.7 us -> none  [on_device(): lax.all_gather(fresh_rows, 'dp', axis=0, tiled=True)]
    scatter x2 -> x0, local copies, waits for them, and re-layouts: 28.5 us -> none  [the longest x1 16.1 us: on_device(): jnp.full((slot_count,), row_count, jnp.int32).at[position].set(local_flat)]
    all_to_all x4 -> x3, starting transfers between devices: 39.2 us -> 16.1 us  [exchange(): lax.all_to_all(values, 'table', split_axis=0, concat_axis=0, axis_index_g...]
  transfers between devices with their start and end apart: 6 -> 19, of which waited for: 3 -> 12; matrix products, arithmetic and copies ran while one was open for 24% -> 7% of each run, Pallas kernels for 0% -> 22%
where the time goes in v3:
time: 145 us
  waiting for transfers between devices  60.5 us (42%)
  Pallas kernels  37 us (26%)
  starting transfers between devices  28.2 us (19%)
  local copies, waits for them, and re-layouts  9.73 us (7%)
  other arithmetic  8.26 us (6%)
    all_to_all x3, waiting for transfers between devices, exchange(): lax.all_to_all(values, 'table', split_axis=0, concat_axis=0, axis_index_g...  25.6 us
    ppermute x13, waiting for transfers between devices, swap(): lax.ppermute(values, 'table', [(i, i ^ distance) for i in range(table_cou...  19.3 us
    all_to_all x3, starting transfers between devices, exchange(): lax.all_to_all(values, 'table', split_axis=0, concat_axis=0, axis_index_g...  16.1 us
    ppermute x2, waiting for transfers between devices, on_device(): other = lax.ppermute(mine, 'dp', [(i, i ^ 1) for i in range(dp_count)])  13.5 us
    pallas_call x2, Pallas kernels, row_gradients(): pl.pallas_call(functools.partial(segment_kernel, base=base), in_specs=[SM...  11.1 us
    pallas_call x1, Pallas kernels, chip_rows(): pl.pallas_call(functools.partial(gather_kernel, together=2), in_specs=[SM...  10.9 us
    ppermute x13, starting transfers between devices, swap(): lax.ppermute(values, 'table', [(i, i ^ distance) for i in range(table_cou...  8.41 us
    pallas_call x2, Pallas kernels, parity_changes(): pl.pallas_call(functools.partial(parity_kernel, base=base, holder_rows=ho...  8 us
  transfers between devices with their start and end apart: 19, of which 12 were waited for; matrix products, arithmetic and copies ran while one was open for 7% of the time, Pallas kernels for 22%

profile of v3, /device:TPU:0, one launch (start us, length us, event | category | flops | bytes accessed | tf_op | source)
XLA Modules:
  0.0 144.6 jit_solution(5467395617602431626)
XLA Ops:
  0.6 4.1 %collective-permute-start.2 = (bf16[512,128]{1,0:T(8,128)(2,1)}, bf16[512,128]{1,0:T(8,128)(2,1)S(1)}, u32[]{:S(2)}, u32[]{:S(2)}) collective-permute-start(bf16[512,128]{1,0:T(8,128)(2,1)} %param.9), channel_id=1, source_target_pairs={{0,16},{2,18},{4,20},{6,22},{8,24},{10,26},{12,28},{14,30},{16,0},... | collective-permute-start | bytes 393224 | tf_op jit(solution)/shard_map/ppermute | solution.py:252
  5.7 5.6 %collective-permute-done.2 = bf16[512,128]{1,0:T(8,128)(2,1)S(1)} collective-permute-done((bf16[512,128]{1,0:T(8,128)(2,1)}, bf16[512,128]{1,0:T(8,128)(2,1)S(1)}, u32[]{:S(2)}, u32[]{:S(2)}) %collective-permute-start.2) | collective-permute-done | bytes 131104 | tf_op jit(solution)/shard_map/ppermute | solution.py:252
  11.3 1.6 %collective-permute-start.3 = (bf16[1024,128]{1,0:T(8,128)(2,1)S(1)}, bf16[1024,128]{1,0:T(8,128)(2,1)S(1)}, u32[]{:S(2)}, u32[]{:S(2)}) collective-permute-start(bf16[1024,128]{1,0:T(8,128)(2,1)S(1)} %constant_dynamic-update-slice_fusion.refs_0_), channel_id=1, source_target_pairs={{0,4},{2,6},{4,0},{6,2},{8,12},{10,14},{12,8},{14,10},{16,20},{18,... | collective-permute-start | bytes 786440 | tf_op jit(solution)/shard_map/ppermute | solution.py:252
  14.9 4.7 %collective-permute-done.3.refs_1_ = bf16[1024,128]{1,0:T(8,128)(2,1)S(1)} collective-permute-done((bf16[1024,128]{1,0:T(8,128)(2,1)S(1)}, bf16[1024,128]{1,0:T(8,128)(2,1)S(1)}, u32[]{:S(2)}, u32[]{:S(2)}) %collective-permute-start.3) | collective-permute-done | bytes 262176 | tf_op jit(solution)/shard_map/ppermute | solution.py:252
  19.6 2.5 %collective-permute-done.4.refs_2_ = bf16[1024,128]{1,0:T(8,128)(2,1)S(1)} collective-permute-done((bf16[1024,128]{1,0:T(8,128)(2,1)S(1)}, bf16[1024,128]{1,0:T(8,128)(2,1)S(1)}, u32[]{:S(2)}, u32[]{:S(2)}) %collective-permute-start.4) | collective-permute-done | bytes 262176 | tf_op jit(solution)/shard_map/ppermute | solution.py:252
  22.1 3.5 %collective-permute-done.5.refs_3_ = bf16[1024,128]{1,0:T(8,128)(2,1)S(1)} collective-permute-done((bf16[1024,128]{1,0:T(8,128)(2,1)S(1)}, bf16[1024,128]{1,0:T(8,128)(2,1)S(1)}, u32[]{:S(2)}, u32[]{:S(2)}) %collective-permute-start.5) | collective-permute-done | bytes 262176 | tf_op jit(solution)/shard_map/ppermute | solution.py:252
  27.8 6.5 %all-to-all-start = ((s32[8,1,1024]{2,1,0:T(1,128)}), s32[8,1,1024]{2,1,0:T(1,128)S(1)}, u32[]{:S(2)}, u32[]{:S(2)}) async-start(s32[8,1,1024]{2,1,0:T(1,128)} %reduce_max.12), calls=%async_computation | async-start | bytes 65536 | tf_op jit(solution)/shard_map/all_to_all | solution.py:255
  34.4 6.7 %all-to-all-done.asked_ref = s32[8,1,1024]{2,1,0:T(1,128)S(1)} async-done(((s32[8,1,1024]{2,1,0:T(1,128)}), s32[8,1,1024]{2,1,0:T(1,128)S(1)}, u32[]{:S(2)}, u32[]{:S(2)}) %all-to-all-start) | async-done | bytes 32800 | tf_op jit(solution)/shard_map/all_to_all | solution.py:255
  42.3 5.6 %shard_map.103.own_ref = bf16[2048,128]{1,0:T(8,128)(2,1)S(1)} custom-call(s32[3]{0:T(128)} %pad_add_fusion.place_ref, s32[8,1,1024]{2,1,0:T(1,128)S(1)} %all-to-all-done.asked_ref, s32[8,1,1024]{2,1,0:T(1,128)S(1)} %collective-permute-done.1.peer_asked_ref, bf16[1024,128]{1,0:T(8,128)(2,1)S(1)} %constant_dynamic-update-slice_fusion.refs_0_, ...), custom_call_target="tpu_custom_call" | custom-call | tf_op jit(solution)/shard_map/pallas_call | solution.py:90
  49.4 5.6 %shard_map.105.own_ref = bf16[2048,128]{1,0:T(8,128)(2,1)S(1)} custom-call(s32[3]{0:T(128)} %pad_add_fusion.place_ref, s32[8,1,1024]{2,1,0:T(1,128)S(1)} %all-to-all-done.asked_ref, s32[8,1,1024]{2,1,0:T(1,128)S(1)} %collective-permute-done.1.peer_asked_ref, bf16[1024,128]{1,0:T(8,128)(2,1)S(1)} %constant_dynamic-update-slice_fusion.refs_0_, ...), custom_call_target="tpu_custom_call" | custom-call | tf_op jit(solution)/shard_map/pallas_call | solution.py:90
  55.6 7.2 %collective-permute-done.10.other_ref = bf16[2048,128]{1,0:T(8,128)(2,1)} collective-permute-done((bf16[2048,128]{1,0:T(8,128)(2,1)S(1)}, bf16[2048,128]{1,0:T(8,128)(2,1)}, u32[]{:S(2)}, u32[]{:S(2)}) %collective-permute-start.10) | collective-permute-done | bytes 524320 | tf_op jit(solution)/shard_map/ppermute | solution.py:288
  62.8 4.0 %shard_map.104 = (f32[2048,128]{1,0:T(8,128)}, f32[16,128]{1,0:T(8,128)}, bf16[2048,128]{1,0:T(8,128)(2,1)S(1)}) custom-call(bf16[2048,128]{1,0:T(8,128)(2,1)S(1)} %shard_map.103.own_ref, bf16[2048,128]{1,0:T(8,128)(2,1)} %collective-permute-done.10.other_ref, f32[4096,128]{1,0:T(8,128)} %table_ref.3, f32[32,128]{1,0:T(8,128)S(1)} %bitcast.17), custom_call_target="tpu_custom_call" | custom-call | tf_op jit(solution)/shard_map/pallas_call | solution.py:177
  66.9 6.3 %collective-permute-done.11.other_ref = bf16[2048,128]{1,0:T(8,128)(2,1)S(1)} collective-permute-done((bf16[2048,128]{1,0:T(8,128)(2,1)S(1)}, bf16[2048,128]{1,0:T(8,128)(2,1)S(1)}, u32[]{:S(2)}, u32[]{:S(2)}) %collective-permute-start.11) | collective-permute-done | bytes 524320 | tf_op jit(solution)/shard_map/ppermute | solution.py:288
  73.1 3.1 %shard_map.106 = (f32[2048,128]{1,0:T(8,128)}, f32[16,128]{1,0:T(8,128)}, bf16[2048,128]{1,0:T(8,128)(2,1)}) custom-call(bf16[2048,128]{1,0:T(8,128)(2,1)S(1)} %shard_map.105.own_ref, bf16[2048,128]{1,0:T(8,128)(2,1)S(1)} %collective-permute-done.11.other_ref, f32[4096,128]{1,0:T(8,128)} %table_ref.3, f32[32,128]{1,0:T(8,128)S(1)} %bitcast.18), custom_call_target="tpu_custom_call" | custom-call | tf_op jit(solution)/shard_map/pallas_call | solution.py:177
  76.3 2.7 %convert_element_type.22 = bf16[4096,128]{1,0:T(8,128)(2,1)} convert(f32[4096,128]{1,0:T(8,128)} %table_ref.3) | non-fusion elementwise | flops 524288 | bytes 3145728 | tf_op jit(solution)/shard_map/convert_element_type | solution.py:268
  79.6 2.4 %collective-permute-done.12.peer_slot_ref = s32[8,512]{1,0:T(8,128)S(1)} collective-permute-done((s32[8,512]{1,0:T(8,128)S(1)}, s32[8,512]{1,0:T(8,128)S(1)}, u32[]{:S(2)}, u32[]{:S(2)}) %collective-permute-start.12) | collective-permute-done | bytes 16416 | tf_op jit(solution)/shard_map/ppermute | solution.py:252
  84.9 3.4 %shard_map.107.refs_0_ = f32[512,512]{1,0:T(8,128)S(1)} custom-call(s32[3]{0:T(128)} %pad_add_fusion.place_ref, s32[8,512]{1,0:T(8,128)S(1)} %reshape.102.slot_ref, s32[8,512]{1,0:T(8,128)S(1)} %collective-permute-done.12.peer_slot_ref, bf16[2048,128]{1,0:T(8,128)(2,1)S(1)} %copy-done.4, bf16[2048,128]{1,0:T(8,128)(2,1)S(1)} %copy-done.6), custom_call_target="tpu_custom_call" | custom-call | tf_op jit(solution)/shard_map/pallas_call | solution.py:226
  88.3 4.6 %shard_map.108 = bf16[2048,128]{1,0:T(8,128)(2,1)} custom-call(s32[3]{0:T(128)} %pad_add_fusion.place_ref, s32[8,512]{1,0:T(8,128)S(1)} %reshape.102.slot_ref, s32[8,512]{1,0:T(8,128)S(1)} %collective-permute-done.12.peer_slot_ref, bf16[2048,128]{1,0:T(8,128)(2,1)} %get-tuple-element.14.delta_ref, bf16[2048,128]{1,0:T(8,128)(2,1)} %collective-permute-done.13.peer_delta_ref, ...), custom_call_target="tpu_custom_call" | custom-call | tf_op jit(solution)/shard_map/pallas_call | solution.py:226
  92.9 4.1 %all-to-all-start.2 = ((bf16[8,256,128]{2,1,0:T(8,128)(2,1)}), bf16[8,256,128]{2,1,0:T(8,128)(2,1)}, u32[]{:S(2)}, u32[]{:S(2)}) async-start(bf16[8,256,128]{2,1,0:T(8,128)(2,1)} %bitcast.20), calls=%async_computation.2 | async-start | bytes 1048576 | tf_op jit(solution)/shard_map/all_to_all | solution.py:255
  98.0 1.6 %copy-done = f32[4096,128]{1,0:T(8,128)S(1)} copy-done((f32[4096,128]{1,0:T(8,128)S(1)}, f32[4096,128]{1,0:T(8,128)}, u32[]{:S(2)}) %copy-start) | copy-done | bytes 2097176
  100.8 10.9 %shard_map.102 = bf16[4096,128]{1,0:T(8,128)(2,1)} custom-call(s32[3]{0:T(128)} %pad_add_fusion.place_ref, s32[8,1,1024]{2,1,0:T(1,128)S(1)} %all-to-all-done.asked_ref, f32[4096,128]{1,0:T(8,128)S(1)} %copy-done, bf16[4096,128]{1,0:T(8,128)(2,1)S(1)} %copy-done.2), custom_call_target="tpu_custom_call" | custom-call | tf_op jit(solution)/shard_map/pallas_call | solution.py:132
  112.3 5.4 %all-to-all-start.1 = ((bf16[8,512,128]{2,1,0:T(8,128)(2,1)}), bf16[8,512,128]{2,1,0:T(8,128)(2,1)S(1)}, u32[]{:S(2)}, u32[]{:S(2)}) async-start(bf16[8,512,128]{2,1,0:T(8,128)(2,1)} %bitcast.19), calls=%async_computation.1 | async-start | bytes 2097152 | tf_op jit(solution)/shard_map/all_to_all | solution.py:255
  122.5 2.2 %collective-permute-done.15 = bf16[256,128]{1,0:T(8,128)(2,1)S(1)} collective-permute-done((bf16[256,128]{1,0:T(8,128)(2,1)S(1)}, bf16[256,128]{1,0:T(8,128)(2,1)S(1)}, u32[]{:S(2)}, u32[]{:S(2)}) %collective-permute-start.15) | collective-permute-done | bytes 65568 | tf_op jit(solution)/shard_map/ppermute | solution.py:317
  125.5 18.3 %all-to-all-done.1 = bf16[8,512,128]{2,1,0:T(8,128)(2,1)S(1)} async-done(((bf16[8,512,128]{2,1,0:T(8,128)(2,1)}), bf16[8,512,128]{2,1,0:T(8,128)(2,1)S(1)}, u32[]{:S(2)}, u32[]{:S(2)}) %all-to-all-start.1) | async-done | bytes 1048608 | tf_op jit(solution)/shard_map/all_to_all | solution.py:255
  (67 shorter events, 21.3 us)
Async XLA Ops:
  0.6 10.6 %collective-permute-start.2 = (bf16[512,128]{1,0:T(8,128)(2,1)}, bf16[512,128]{1,0:T(8,128)(2,1)S(1)}, u32[]{:S(2)}, u32[]{:S(2)}) collective-permute-start(bf16[512,128]{1,0:T(8,128)(2,1)} %param.9), channel_id=1, source_target_pairs={{0,16},{2,18},{4,20},{6,22},{8,24},{10,26},{12,28},{14,30},{16,0},... | collective-permute-start | bytes 393224 | tf_op jit(solution)/shard_map/ppermute | solution.py:252
  11.3 8.3 %collective-permute-start.3 = (bf16[1024,128]{1,0:T(8,128)(2,1)S(1)}, bf16[1024,128]{1,0:T(8,128)(2,1)S(1)}, u32[]{:S(2)}, u32[]{:S(2)}) collective-permute-start(bf16[1024,128]{1,0:T(8,128)(2,1)S(1)} %constant_dynamic-update-slice_fusion.refs_0_), channel_id=1, source_target_pairs={{0,4},{2,6},{4,0},{6,2},{8,12},{10,14},{12,8},{14,10},{16,20},{18,... | collective-permute-start | bytes 786440 | tf_op jit(solution)/shard_map/ppermute | solution.py:252
  12.9 9.2 %collective-permute-start.4 = (bf16[1024,128]{1,0:T(8,128)(2,1)S(1)}, bf16[1024,128]{1,0:T(8,128)(2,1)S(1)}, u32[]{:S(2)}, u32[]{:S(2)}) collective-permute-start(bf16[1024,128]{1,0:T(8,128)(2,1)S(1)} %constant_dynamic-update-slice_fusion.refs_0_), channel_id=1, source_target_pairs={{0,8},{2,10},{4,12},{6,14},{8,0},{10,2},{12,4},{14,6},{16,24},{18,... | collective-permute-start | bytes 786440 | tf_op jit(solution)/shard_map/ppermute | solution.py:252
  13.7 11.9 %collective-permute-start.5 = (bf16[1024,128]{1,0:T(8,128)(2,1)S(1)}, bf16[1024,128]{1,0:T(8,128)(2,1)S(1)}, u32[]{:S(2)}, u32[]{:S(2)}) collective-permute-start(bf16[1024,128]{1,0:T(8,128)(2,1)S(1)} %constant_dynamic-update-slice_fusion.refs_0_), channel_id=1, source_target_pairs={{0,12},{2,14},{4,8},{6,10},{8,4},{10,6},{12,0},{14,2},{16,28},{18,... | collective-permute-start | bytes 786440 | tf_op jit(solution)/shard_map/ppermute | solution.py:252
  14.9 27.3 %collective-permute-start.6 = (bf16[1024,128]{1,0:T(8,128)(2,1)S(1)}, bf16[1024,128]{1,0:T(8,128)(2,1)S(1)}, u32[]{:S(2)}, u32[]{:S(2)}) collective-permute-start(bf16[1024,128]{1,0:T(8,128)(2,1)S(1)} %constant_dynamic-update-slice_fusion.refs_0_), channel_id=1, source_target_pairs={{0,2},{2,0},{4,6},{6,4},{8,10},{10,8},{12,14},{14,12},{16,18},{18,... | collective-permute-start | bytes 786440 | tf_op jit(solution)/shard_map/ppermute | solution.py:252
  19.6 22.6 %collective-permute-start.7 = (bf16[1024,128]{1,0:T(8,128)(2,1)S(1)}, bf16[1024,128]{1,0:T(8,128)(2,1)S(1)}, u32[]{:S(2)}, u32[]{:S(2)}) collective-permute-start(bf16[1024,128]{1,0:T(8,128)(2,1)S(1)} %collective-permute-done.3.refs_1_), channel_id=1, source_target_pairs={{0,2},{2,0},{4,6},{6,4},{8,10},{10,8},{12,14},{14,12},{16,18},{18,... | collective-permute-start | bytes 786440 | tf_op jit(solution)/shard_map/ppermute | solution.py:252
  22.1 20.2 %collective-permute-start.8 = (bf16[1024,128]{1,0:T(8,128)(2,1)S(1)}, bf16[1024,128]{1,0:T(8,128)(2,1)S(1)}, u32[]{:S(2)}, u32[]{:S(2)}) collective-permute-start(bf16[1024,128]{1,0:T(8,128)(2,1)S(1)} %collective-permute-done.4.refs_2_), channel_id=1, source_target_pairs={{0,2},{2,0},{4,6},{6,4},{8,10},{10,8},{12,14},{14,12},{16,18},{18,... | collective-permute-start | bytes 786440 | tf_op jit(solution)/shard_map/ppermute | solution.py:252
  25.6 16.6 %collective-permute-start.9 = (bf16[1024,128]{1,0:T(8,128)(2,1)S(1)}, bf16[1024,128]{1,0:T(8,128)(2,1)S(1)}, u32[]{:S(2)}, u32[]{:S(2)}) collective-permute-start(bf16[1024,128]{1,0:T(8,128)(2,1)S(1)} %collective-permute-done.5.refs_3_), channel_id=1, source_target_pairs={{0,2},{2,0},{4,6},{6,4},{8,10},{10,8},{12,14},{14,12},{16,18},{18,... | collective-permute-start | bytes 786440 | tf_op jit(solution)/shard_map/ppermute | solution.py:252
  27.8 13.2 %all-to-all-start = ((s32[8,1,1024]{2,1,0:T(1,128)}), s32[8,1,1024]{2,1,0:T(1,128)S(1)}, u32[]{:S(2)}, u32[]{:S(2)}) async-start(s32[8,1,1024]{2,1,0:T(1,128)} %reduce_max.12), calls=%async_computation | async-start | bytes 65536 | tf_op jit(solution)/shard_map/all_to_all | solution.py:255
  41.1 1.2 collective-permute-start.1
  41.7 21.1 %copy-start.7 = (f32[4096]{0:T(1024)S(1)}, f32[4096]{0:T(1024)}, u32[]{:S(2)}) copy-start(f32[4096]{0:T(1024)} %param.11) | copy-start | bytes 49156
  47.8 15.0 %collective-permute-start.10 = (bf16[2048,128]{1,0:T(8,128)(2,1)S(1)}, bf16[2048,128]{1,0:T(8,128)(2,1)}, u32[]{:S(2)}, u32[]{:S(2)}) collective-permute-start(bf16[2048,128]{1,0:T(8,128)(2,1)S(1)} %shard_map.103.own_ref), channel_id=1, source_target_pairs={{0,1},{1,0},{2,3},{3,2},{4,5},{5,4},{6,7},{7,6},{8,9},{9,8},{10,11... | collective-permute-start | bytes 1572872 | tf_op jit(solution)/shard_map/ppermute | solution.py:288
  55.0 18.2 %collective-permute-start.11 = (bf16[2048,128]{1,0:T(8,128)(2,1)S(1)}, bf16[2048,128]{1,0:T(8,128)(2,1)S(1)}, u32[]{:S(2)}, u32[]{:S(2)}) collective-permute-start(bf16[2048,128]{1,0:T(8,128)(2,1)S(1)} %shard_map.105.own_ref), channel_id=1, source_target_pairs={{0,1},{1,0},{2,3},{3,2},{4,5},{5,4},{6,7},{7,6},{8,9},{9,8},{10,11... | collective-permute-start | bytes 1572872 | tf_op jit(solution)/shard_map/ppermute | solution.py:288
  66.8 12.2 %copy-start.3 = (bf16[2048,128]{1,0:T(8,128)(2,1)}, bf16[2048,128]{1,0:T(8,128)(2,1)S(1)}, u32[]{:S(2)}) copy-start(bf16[2048,128]{1,0:T(8,128)(2,1)S(1)} %get-tuple-element.15.delta_ref) | copy-start | bytes 1572868
  66.8 15.2 %collective-permute-start.14 = (bf16[2048,128]{1,0:T(8,128)(2,1)S(1)}, bf16[2048,128]{1,0:T(8,128)(2,1)S(1)}, u32[]{:S(2)}, u32[]{:S(2)}) collective-permute-start(bf16[2048,128]{1,0:T(8,128)(2,1)S(1)} %get-tuple-element.15.delta_ref), channel_id=1, source_target_pairs={{0,2},{2,0},{4,6},{6,4},{8,10},{10,8},{12,14},{14,12},{16,18},{18,... | collective-permute-start | bytes 1572872 | tf_op jit(solution)/shard_map/ppermute | solution.py:252
  76.2 12.1 %collective-permute-start.13 = (bf16[2048,128]{1,0:T(8,128)(2,1)}, bf16[2048,128]{1,0:T(8,128)(2,1)}, u32[]{:S(2)}, u32[]{:S(2)}) collective-permute-start(bf16[2048,128]{1,0:T(8,128)(2,1)} %get-tuple-element.14.delta_ref), channel_id=1, source_target_pairs={{0,2},{2,0},{4,6},{6,4},{8,10},{10,8},{12,14},{14,12},{16,18},{18,... | collective-permute-start | bytes 1572872 | tf_op jit(solution)/shard_map/ppermute | solution.py:252
  79.0 18.1 %collective-permute-start = (bf16[4096,128]{1,0:T(8,128)(2,1)}, bf16[4096,128]{1,0:T(8,128)(2,1)S(1)}, u32[]{:S(2)}, u32[]{:S(2)}) collective-permute-start(bf16[4096,128]{1,0:T(8,128)(2,1)} %convert_element_type.22), channel_id=1, source_target_pairs={{0,2},{2,0},{4,6},{6,4},{8,10},{10,8},{12,14},{14,12},{16,18},{18,... | collective-permute-start | bytes 3145736 | tf_op jit(solution)/shard_map/ppermute | solution.py:252
  79.5 2.5 %collective-permute-start.12 = (s32[8,512]{1,0:T(8,128)S(1)}, s32[8,512]{1,0:T(8,128)S(1)}, u32[]{:S(2)}, u32[]{:S(2)}) collective-permute-start(s32[8,512]{1,0:T(8,128)S(1)} %reshape.102.slot_ref), channel_id=1, source_target_pairs={{0,2},{2,0},{4,6},{6,4},{8,10},{10,8},{12,14},{14,12},{16,18},{18,... | collective-permute-start | bytes 49160 | tf_op jit(solution)/shard_map/ppermute | solution.py:252
  92.9 19.4 %all-to-all-start.2 = ((bf16[8,256,128]{2,1,0:T(8,128)(2,1)}), bf16[8,256,128]{2,1,0:T(8,128)(2,1)}, u32[]{:S(2)}, u32[]{:S(2)}) async-start(bf16[8,256,128]{2,1,0:T(8,128)(2,1)} %bitcast.20), calls=%async_computation.2 | async-start | bytes 1048576 | tf_op jit(solution)/shard_map/all_to_all | solution.py:255
  111.7 6.0 %copy-start.8 = (f32[2048,128]{1,0:T(8,128)S(1)}, f32[2048,128]{1,0:T(8,128)}, u32[]{:S(2)}) copy-start(f32[2048,128]{1,0:T(8,128)} %get-tuple-element.10) | copy-start | bytes 3145732
  111.7 6.0 %copy-start.9 = (f32[2048,128]{1,0:T(8,128)S(1)}, f32[2048,128]{1,0:T(8,128)}, u32[]{:S(2)}) copy-start(f32[2048,128]{1,0:T(8,128)} %get-tuple-element.11) | copy-start | bytes 3145732
  112.3 31.4 %all-to-all-start.1 = ((bf16[8,512,128]{2,1,0:T(8,128)(2,1)}), bf16[8,512,128]{2,1,0:T(8,128)(2,1)S(1)}, u32[]{:S(2)}, u32[]{:S(2)}) async-start(bf16[8,512,128]{2,1,0:T(8,128)(2,1)} %bitcast.19), calls=%async_computation.1 | async-start | bytes 2097152 | tf_op jit(solution)/shard_map/all_to_all | solution.py:255
  117.8 6.9 %copy-start.10 = (f32[512,128]{1,0:T(8,128)S(1)}, f32[512,128]{1,0:T(8,128)}, u32[]{:S(2)}) copy-start(f32[512,128]{1,0:T(8,128)} %param.12) | copy-start | bytes 786436
  120.4 4.3 %collective-permute-start.15 = (bf16[256,128]{1,0:T(8,128)(2,1)S(1)}, bf16[256,128]{1,0:T(8,128)(2,1)S(1)}, u32[]{:S(2)}, u32[]{:S(2)}) collective-permute-start(bf16[256,128]{1,0:T(8,128)(2,1)S(1)} %reduce_sum.25), channel_id=1, source_target_pairs={{0,1},{1,0},{2,3},{3,2},{4,5},{5,4},{6,7},{7,6},{8,9},{9,8},{10,11... | collective-permute-start | bytes 196616 | tf_op jit(solution)/shard_map/ppermute | solution.py:317
  (9 other events, 18.2 us)

commit v4 on v3

v4 whole, which is shorter than its diff:
```python
import functools
import jax
import jax.numpy as jnp
from jax import lax
from jax.experimental import pallas as pl
from jax.experimental.pallas import tpu as pltpu
from jax.sharding import PartitionSpec as P

LEARN = 0.5
EPSILON = 1e-06
SPLIT = 4
PARTS = (2, 2)
NEAR_BYTES = 1 << 21
VMEM = pl.BlockSpec(memory_space=pltpu.VMEM)


def near(values, copies=1):
    if copies * values.size * values.dtype.itemsize > NEAR_BYTES:
        return values
    return pltpu.with_memory_space_constraint(values, pltpu.MemorySpace.VMEM)


def column_of(row, lanes):
    return jnp.broadcast_to(row, (lanes, row.shape[1])).T


def bits_of(count):
    assert count & (count - 1) == 0
    return count.bit_length() - 1


def split_index(index, low_count):
    return lax.shift_right_arithmetic(index, bits_of(low_count)), lax.bitwise_and(index, low_count - 1)


def position():
    device = lax.axis_index("table")
    return lax.bitwise_and(device, 1), lax.shift_right_logical(device, 1), lax.axis_index("dp")


def side_of(line, side):
    count = line.shape[1] // 2
    return jnp.where(side == 0, line[:, :count], line[:, count:])


def add_segments(total_ref, index, rows, first):
    low_count, spread_width = total_ref.shape
    width = rows.shape[1]
    split = spread_width // width
    block, low = split_index(index, low_count)
    low = jnp.where((block < 0) | (block >= split), -1, low)
    hits = (
        (lax.broadcasted_iota(jnp.int32, (low_count, index.shape[1]), 0) == low)
        .astype(jnp.float32)
        .astype(jnp.bfloat16)
    )
    block_column = column_of(block, width)
    rows = rows.astype(jnp.float32)
    spread = jnp.concatenate(
        [jnp.where(block_column == i, rows, 0.0).astype(jnp.bfloat16) for i in range(split)], axis=1
    )
    part = jnp.dot(hits, spread, preferred_element_type=jnp.float32)
    if first:
        total_ref[...] = part
    else:
        total_ref[...] += part


def put_segments(out_ref, total_ref):
    low_count, width = total_ref.shape[0], out_ref.shape[1]
    for i in range(total_ref.shape[1] // width):
        out_ref[i * low_count : (i + 1) * low_count, :] = total_ref[
            :, i * width : (i + 1) * width
        ].astype(out_ref.dtype)


def segment_kernel(asked_ref, peer_asked_ref, *refs, base):
    out_ref, total_ref = refs[-2:]
    count = (len(refs) - 2) // 2
    core, chip, _ = position()
    for k in range(count):
        lines = []
        for ref in (asked_ref, peer_asked_ref):
            for source in (chip ^ k, chip ^ k ^ count):
                lines.append(side_of(ref[source], core))
        index = jnp.concatenate(lines, axis=1) - base
        rows = jnp.concatenate([refs[k][...], refs[count + k][...]], axis=0)
        add_segments(total_ref, index, rows, k == 0)
    put_segments(out_ref, total_ref)


def row_gradients(asked, peer_asked, grads, peer_grads, base, row_count):
    width = grads[0].shape[1]
    split = SPLIT if row_count > 4 * 256 else SPLIT // 2
    return pl.pallas_call(
        functools.partial(segment_kernel, base=base),
        in_specs=[VMEM] * (2 + 2 * len(grads)),
        out_specs=VMEM,
        out_shape=pltpu.VMEM((row_count, width), jnp.bfloat16),
        scratch_shapes=[pltpu.VMEM((row_count // split, split * width), jnp.float32)],
    )(near(asked), near(peer_asked), *[near(g, 2 * len(grads)) for g in (*grads, *peer_grads)])


def round_kernel(rows_ref, out_ref, held_ref, sems):
    chunk = rows_ref.shape[0] // SPLIT
    copies = []
    for i in range(SPLIT):
        at = pl.ds(i * chunk, chunk)
        copies.append(pltpu.make_async_copy(rows_ref.at[at, :], held_ref.at[at, :], sems.at[i]))
        copies[i].start()
    for i in range(SPLIT):
        copies[i].wait()
        at = slice(i * chunk, (i + 1) * chunk)
        out_ref[at, :] = held_ref[at, :].astype(jnp.bfloat16)


def rounded(table):
    return pl.pallas_call(
        round_kernel,
        in_specs=[pl.BlockSpec(memory_space=pl.ANY)],
        out_specs=VMEM,
        out_shape=jax.ShapeDtypeStruct(table.shape, jnp.bfloat16),
        scratch_shapes=[pltpu.VMEM(table.shape, table.dtype), pltpu.SemaphoreType.DMA((SPLIT,))],
    )(table)


def gather_kernel(asked_ref, own_ref, peer_ref, out_ref, held_ref, *, together):
    chips = asked_ref.shape[0]
    low_count, width = held_ref.shape[1], out_ref.shape[1]
    bags = out_ref.shape[0] // chips
    core, _, _ = position()
    for i in range(SPLIT):
        at = slice(i * low_count, (i + 1) * low_count)
        held_ref[0, :, i * width : (i + 1) * width] = own_ref[at, :]
        held_ref[1, :, i * width : (i + 1) * width] = peer_ref[at, :]
    for j in range(0, chips, together):
        total = jnp.zeros((together * bags, width), jnp.float32)
        lane = lax.broadcasted_iota(jnp.int32, total.shape, 1)
        for side in range(2):
            index = jnp.concatenate(
                [side_of(asked_ref[j + i], core ^ side) for i in range(together)], axis=1
            )
            block, low = split_index(column_of(index, width), low_count)
            hits = jnp.concatenate(
                [
                    (lane == low - first).astype(jnp.float32).astype(jnp.bfloat16)
                    for first in range(0, low_count, width)
                ],
                axis=1,
            )
            found = jnp.dot(hits, held_ref[side], preferred_element_type=jnp.float32)
            for i in range(SPLIT):
                total += jnp.where(block == i, found[:, i * width : (i + 1) * width], 0.0)
        out_ref[j * bags : (j + together) * bags, :] = total.astype(out_ref.dtype)


def chip_rows(asked, own_rows, peer_rows):
    row_count, width = own_rows.shape
    chips, bags = asked.shape[0], asked.shape[2] // 2
    return pl.pallas_call(
        functools.partial(gather_kernel, together=2),
        in_specs=[VMEM, VMEM, VMEM],
        out_specs=VMEM,
        out_shape=jax.ShapeDtypeStruct((chips * bags, width), jnp.bfloat16),
        scratch_shapes=[pltpu.VMEM((2, row_count // SPLIT, SPLIT * width), jnp.bfloat16)],
    )(near(asked), own_rows, near(peer_rows))


def update_kernel(own_ref, other_ref, table_ref, accum_ref, *refs, base, chunk):
    new_table_ref, new_accum_ref, delta_ref, old_ref, fresh_ref, in_sems, out_sems = refs[-7:]
    rows, width = own_ref.shape
    loads, stores = [], []
    for i in range(rows // chunk):
        here, there = pl.ds(i * chunk, chunk), pl.ds(base + i * chunk, chunk)
        loads.append(pltpu.make_async_copy(table_ref.at[there, :], old_ref.at[here, :], in_sems.at[i]))
        stores.append(
            pltpu.make_async_copy(fresh_ref.at[here, :], new_table_ref.at[there, :], out_sems.at[i])
        )
    for copy in loads:
        copy.start()
    diagonal = lax.broadcasted_iota(jnp.int32, (width, width), 0) == lax.broadcasted_iota(
        jnp.int32, (width, width), 1
    )
    for j in range(rows // width):
        i, within = divmod(j * width, chunk)
        if within == 0:
            loads[i].wait()
        at = slice(j * width, (j + 1) * width)
        line = base // width + j
        grads = own_ref[at, :].astype(jnp.float32) + other_ref[at, :].astype(jnp.float32)
        scaled = jnp.where(diagonal, accum_ref[line : line + 1, :] * width, 0.0)
        fresh_accum = jnp.sum(grads * grads + scaled, axis=1, keepdims=True) * (1.0 / width)
        old_rows = old_ref[at, :]
        fresh_rows = old_rows - LEARN * grads / jnp.sqrt(fresh_accum + EPSILON)
        fresh_ref[at, :] = fresh_rows
        if within + width == chunk:
            stores[i].start()
        delta_ref[at, :] = (fresh_rows - old_rows).astype(jnp.bfloat16)
        new_accum_ref[j : j + 1, :] = jnp.sum(
            jnp.where(diagonal, fresh_accum, 0.0), axis=0, keepdims=True
        )
    for copy in stores:
        copy.wait()


def update(own, other, table, accum, base, unfinished):
    rows, width = own.shape
    chunk = min(256, rows)
    anywhere = pl.BlockSpec(memory_space=pl.ANY)
    return pl.pallas_call(
        functools.partial(update_kernel, base=base, chunk=chunk),
        in_specs=[VMEM, VMEM, anywhere, VMEM] + [anywhere] * len(unfinished),
        out_specs=[anywhere, VMEM, VMEM],
        out_shape=[
            jax.ShapeDtypeStruct(table.shape, jnp.float32),
            jax.ShapeDtypeStruct((rows // width, width), jnp.float32),
            pltpu.VMEM((rows, width), jnp.bfloat16),
        ],
        scratch_shapes=[
            pltpu.VMEM((rows, width), jnp.float32),
            pltpu.VMEM((rows, width), jnp.float32),
            pltpu.SemaphoreType.DMA((rows // chunk,)),
            pltpu.SemaphoreType.DMA((rows // chunk,)),
        ],
        input_output_aliases={4: 0} if unfinished else {},
    )(near(own), near(other), table, near(accum), *unfinished)


def parity_kernel(slot_ref, peer_slot_ref, delta_ref, peer_delta_ref, *refs, base, holder_rows, dp_count, tile, last):
    refs, total_ref = refs[:-1], refs[-1]
    if base > 0:
        start_ref, refs, held_ref, sem = refs[0], refs[1:-2], refs[-2], refs[-1]
        copy = pltpu.make_async_copy(start_ref, held_ref, sem)
        copy.start()
    core, chip, dp_index = position()
    part_count = holder_rows // dp_count
    line_width = slot_ref.shape[1]
    width = delta_ref.shape[1]
    for k in range(delta_ref.shape[0] // tile):
        first = (base + k * tile) // line_width
        slot = jnp.concatenate(
            [
                ref[first + i : first + i + 1, :]
                for ref in (slot_ref, peer_slot_ref)
                for i in range(tile // line_width)
            ],
            axis=1,
        )
        holder, offset = split_index(slot, holder_rows)
        part, offset = split_index(offset, part_count)
        mine = (lax.bitwise_and(holder, 1) == core) & (part == dp_index)
        target = lax.bitwise_xor(lax.shift_right_arithmetic(holder, 1), chip) * part_count + offset
        at = slice(k * tile, (k + 1) * tile)
        rows = jnp.concatenate([delta_ref[at, :], peer_delta_ref[at, :]], axis=0)
        add_segments(total_ref, jnp.where(mine, target, -1), rows, k == 0)
    if base > 0:
        copy.wait()
        total_ref[...] += held_ref[...]
    if not last:
        refs[-1][...] = total_ref[...]
        return
    low_count = total_ref.shape[0]
    out_refs = refs[-(low_count * SPLIT // part_count) :]
    for i, out_ref in enumerate(out_refs):
        block, low = divmod(i * part_count, low_count)
        out_ref[...] = total_ref[
            low : low + part_count, block * width : (block + 1) * width
        ].astype(out_ref.dtype)


def parity_changes(slot, peer_slot, delta, peer_delta, base, holder_rows, dp_count, chip_count, start, last):
    width = delta.shape[1]
    part_count = holder_rows // dp_count
    segment_count = chip_count * part_count
    held = pltpu.VMEM((segment_count // SPLIT, SPLIT * width), jnp.float32)
    return pl.pallas_call(
        functools.partial(
            parity_kernel, base=base, holder_rows=holder_rows, dp_count=dp_count,
            tile=min(1024, delta.shape[0]), last=last,
        ),
        in_specs=[VMEM] * 4 + [pl.BlockSpec(memory_space=pl.ANY)] * len(start),
        out_specs=[VMEM] * chip_count if last else VMEM,
        out_shape=[pltpu.VMEM((part_count, width), jnp.bfloat16)] * chip_count
        if last
        else jax.ShapeDtypeStruct(held.shape, held.dtype),
        scratch_shapes=([held, pltpu.SemaphoreType.DMA] if start else []) + [held],
    )(*map(near, (slot, peer_slot, delta, peer_delta)), *start)


def on_device(owners, local_rows, grad_pooled, table, accum, parity, parity_slot):
    table_count = lax.axis_size("table")
    dp_count = lax.axis_size("dp")
    chip_count = table_count // 2
    half = table_count // 2
    bag_count, per_bag = owners.shape
    row_count, width = table.shape
    parity_count = parity.shape[0]
    dp_index = lax.axis_index("dp")
    same_core = [list(range(c, table_count, 2)) for c in range(2)]

    def swap(values, distance):
        return lax.ppermute(values, "table", [(i, i ^ distance) for i in range(table_count)])

    def exchange(values):
        return lax.all_to_all(
            values, "table", split_axis=0, concat_axis=0, axis_index_groups=same_core, tiled=True
        )

    far_grads = swap(grad_pooled, half)

    lanes = jnp.arange(2 * bag_count, dtype=jnp.int32)[None, None, None, :]
    chips = jnp.arange(chip_count, dtype=jnp.int32)[:, None, None, None]
    owners_twice = jnp.tile(owners.T, (1, 2)).reshape(1, 1, per_bag, 2 * bag_count)
    rows_twice = jnp.tile(local_rows.T, (1, 2)).reshape(1, 1, per_bag, 2 * bag_count)
    named = owners_twice == 2 * chips + (lanes >= bag_count).astype(jnp.int32)
    requests = jnp.max(jnp.where(named, rows_twice, -1), axis=2)
    asked = exchange(requests)
    own_table = rounded(table)
    peer_table = swap(own_table, 1)
    line_width = 4 * width
    slot_lines = parity_slot.reshape(-1, line_width)
    peer_slot_lines = swap(slot_lines, 1)

    grads = [jnp.concatenate([grad_pooled, far_grads], axis=0)]
    for k in range(1, chip_count // 2):
        grads.append(swap(grads[0], 2 * k))
    peer_asked = swap(asked, 1)
    peer_grads = []
    for values in grads:
        peer_grads.append(swap(values, 1))

    fetched = chip_rows(asked, own_table, peer_table)

    halves, bases = [], []
    for part, share in enumerate(PARTS):
        part_rows = row_count // share
        bases.append(sum(row_count // other for other in PARTS[:part]))
        mine = row_gradients(asked, peer_asked, grads, peer_grads, bases[part], part_rows)
        distance = 1
        other = lax.ppermute(mine, "dp", [(i, i ^ 1) for i in range(dp_count)])
        while 2 * distance < dp_count:
            distance *= 2
            mine = (mine.astype(jnp.float32) + other.astype(jnp.float32)).astype(jnp.bfloat16)
            other = lax.ppermute(mine, "dp", [(i, i ^ distance) for i in range(dp_count)])
        halves.append((mine, other))

    returned = exchange(fetched.reshape(chip_count, bag_count, width))

    new_table, accums, changes = [], [], []
    accum_lines = accum.reshape(-1, width)
    for part, (mine, other) in enumerate(halves):
        fresh, fresh_accum, delta = update(mine, other, table, accum_lines, bases[part], new_table)
        new_table = [fresh]
        accums.append(fresh_accum)
        peer_delta = swap(delta, 1)
        changes = parity_changes(
            slot_lines, peer_slot_lines, delta, peer_delta, bases[part],
            parity_count, dp_count, chip_count, changes, part == len(PARTS) - 1,
        )
        if part < len(PARTS) - 1:
            changes = [changes]
    arrived = [changes[0]]
    for k in range(1, chip_count):
        arrived.append(swap(changes[k], 2 * k))
    pooled = jnp.sum(returned.astype(jnp.float32), axis=0).astype(jnp.bfloat16)
    new_accum = jnp.concatenate(accums, axis=0).reshape(row_count)
    part = sum(values.astype(jnp.float32) for values in arrived).astype(jnp.bfloat16)
    if dp_count == 2:
        other = lax.ppermute(part, "dp", [(0, 1), (1, 0)])
        parts = jnp.where(dp_index == 0, jnp.stack([part, other]), jnp.stack([other, part]))
    else:
        parts = lax.all_gather(part, "dp", axis=0)
    new_parity = parity + parts.reshape(parity_count, width).astype(jnp.float32)
    return (pooled, new_table[0], new_accum, new_parity)


def solution(mesh):
    in_specs = (
        P(("table", "dp"), None),
        P(("table", "dp"), None),
        P(("table", "dp"), None),
        P("table", None),
        P("table"),
        P("table", None),
        P("table"),
    )
    out_specs = (P(("table", "dp"), None), P("table", None), P("table"), P("table", None))

    return jax.shard_map(on_device, mesh=mesh, in_specs=in_specs, out_specs=out_specs, check_vma=False)
```

time: 145 us -> 111 us (0.77)
  waiting for transfers between devices: 60.5 us -> 16.7 us
  blocking collectives: 0 us -> 13.8 us
  local copies, waits for them, and re-layouts: 9.73 us -> 0.1 us
  starting transfers between devices: 28.2 us -> 34.9 us
  other arithmetic: 8.26 us -> 3.68 us
  Pallas kernels: 37 us -> 40.8 us
    all_to_all x3 -> x1, waiting for transfers between devices: 25.6 us -> 0.01 us  [exchange(): lax.all_to_all(values, 'table', split_axis=0, concat_axis=0, axis_index_g...]
    ppermute x13 -> x20, starting transfers between devices: 8.41 us -> 26.9 us  [swap(): lax.ppermute(values, 'table', [(i, i ^ distance) for i in range(table_cou...]
    all_to_all x0 -> x1, blocking collectives: none -> 13.8 us  [exchange(): lax.all_to_all(values, 'table', split_axis=0, concat_axis=0, axis_index_g...]
    ppermute x2, waiting for transfers between devices: 13.5 us -> 0.01 us  [on_device(): other = lax.ppermute(mine, 'dp', [(i, i ^ 1) for i in range(dp_count)])]
    all_to_all x3 -> x1, starting transfers between devices: 16.1 us -> 4.24 us  [exchange(): lax.all_to_all(values, 'table', split_axis=0, concat_axis=0, axis_index_g...]
    unnamed x29 -> x17, local copies, waits for them, and re-layouts: 7.63 us -> 0.05 us
    ppermute x13 -> x20, waiting for transfers between devices: 19.3 us -> 14.5 us  [swap(): lax.ppermute(values, 'table', [(i, i ^ distance) for i in range(table_cou...]
    pallas_call x5 -> x6, Pallas kernels: 29 us -> 33.7 us  [the longest x1 11.9 us: chip_rows(): pl.pallas_call(functools.partial(gather_kernel, together=2), in_specs=[VM...]
  transfers between devices with their start and end apart: 19 -> 24, of which waited for: 12 -> 11; matrix products, arithmetic and copies ran while one was open for 7% -> 2% of each run, Pallas kernels for 22% -> 34%
where the time goes in v4:
time: 111 us
  Pallas kernels  40.8 us (37%)
  starting transfers between devices  34.9 us (31%)
  waiting for transfers between devices  16.7 us (15%)
  blocking collectives  13.8 us (12%)
  other arithmetic  3.68 us (3%)
    ppermute x20, starting transfers between devices, swap(): lax.ppermute(values, 'table', [(i, i ^ distance) for i in range(table_cou...  26.9 us
    ppermute x20, waiting for transfers between devices, swap(): lax.ppermute(values, 'table', [(i, i ^ distance) for i in range(table_cou...  14.5 us
    all_to_all x1, blocking collectives, exchange(): lax.all_to_all(values, 'table', split_axis=0, concat_axis=0, axis_index_g...  13.8 us
    pallas_call x1, Pallas kernels, chip_rows(): pl.pallas_call(functools.partial(gather_kernel, together=2), in_specs=[VM...  11.9 us
    pallas_call x2, Pallas kernels, row_gradients(): pl.pallas_call(functools.partial(segment_kernel, base=base), in_specs=[VM...  9.79 us
    pallas_call x2, Pallas kernels, update(): pl.pallas_call(functools.partial(update_kernel, base=base, chunk=chunk),...  9.32 us
    pallas_call x2, Pallas kernels, parity_changes(): pl.pallas_call(functools.partial(parity_kernel, base=base, holder_rows=ho...  7.11 us
    all_to_all x1, starting transfers between devices, exchange(): lax.all_to_all(values, 'table', split_axis=0, concat_axis=0, axis_index_g...  4.24 us
  transfers between devices with their start and end apart: 24, of which 11 were waited for; matrix products, arithmetic and copies ran while one was open for 2% of the time, Pallas kernels for 34%

profile of v4, /device:TPU:0, one launch (start us, length us, event | category | flops | bytes accessed | tf_op | source)
XLA Modules:
  0.0 110.7 jit_solution(14721443384627140922)
XLA Ops:
  0.7 2.6 %shard_map.102.own_ref = bf16[4096,128]{1,0:T(8,128)(2,1)} custom-call(f32[4096,128]{1,0:T(8,128)} %table_ref.3), custom_call_target="tpu_custom_call" | custom-call | tf_op jit(solution)/shard_map/pallas_call | solution.py:118
  3.8 3.7 %collective-permute-start.2 = (bf16[512,128]{1,0:T(8,128)(2,1)S(1)}, bf16[512,128]{1,0:T(8,128)(2,1)S(1)}, u32[]{:S(2)}, u32[]{:S(2)}) collective-permute-start(bf16[512,128]{1,0:T(8,128)(2,1)S(1)} %copy-done.2), channel_id=1, source_target_pairs={{0,16},{2,18},{4,20},{6,22},{8,24},{10,26},{12,28},{14,30},{16,0},... | collective-permute-start | bytes 393224 | tf_op jit(solution)/shard_map/ppermute | solution.py:302
  7.5 6.9 %collective-permute-done.2 = bf16[512,128]{1,0:T(8,128)(2,1)S(1)} collective-permute-done((bf16[512,128]{1,0:T(8,128)(2,1)S(1)}, bf16[512,128]{1,0:T(8,128)(2,1)S(1)}, u32[]{:S(2)}, u32[]{:S(2)}) %collective-permute-start.2) | collective-permute-done | bytes 131104 | tf_op jit(solution)/shard_map/ppermute | solution.py:302
  14.4 1.6 %collective-permute-start.3 = (bf16[1024,128]{1,0:T(8,128)(2,1)S(1)}, bf16[1024,128]{1,0:T(8,128)(2,1)S(1)}, u32[]{:S(2)}, u32[]{:S(2)}) collective-permute-start(bf16[1024,128]{1,0:T(8,128)(2,1)S(1)} %constant_dynamic-update-slice_fusion.refs_0_), channel_id=1, source_target_pairs={{0,4},{2,6},{4,0},{6,2},{8,12},{10,14},{12,8},{14,10},{16,20},{18,... | collective-permute-start | bytes 786440 | tf_op jit(solution)/shard_map/ppermute | solution.py:302
  16.7 1.2 %collective-permute-start.5 = (bf16[1024,128]{1,0:T(8,128)(2,1)S(1)}, bf16[1024,128]{1,0:T(8,128)(2,1)S(1)}, u32[]{:S(2)}, u32[]{:S(2)}) collective-permute-start(bf16[1024,128]{1,0:T(8,128)(2,1)S(1)} %constant_dynamic-update-slice_fusion.refs_0_), channel_id=1, source_target_pairs={{0,12},{2,14},{4,8},{6,10},{8,4},{10,6},{12,0},{14,2},{16,28},{18,... | collective-permute-start | bytes 786440 | tf_op jit(solution)/shard_map/ppermute | solution.py:302
  18.2 13.8 %all_to_all.10.asked_ref = s32[8,1,1024]{2,1,0:T(1,128)S(1)} all-to-all(s32[8,1,1024]{2,1,0:T(1,128)S(1)} %reduce_max.12), channel_id=1, replica_groups={{0,4,8,12,16,20,24,28},{2,6,10,14,18,22,26,30},{1,5,9,13,17,21,25,29},{..., dimensions={0} | all-to-all | bytes 65536 | tf_op jit(solution)/shard_map/all_to_all | solution.py:305
  35.9 4.9 %shard_map.105.own_ref = bf16[2048,128]{1,0:T(8,128)(2,1)S(1)} custom-call(s32[8,1,1024]{2,1,0:T(1,128)S(1)} %all_to_all.10.asked_ref, s32[8,1,1024]{2,1,0:T(1,128)S(1)} %collective-permute-done.1.peer_asked_ref, bf16[1024,128]{1,0:T(8,128)(2,1)S(1)} %constant_dynamic-update-slice_fusion.refs_0_, bf16[1024,128]{1,0:T(8,128)(2,1)S(1)} %collective-permute-done.3.refs_1_, ...), custom_call_target="tpu_custom_call" | custom-call | tf_op jit(solution)/shard_map/pallas_call | solution.py:95
  40.8 1.6 %collective-permute-start.11 = (bf16[2048,128]{1,0:T(8,128)(2,1)S(1)}, bf16[2048,128]{1,0:T(8,128)(2,1)}, u32[]{:S(2)}, u32[]{:S(2)}) collective-permute-start(bf16[2048,128]{1,0:T(8,128)(2,1)S(1)} %shard_map.105.own_ref), channel_id=1, source_target_pairs={{0,1},{1,0},{2,3},{3,2},{4,5},{5,4},{6,7},{7,6},{8,9},{9,8},{10,11... | collective-permute-start | bytes 1572872 | tf_op jit(solution)/shard_map/ppermute | solution.py:340
  42.3 4.9 %shard_map.104.own_ref = bf16[2048,128]{1,0:T(8,128)(2,1)S(1)} custom-call(s32[8,1,1024]{2,1,0:T(1,128)S(1)} %all_to_all.10.asked_ref, s32[8,1,1024]{2,1,0:T(1,128)S(1)} %collective-permute-done.1.peer_asked_ref, bf16[1024,128]{1,0:T(8,128)(2,1)S(1)} %constant_dynamic-update-slice_fusion.refs_0_, bf16[1024,128]{1,0:T(8,128)(2,1)S(1)} %collective-permute-done.3.refs_1_, ...), custom_call_target="tpu_custom_call" | custom-call | tf_op jit(solution)/shard_map/pallas_call | solution.py:95
  47.8 11.9 %shard_map.103 = bf16[4096,128]{1,0:T(8,128)(2,1)} custom-call(s32[8,1,1024]{2,1,0:T(1,128)S(1)} %all_to_all.10.asked_ref, bf16[4096,128]{1,0:T(8,128)(2,1)} %shard_map.102.own_ref, bf16[4096,128]{1,0:T(8,128)(2,1)} %collective-permute-done.peer_ref), custom_call_target="tpu_custom_call" | custom-call | tf_op jit(solution)/shard_map/pallas_call | solution.py:160
  59.8 4.2 %all-to-all-start.1 = ((bf16[8,512,128]{2,1,0:T(8,128)(2,1)}), bf16[8,512,128]{2,1,0:T(8,128)(2,1)}, u32[]{:S(2)}, u32[]{:S(2)}) async-start(bf16[8,512,128]{2,1,0:T(8,128)(2,1)} %bitcast.15), calls=%async_computation.1 | async-start | bytes 2097152 | tf_op jit(solution)/shard_map/all_to_all | solution.py:305
  64.1 4.7 %shard_map.106 = (f32[4096,128]{1,0:T(8,128)}, f32[16,128]{1,0:T(8,128)}, bf16[2048,128]{1,0:T(8,128)(2,1)S(1)}) custom-call(bf16[2048,128]{1,0:T(8,128)(2,1)S(1)} %shard_map.105.own_ref, bf16[2048,128]{1,0:T(8,128)(2,1)} %collective-permute-done.11.other_ref, f32[4096,128]{1,0:T(8,128)} %table_ref.3, f32[32,128]{1,0:T(8,128)S(1)} %bitcast.13), custom_call_target="tpu_custom_call" | custom-call | tf_op jit(solution)/shard_map/pallas_call | solution.py:210
  68.8 4.7 %shard_map.107 = (f32[4096,128]{1,0:T(8,128)}, f32[16,128]{1,0:T(8,128)}, bf16[2048,128]{1,0:T(8,128)(2,1)S(1)}) custom-call(bf16[2048,128]{1,0:T(8,128)(2,1)S(1)} %shard_map.104.own_ref, bf16[2048,128]{1,0:T(8,128)(2,1)} %collective-permute-done.10.other_ref, f32[4096,128]{1,0:T(8,128)} %table_ref.3, ...), custom_call_target="tpu_custom_call", output_to_operand_aliasing={{0}: (4, {})} | custom-call | tf_op jit(solution)/shard_map/pallas_call | solution.py:210
  74.2 1.4 %collective-permute-done.12.peer_slot_ref = s32[8,512]{1,0:T(8,128)S(1)} collective-permute-done((s32[8,512]{1,0:T(8,128)S(1)}, s32[8,512]{1,0:T(8,128)S(1)}, u32[]{:S(2)}, u32[]{:S(2)}) %collective-permute-start.12) | collective-permute-done | bytes 16416 | tf_op jit(solution)/shard_map/ppermute | solution.py:302
  75.6 3.5 %shard_map.108.refs_0_ = f32[512,512]{1,0:T(8,128)} custom-call(s32[8,512]{1,0:T(8,128)S(1)} %reshape.99.slot_ref, s32[8,512]{1,0:T(8,128)S(1)} %collective-permute-done.12.peer_slot_ref, bf16[2048,128]{1,0:T(8,128)(2,1)S(1)} %get-tuple-element.23.delta_ref, bf16[2048,128]{1,0:T(8,128)(2,1)S(1)} %collective-permute-done.14.peer_delta_ref), custom_call_target="tpu_custom_call" | custom-call | tf_op jit(solution)/shard_map/pallas_call | solution.py:276
  79.2 3.6 %shard_map.109 = (bf16[256,128]{1,0:T(8,128)(2,1)S(1)}, bf16[256,128]{1,0:T(8,128)(2,1)S(1)}, bf16[256,128]{1,0:T(8,128)(2,1)S(1)}, bf16[256,128]{1,0:T(8,128)(2...) custom-call(s32[8,512]{1,0:T(8,128)S(1)} %reshape.99.slot_ref, ...), custom_call_target="tpu_custom_call" | custom-call | tf_op jit(solution)/shard_map/pallas_call | solution.py:276
  82.7 4.7 %collective-permute-start.21 = (bf16[256,128]{1,0:T(8,128)(2,1)S(1)}, bf16[256,128]{1,0:T(8,128)(2,1)S(1)}, u32[]{:S(2)}, u32[]{:S(2)}) collective-permute-start(bf16[256,128]{1,0:T(8,128)(2,1)S(1)} %get-tuple-element.31), channel_id=1, source_target_pairs={{0,28},{2,30},{4,24},{6,26},{8,20},{10,22},{12,16},{14,18},{16,12}... | collective-permute-start | bytes 196616 | tf_op jit(solution)/shard_map/ppermute | solution.py:302
  88.5 1.9 %collective-permute-start.18 = (bf16[256,128]{1,0:T(8,128)(2,1)S(1)}, bf16[256,128]{1,0:T(8,128)(2,1)S(1)}, u32[]{:S(2)}, u32[]{:S(2)}) collective-permute-start(bf16[256,128]{1,0:T(8,128)(2,1)S(1)} %get-tuple-element.28), channel_id=1, source_target_pairs={{0,16},{2,18},{4,20},{6,22},{8,24},{10,26},{12,28},{14,30},{16,0},... | collective-permute-start | bytes 196616 | tf_op jit(solution)/shard_map/ppermute | solution.py:302
  90.4 2.3 %collective-permute-start.17 = (bf16[256,128]{1,0:T(8,128)(2,1)S(1)}, bf16[256,128]{1,0:T(8,128)(2,1)S(1)}, u32[]{:S(2)}, u32[]{:S(2)}) collective-permute-start(bf16[256,128]{1,0:T(8,128)(2,1)S(1)} %get-tuple-element.27), channel_id=1, source_target_pairs={{0,12},{2,14},{4,8},{6,10},{8,4},{10,6},{12,0},{14,2},{16,28},{18,... | collective-permute-start | bytes 196616 | tf_op jit(solution)/shard_map/ppermute | solution.py:302
  92.7 6.5 %collective-permute-start.16 = (bf16[256,128]{1,0:T(8,128)(2,1)S(1)}, bf16[256,128]{1,0:T(8,128)(2,1)S(1)}, u32[]{:S(2)}, u32[]{:S(2)}) collective-permute-start(bf16[256,128]{1,0:T(8,128)(2,1)S(1)} %get-tuple-element.26), channel_id=1, source_target_pairs={{0,8},{2,10},{4,12},{6,14},{8,0},{10,2},{12,4},{14,6},{16,24},{18,... | collective-permute-start | bytes 196616 | tf_op jit(solution)/shard_map/ppermute | solution.py:302
  101.7 1.8 %collective-permute-done.15 = bf16[256,128]{1,0:T(8,128)(2,1)S(1)} collective-permute-done((bf16[256,128]{1,0:T(8,128)(2,1)S(1)}, bf16[256,128]{1,0:T(8,128)(2,1)S(1)}, u32[]{:S(2)}, u32[]{:S(2)}) %collective-permute-start.15) | collective-permute-done | bytes 65568 | tf_op jit(solution)/shard_map/ppermute | solution.py:302
  103.5 1.6 %collective-permute-start.22 = (bf16[256,128]{1,0:T(8,128)(2,1)S(1)}, bf16[256,128]{1,0:T(8,128)(2,1)S(1)}, u32[]{:S(2)}, u32[]{:S(2)}) collective-permute-start(bf16[256,128]{1,0:T(8,128)(2,1)S(1)} %add_convert_fusion), channel_id=1, source_target_pairs={{0,1},{1,0},{2,3},{3,2},{4,5},{5,4},{6,7},{7,6},{8,9},{9,8},{10,11... | collective-permute-start | bytes 196616 | tf_op jit(solution)/shard_map/ppermute | solution.py:369
  105.7 2.2 %collective-permute-done.22 = bf16[256,128]{1,0:T(8,128)(2,1)S(1)} collective-permute-done((bf16[256,128]{1,0:T(8,128)(2,1)S(1)}, bf16[256,128]{1,0:T(8,128)(2,1)S(1)}, u32[]{:S(2)}, u32[]{:S(2)}) %collective-permute-start.22) | collective-permute-done | bytes 65568 | tf_op jit(solution)/shard_map/ppermute | solution.py:369
  108.6 2.1 %reduce_sum.12 = bf16[512,128]{1,0:T(8,128)(2,1)} reduce(bf16[8,512,128]{2,1,0:T(8,128)(2,1)} %all-to-all-done.1, bf16[]{:T(256)} %constant.5.clone.1), dimensions={0}, to_apply=%region_1.2 | reduce | flops 458752 | bytes 1179650 | tf_op jit(solution)/shard_map/reduce_sum | solution.py:365
  (64 shorter events, 11.8 us)
Async XLA Ops:
  3.3 44.6 %collective-permute-start = (bf16[4096,128]{1,0:T(8,128)(2,1)}, bf16[4096,128]{1,0:T(8,128)(2,1)}, u32[]{:S(2)}, u32[]{:S(2)}) collective-permute-start(bf16[4096,128]{1,0:T(8,128)(2,1)} %shard_map.102.own_ref), channel_id=1, source_target_pairs={{0,2},{2,0},{4,6},{6,4},{8,10},{10,8},{12,14},{14,12},{16,18},{18,... | collective-permute-start | bytes 3145736 | tf_op jit(solution)/shard_map/ppermute | solution.py:302
  3.8 10.6 %collective-permute-start.2 = (bf16[512,128]{1,0:T(8,128)(2,1)S(1)}, bf16[512,128]{1,0:T(8,128)(2,1)S(1)}, u32[]{:S(2)}, u32[]{:S(2)}) collective-permute-start(bf16[512,128]{1,0:T(8,128)(2,1)S(1)} %copy-done.2), channel_id=1, source_target_pairs={{0,16},{2,18},{4,20},{6,22},{8,24},{10,26},{12,28},{14,30},{16,0},... | collective-permute-start | bytes 393224 | tf_op jit(solution)/shard_map/ppermute | solution.py:302
  14.4 18.9 %collective-permute-start.3 = (bf16[1024,128]{1,0:T(8,128)(2,1)S(1)}, bf16[1024,128]{1,0:T(8,128)(2,1)S(1)}, u32[]{:S(2)}, u32[]{:S(2)}) collective-permute-start(bf16[1024,128]{1,0:T(8,128)(2,1)S(1)} %constant_dynamic-update-slice_fusion.refs_0_), channel_id=1, source_target_pairs={{0,4},{2,6},{4,0},{6,2},{8,12},{10,14},{12,8},{14,10},{16,20},{18,... | collective-permute-start | bytes 786440 | tf_op jit(solution)/shard_map/ppermute | solution.py:302
  16.0 17.7 %collective-permute-start.4 = (bf16[1024,128]{1,0:T(8,128)(2,1)S(1)}, bf16[1024,128]{1,0:T(8,128)(2,1)S(1)}, u32[]{:S(2)}, u32[]{:S(2)}) collective-permute-start(bf16[1024,128]{1,0:T(8,128)(2,1)S(1)} %constant_dynamic-update-slice_fusion.refs_0_), channel_id=1, source_target_pairs={{0,8},{2,10},{4,12},{6,14},{8,0},{10,2},{12,4},{14,6},{16,24},{18,... | collective-permute-start | bytes 786440 | tf_op jit(solution)/shard_map/ppermute | solution.py:302
  16.7 17.1 %collective-permute-start.5 = (bf16[1024,128]{1,0:T(8,128)(2,1)S(1)}, bf16[1024,128]{1,0:T(8,128)(2,1)S(1)}, u32[]{:S(2)}, u32[]{:S(2)}) collective-permute-start(bf16[1024,128]{1,0:T(8,128)(2,1)S(1)} %constant_dynamic-update-slice_fusion.refs_0_), channel_id=1, source_target_pairs={{0,12},{2,14},{4,8},{6,10},{8,4},{10,6},{12,0},{14,2},{16,28},{18,... | collective-permute-start | bytes 786440 | tf_op jit(solution)/shard_map/ppermute | solution.py:302
  32.0 1.2 %collective-permute-start.1 = (s32[8,1,1024]{2,1,0:T(1,128)S(1)}, s32[8,1,1024]{2,1,0:T(1,128)S(1)}, u32[]{:S(2)}, u32[]{:S(2)}) collective-permute-start(s32[8,1,1024]{2,1,0:T(1,128)S(1)} %all_to_all.10.asked_ref), channel_id=1, source_target_pairs={{0,2},{2,0},{4,6},{6,4},{8,10},{10,8},{12,14},{14,12},{16,18},{18,... | collective-permute-start | bytes 98312 | tf_op jit(solution)/shard_map/ppermute | solution.py:302
  33.2 1.5 %collective-permute-start.6 = (bf16[1024,128]{1,0:T(8,128)(2,1)S(1)}, bf16[1024,128]{1,0:T(8,128)(2,1)S(1)}, u32[]{:S(2)}, u32[]{:S(2)}) collective-permute-start(bf16[1024,128]{1,0:T(8,128)(2,1)S(1)} %constant_dynamic-update-slice_fusion.refs_0_), channel_id=1, source_target_pairs={{0,2},{2,0},{4,6},{6,4},{8,10},{10,8},{12,14},{14,12},{16,18},{18,... | collective-permute-start | bytes 786440 | tf_op jit(solution)/shard_map/ppermute | solution.py:302
  33.4 1.7 %collective-permute-start.7 = (bf16[1024,128]{1,0:T(8,128)(2,1)S(1)}, bf16[1024,128]{1,0:T(8,128)(2,1)S(1)}, u32[]{:S(2)}, u32[]{:S(2)}) collective-permute-start(bf16[1024,128]{1,0:T(8,128)(2,1)S(1)} %collective-permute-done.3.refs_1_), channel_id=1, source_target_pairs={{0,2},{2,0},{4,6},{6,4},{8,10},{10,8},{12,14},{14,12},{16,18},{18,... | collective-permute-start | bytes 786440 | tf_op jit(solution)/shard_map/ppermute | solution.py:302
  33.7 1.8 %collective-permute-start.8 = (bf16[1024,128]{1,0:T(8,128)(2,1)S(1)}, bf16[1024,128]{1,0:T(8,128)(2,1)S(1)}, u32[]{:S(2)}, u32[]{:S(2)}) collective-permute-start(bf16[1024,128]{1,0:T(8,128)(2,1)S(1)} %collective-permute-done.4.refs_2_), channel_id=1, source_target_pairs={{0,2},{2,0},{4,6},{6,4},{8,10},{10,8},{12,14},{14,12},{16,18},{18,... | collective-permute-start | bytes 786440 | tf_op jit(solution)/shard_map/ppermute | solution.py:302
  33.9 2.0 %collective-permute-start.9 = (bf16[1024,128]{1,0:T(8,128)(2,1)S(1)}, bf16[1024,128]{1,0:T(8,128)(2,1)S(1)}, u32[]{:S(2)}, u32[]{:S(2)}) collective-permute-start(bf16[1024,128]{1,0:T(8,128)(2,1)S(1)} %collective-permute-done.5.refs_3_), channel_id=1, source_target_pairs={{0,2},{2,0},{4,6},{6,4},{8,10},{10,8},{12,14},{14,12},{16,18},{18,... | collective-permute-start | bytes 786440 | tf_op jit(solution)/shard_map/ppermute | solution.py:302
  40.8 23.3 %collective-permute-start.11 = (bf16[2048,128]{1,0:T(8,128)(2,1)S(1)}, bf16[2048,128]{1,0:T(8,128)(2,1)}, u32[]{:S(2)}, u32[]{:S(2)}) collective-permute-start(bf16[2048,128]{1,0:T(8,128)(2,1)S(1)} %shard_map.105.own_ref), channel_id=1, source_target_pairs={{0,1},{1,0},{2,3},{3,2},{4,5},{5,4},{6,7},{7,6},{8,9},{9,8},{10,11... | collective-permute-start | bytes 1572872 | tf_op jit(solution)/shard_map/ppermute | solution.py:340
  47.2 21.6 %collective-permute-start.10 = (bf16[2048,128]{1,0:T(8,128)(2,1)S(1)}, bf16[2048,128]{1,0:T(8,128)(2,1)}, u32[]{:S(2)}, u32[]{:S(2)}) collective-permute-start(bf16[2048,128]{1,0:T(8,128)(2,1)S(1)} %shard_map.104.own_ref), channel_id=1, source_target_pairs={{0,1},{1,0},{2,3},{3,2},{4,5},{5,4},{6,7},{7,6},{8,9},{9,8},{10,11... | collective-permute-start | bytes 1572872 | tf_op jit(solution)/shard_map/ppermute | solution.py:340
  59.8 48.9 %all-to-all-start.1 = ((bf16[8,512,128]{2,1,0:T(8,128)(2,1)}), bf16[8,512,128]{2,1,0:T(8,128)(2,1)}, u32[]{:S(2)}, u32[]{:S(2)}) async-start(bf16[8,512,128]{2,1,0:T(8,128)(2,1)} %bitcast.15), calls=%async_computation.1 | async-start | bytes 2097152 | tf_op jit(solution)/shard_map/all_to_all | solution.py:305
  68.7 6.9 %collective-permute-start.14 = (bf16[2048,128]{1,0:T(8,128)(2,1)S(1)}, bf16[2048,128]{1,0:T(8,128)(2,1)S(1)}, u32[]{:S(2)}, u32[]{:S(2)}) collective-permute-start(bf16[2048,128]{1,0:T(8,128)(2,1)S(1)} %get-tuple-element.23.delta_ref), channel_id=1, source_target_pairs={{0,2},{2,0},{4,6},{6,4},{8,10},{10,8},{12,14},{14,12},{16,18},{18,... | collective-permute-start | bytes 1572872 | tf_op jit(solution)/shard_map/ppermute | solution.py:302
  73.5 5.7 %collective-permute-start.13 = (bf16[2048,128]{1,0:T(8,128)(2,1)S(1)}, bf16[2048,128]{1,0:T(8,128)(2,1)S(1)}, u32[]{:S(2)}, u32[]{:S(2)}) collective-permute-start(bf16[2048,128]{1,0:T(8,128)(2,1)S(1)} %get-tuple-element.22.delta_ref), channel_id=1, source_target_pairs={{0,2},{2,0},{4,6},{6,4},{8,10},{10,8},{12,14},{14,12},{16,18},{18,... | collective-permute-start | bytes 1572872 | tf_op jit(solution)/shard_map/ppermute | solution.py:302
  74.1 1.5 %collective-permute-start.12 = (s32[8,512]{1,0:T(8,128)S(1)}, s32[8,512]{1,0:T(8,128)S(1)}, u32[]{:S(2)}, u32[]{:S(2)}) collective-permute-start(s32[8,512]{1,0:T(8,128)S(1)} %reshape.99.slot_ref), channel_id=1, source_target_pairs={{0,2},{2,0},{4,6},{6,4},{8,10},{10,8},{12,14},{14,12},{16,18},{18,... | collective-permute-start | bytes 49160 | tf_op jit(solution)/shard_map/ppermute | solution.py:302
  82.7 10.0 %collective-permute-start.21 = (bf16[256,128]{1,0:T(8,128)(2,1)S(1)}, bf16[256,128]{1,0:T(8,128)(2,1)S(1)}, u32[]{:S(2)}, u32[]{:S(2)}) collective-permute-start(bf16[256,128]{1,0:T(8,128)(2,1)S(1)} %get-tuple-element.31), channel_id=1, source_target_pairs={{0,28},{2,30},{4,24},{6,26},{8,20},{10,22},{12,16},{14,18},{16,12}... | collective-permute-start | bytes 196616 | tf_op jit(solution)/shard_map/ppermute | solution.py:302
  87.4 11.8 %collective-permute-start.20 = (bf16[256,128]{1,0:T(8,128)(2,1)S(1)}, bf16[256,128]{1,0:T(8,128)(2,1)S(1)}, u32[]{:S(2)}, u32[]{:S(2)}) collective-permute-start(bf16[256,128]{1,0:T(8,128)(2,1)S(1)} %get-tuple-element.30), channel_id=1, source_target_pairs={{0,24},{2,26},{4,28},{6,30},{8,16},{10,18},{12,20},{14,22},{16,8},... | collective-permute-start | bytes 196616 | tf_op jit(solution)/shard_map/ppermute | solution.py:302
  87.9 13.2 %collective-permute-start.19 = (bf16[256,128]{1,0:T(8,128)(2,1)S(1)}, bf16[256,128]{1,0:T(8,128)(2,1)S(1)}, u32[]{:S(2)}, u32[]{:S(2)}) collective-permute-start(bf16[256,128]{1,0:T(8,128)(2,1)S(1)} %get-tuple-element.29), channel_id=1, source_target_pairs={{0,20},{2,22},{4,16},{6,18},{8,28},{10,30},{12,24},{14,26},{16,4},... | collective-permute-start | bytes 196616 | tf_op jit(solution)/shard_map/ppermute | solution.py:302
  88.5 12.6 %collective-permute-start.18 = (bf16[256,128]{1,0:T(8,128)(2,1)S(1)}, bf16[256,128]{1,0:T(8,128)(2,1)S(1)}, u32[]{:S(2)}, u32[]{:S(2)}) collective-permute-start(bf16[256,128]{1,0:T(8,128)(2,1)S(1)} %get-tuple-element.28), channel_id=1, source_target_pairs={{0,16},{2,18},{4,20},{6,22},{8,24},{10,26},{12,28},{14,30},{16,0},... | collective-permute-start | bytes 196616 | tf_op jit(solution)/shard_map/ppermute | solution.py:302
  90.4 10.7 %collective-permute-start.17 = (bf16[256,128]{1,0:T(8,128)(2,1)S(1)}, bf16[256,128]{1,0:T(8,128)(2,1)S(1)}, u32[]{:S(2)}, u32[]{:S(2)}) collective-permute-start(bf16[256,128]{1,0:T(8,128)(2,1)S(1)} %get-tuple-element.27), channel_id=1, source_target_pairs={{0,12},{2,14},{4,8},{6,10},{8,4},{10,6},{12,0},{14,2},{16,28},{18,... | collective-permute-start | bytes 196616 | tf_op jit(solution)/shard_map/ppermute | solution.py:302
  92.7 9.0 %collective-permute-start.16 = (bf16[256,128]{1,0:T(8,128)(2,1)S(1)}, bf16[256,128]{1,0:T(8,128)(2,1)S(1)}, u32[]{:S(2)}, u32[]{:S(2)}) collective-permute-start(bf16[256,128]{1,0:T(8,128)(2,1)S(1)} %get-tuple-element.26), channel_id=1, source_target_pairs={{0,8},{2,10},{4,12},{6,14},{8,0},{10,2},{12,4},{14,6},{16,24},{18,... | collective-permute-start | bytes 196616 | tf_op jit(solution)/shard_map/ppermute | solution.py:302
  99.2 4.3 %collective-permute-start.15 = (bf16[256,128]{1,0:T(8,128)(2,1)S(1)}, bf16[256,128]{1,0:T(8,128)(2,1)S(1)}, u32[]{:S(2)}, u32[]{:S(2)}) collective-permute-start(bf16[256,128]{1,0:T(8,128)(2,1)S(1)} %get-tuple-element.25), channel_id=1, source_target_pairs={{0,4},{2,6},{4,0},{6,2},{8,12},{10,14},{12,8},{14,10},{16,20},{18,... | collective-permute-start | bytes 196616 | tf_op jit(solution)/shard_map/ppermute | solution.py:302
  103.5 4.3 %collective-permute-start.22 = (bf16[256,128]{1,0:T(8,128)(2,1)S(1)}, bf16[256,128]{1,0:T(8,128)(2,1)S(1)}, u32[]{:S(2)}, u32[]{:S(2)}) collective-permute-start(bf16[256,128]{1,0:T(8,128)(2,1)S(1)} %add_convert_fusion), channel_id=1, source_target_pairs={{0,1},{1,0},{2,3},{3,2},{4,5},{5,4},{6,7},{7,6},{8,9},{9,8},{10,11... | collective-permute-start | bytes 196616 | tf_op jit(solution)/shard_map/ppermute | solution.py:369
  (8 other events, 156.0 us)

commit v5 on v4

--- a/solution.py
+++ b/solution.py
@@ -9,7 +9,7 @@
 LEARN = 0.5
 EPSILON = 1e-06
 SPLIT = 4
-PARTS = (2, 2)
+PARTS = (4, 2, 4)
 NEAR_BYTES = 1 << 21
 VMEM = pl.BlockSpec(memory_space=pltpu.VMEM)
 
@@ -181,6 +181,7 @@
     diagonal = lax.broadcasted_iota(jnp.int32, (width, width), 0) == lax.broadcasted_iota(
         jnp.int32, (width, width), 1
     )
+    ones = jnp.ones((3 * width, width), jnp.bfloat16)
     for j in range(rows // width):
         i, within = divmod(j * width, chunk)
         if within == 0:
@@ -189,7 +190,12 @@
         line = base // width + j
         grads = own_ref[at, :].astype(jnp.float32) + other_ref[at, :].astype(jnp.float32)
         scaled = jnp.where(diagonal, accum_ref[line : line + 1, :] * width, 0.0)
-        fresh_accum = jnp.sum(grads * grads + scaled, axis=1, keepdims=True) * (1.0 / width)
+        rest, terms = grads * grads + scaled, []
+        for _ in range(3):
+            terms.append(rest.astype(jnp.bfloat16))
+            rest = rest - terms[-1].astype(jnp.float32)
+        sums = jnp.dot(jnp.concatenate(terms, axis=1), ones, preferred_element_type=jnp.float32)
+        fresh_accum = sums * (1.0 / width)
         old_rows = old_ref[at, :]
         fresh_rows = old_rows - LEARN * grads / jnp.sqrt(fresh_accum + EPSILON)
         fresh_ref[at, :] = fresh_rows

time: 111 us -> 120 us (1.081)
  waiting for transfers between devices: 16.7 us -> 22.8 us
  Pallas kernels: 40.8 us -> 46.7 us
  starting transfers between devices: 34.9 us -> 30.6 us
    ppermute x20 -> x21, starting transfers between devices: 26.9 us -> 22 us  [swap(): lax.ppermute(values, 'table', [(i, i ^ distance) for i in range(table_cou...]
    ppermute x2 -> x3, waiting for transfers between devices: 0.01 us -> 4.45 us  [on_device(): other = lax.ppermute(mine, 'dp', [(i, i ^ 1) for i in range(dp_count)])]
    pallas_call x2 -> x3, Pallas kernels: 9.32 us -> 11.9 us  [update(): pl.pallas_call(functools.partial(update_kernel, base=base, chunk=chunk),...]
    pallas_call x2 -> x3, Pallas kernels: 7.11 us -> 9.35 us  [parity_changes(): pl.pallas_call(functools.partial(parity_kernel, base=base, holder_rows=ho...]
    ppermute x2 -> x3, starting transfers between devices: 2.16 us -> 3.65 us  [on_device(): other = lax.ppermute(mine, 'dp', [(i, i ^ 1) for i in range(dp_count)])]
    pallas_call x2 -> x3, Pallas kernels: 9.79 us -> 11 us  [row_gradients(): pl.pallas_call(functools.partial(segment_kernel, base=base), in_specs=[VM...]
    ppermute x20 -> x21, waiting for transfers between devices: 14.5 us -> 15.2 us  [swap(): lax.ppermute(values, 'table', [(i, i ^ distance) for i in range(table_cou...]
  transfers between devices with their start and end apart: 24 -> 26, of which waited for: 11 -> 12; matrix products, arithmetic and copies ran while one was open for 2% -> 1% of each run, Pallas kernels for 34% -> 37%
where the time goes in v5:
time: 120 us; the launch traced here: 119 us
  Pallas kernels  46.7 us (39%)
  starting transfers between devices  30.6 us (26%)
  waiting for transfers between devices  22.8 us (19%)
  blocking collectives  13.8 us (12%)
  other arithmetic  3.68 us (3%)
    ppermute x21, starting transfers between devices, swap(): lax.ppermute(values, 'table', [(i, i ^ distance) for i in range(table_cou...  22 us
    ppermute x21, waiting for transfers between devices, swap(): lax.ppermute(values, 'table', [(i, i ^ distance) for i in range(table_cou...  15.2 us
    all_to_all x1, blocking collectives, exchange(): lax.all_to_all(values, 'table', split_axis=0, concat_axis=0, axis_index_g...  13.8 us
    pallas_call x3, Pallas kernels, update(): pl.pallas_call(functools.partial(update_kernel, base=base, chunk=chunk),...  11.9 us
    pallas_call x1, Pallas kernels, chip_rows(): pl.pallas_call(functools.partial(gather_kernel, together=2), in_specs=[VM...  11.9 us
    pallas_call x3, Pallas kernels, row_gradients(): pl.pallas_call(functools.partial(segment_kernel, base=base), in_specs=[VM...  11 us
    pallas_call x3, Pallas kernels, parity_changes(): pl.pallas_call(functools.partial(parity_kernel, base=base, holder_rows=ho...  9.35 us
    ppermute x3, waiting for transfers between devices, on_device(): other = lax.ppermute(mine, 'dp', [(i, i ^ 1) for i in range(dp_count)])  4.45 us
  transfers between devices with their start and end apart: 26, of which 12 were waited for; matrix products, arithmetic and copies ran while one was open for 1% of the time, Pallas kernels for 37%

profile of v5, /device:TPU:0, one launch (start us, length us, event | category | flops | bytes accessed | tf_op | source)
XLA Modules:
  0.0 119.4 jit_solution(14563474224233519752)
XLA Ops:
  0.7 2.6 %shard_map.102.own_ref = bf16[4096,128]{1,0:T(8,128)(2,1)} custom-call(f32[4096,128]{1,0:T(8,128)} %table_ref.5), custom_call_target="tpu_custom_call" | custom-call | tf_op jit(solution)/shard_map/pallas_call | solution.py:118
  3.8 3.7 %collective-permute-start.2 = (bf16[512,128]{1,0:T(8,128)(2,1)S(1)}, bf16[512,128]{1,0:T(8,128)(2,1)S(1)}, u32[]{:S(2)}, u32[]{:S(2)}) collective-permute-start(bf16[512,128]{1,0:T(8,128)(2,1)S(1)} %copy-done.12), channel_id=1, source_target_pairs={{0,16},{2,18},{4,20},{6,22},{8,24},{10,26},{12,28},{14,30},{16,0},... | collective-permute-start | bytes 393224 | tf_op jit(solution)/shard_map/ppermute | solution.py:308
  7.5 6.9 %collective-permute-done.2 = bf16[512,128]{1,0:T(8,128)(2,1)S(1)} collective-permute-done((bf16[512,128]{1,0:T(8,128)(2,1)S(1)}, bf16[512,128]{1,0:T(8,128)(2,1)S(1)}, u32[]{:S(2)}, u32[]{:S(2)}) %collective-permute-start.2) | collective-permute-done | bytes 131104 | tf_op jit(solution)/shard_map/ppermute | solution.py:308
  14.4 1.6 %collective-permute-start.3 = (bf16[1024,128]{1,0:T(8,128)(2,1)S(1)}, bf16[1024,128]{1,0:T(8,128)(2,1)S(1)}, u32[]{:S(2)}, u32[]{:S(2)}) collective-permute-start(bf16[1024,128]{1,0:T(8,128)(2,1)S(1)} %constant_dynamic-update-slice_fusion.refs_0_), channel_id=1, source_target_pairs={{0,4},{2,6},{4,0},{6,2},{8,12},{10,14},{12,8},{14,10},{16,20},{18,... | collective-permute-start | bytes 786440 | tf_op jit(solution)/shard_map/ppermute | solution.py:308
  18.2 13.8 %all_to_all.10.asked_ref = s32[8,1,1024]{2,1,0:T(1,128)S(1)} all-to-all(s32[8,1,1024]{2,1,0:T(1,128)S(1)} %reduce_max.12), channel_id=1, replica_groups={{0,4,8,12,16,20,24,28},{2,6,10,14,18,22,26,30},{1,5,9,13,17,21,25,29},{..., dimensions={0} | all-to-all | bytes 65536 | tf_op jit(solution)/shard_map/all_to_all | solution.py:311
  35.9 5.7 %shard_map.105.own_ref = bf16[2048,128]{1,0:T(8,128)(2,1)} custom-call(s32[8,1,1024]{2,1,0:T(1,128)S(1)} %all_to_all.10.asked_ref, s32[8,1,1024]{2,1,0:T(1,128)S(1)} %collective-permute-done.1.peer_asked_ref, bf16[1024,128]{1,0:T(8,128)(2,1)S(1)} %constant_dynamic-update-slice_fusion.refs_0_, bf16[1024,128]{1,0:T(8,128)(2,1)S(1)} %collective-permute-done.3.refs_1_, ...), custom_call_target="tpu_custom_call" | custom-call | tf_op jit(solution)/shard_map/pallas_call | solution.py:95
  43.8 11.9 %shard_map.103 = bf16[4096,128]{1,0:T(8,128)(2,1)} custom-call(s32[8,1,1024]{2,1,0:T(1,128)S(1)} %all_to_all.10.asked_ref, bf16[4096,128]{1,0:T(8,128)(2,1)} %shard_map.102.own_ref, bf16[4096,128]{1,0:T(8,128)(2,1)} %collective-permute-done.peer_ref), custom_call_target="tpu_custom_call" | custom-call | tf_op jit(solution)/shard_map/pallas_call | solution.py:160
  55.7 4.4 %all-to-all-start.1 = ((bf16[8,512,128]{2,1,0:T(8,128)(2,1)}), bf16[8,512,128]{2,1,0:T(8,128)(2,1)}, u32[]{:S(2)}, u32[]{:S(2)}) async-start(bf16[8,512,128]{2,1,0:T(8,128)(2,1)} %bitcast.16), calls=%async_computation.1 | async-start | bytes 2097152 | tf_op jit(solution)/shard_map/all_to_all | solution.py:311
  60.2 2.7 %shard_map.106.own_ref = bf16[1024,128]{1,0:T(8,128)(2,1)S(1)} custom-call(s32[8,1,1024]{2,1,0:T(1,128)S(1)} %all_to_all.10.asked_ref, s32[8,1,1024]{2,1,0:T(1,128)S(1)} %collective-permute-done.1.peer_asked_ref, bf16[1024,128]{1,0:T(8,128)(2,1)S(1)} %constant_dynamic-update-slice_fusion.refs_0_, bf16[1024,128]{1,0:T(8,128)(2,1)S(1)} %collective-permute-done.3.refs_1_, ...), custom_call_target="tpu_custom_call" | custom-call | tf_op jit(solution)/shard_map/pallas_call | solution.py:95
  63.4 2.6 %shard_map.104.own_ref = bf16[1024,128]{1,0:T(8,128)(2,1)S(1)} custom-call(s32[8,1,1024]{2,1,0:T(1,128)S(1)} %all_to_all.10.asked_ref, s32[8,1,1024]{2,1,0:T(1,128)S(1)} %collective-permute-done.1.peer_asked_ref, bf16[1024,128]{1,0:T(8,128)(2,1)S(1)} %constant_dynamic-update-slice_fusion.refs_0_, bf16[1024,128]{1,0:T(8,128)(2,1)S(1)} %collective-permute-done.3.refs_1_, ...), custom_call_target="tpu_custom_call" | custom-call | tf_op jit(solution)/shard_map/pallas_call | solution.py:95
  67.6 4.4 %collective-permute-done.12.other_ref = bf16[1024,128]{1,0:T(8,128)(2,1)S(1)} collective-permute-done((bf16[1024,128]{1,0:T(8,128)(2,1)S(1)}, bf16[1024,128]{1,0:T(8,128)(2,1)S(1)}, u32[]{:S(2)}, u32[]{:S(2)}) %collective-permute-start.12) | collective-permute-done | bytes 262176 | tf_op jit(solution)/shard_map/ppermute | solution.py:346
  72.1 3.2 %shard_map.107 = (f32[4096,128]{1,0:T(8,128)}, f32[8,128]{1,0:T(8,128)}, bf16[1024,128]{1,0:T(8,128)(2,1)S(1)}) custom-call(bf16[1024,128]{1,0:T(8,128)(2,1)S(1)} %shard_map.106.own_ref, bf16[1024,128]{1,0:T(8,128)(2,1)S(1)} %collective-permute-done.12.other_ref, f32[4096,128]{1,0:T(8,128)} %table_ref.5, f32[32,128]{1,0:T(8,128)S(1)} %bitcast.13), custom_call_target="tpu_custom_call" | custom-call | tf_op jit(solution)/shard_map/pallas_call | solution.py:216
  75.3 5.5 %shard_map.108 = (f32[4096,128]{1,0:T(8,128)}, f32[16,128]{1,0:T(8,128)}, bf16[2048,128]{1,0:T(8,128)(2,1)S(1)}) custom-call(bf16[2048,128]{1,0:T(8,128)(2,1)} %shard_map.105.own_ref, bf16[2048,128]{1,0:T(8,128)(2,1)} %collective-permute-done.11.other_ref, f32[4096,128]{1,0:T(8,128)} %table_ref.5, ...), custom_call_target="tpu_custom_call", output_to_operand_aliasing={{0}: (4, {})} | custom-call | tf_op jit(solution)/shard_map/pallas_call | solution.py:216
  81.4 3.2 %shard_map.109 = (f32[4096,128]{1,0:T(8,128)}, f32[8,128]{1,0:T(8,128)}, bf16[1024,128]{1,0:T(8,128)(2,1)S(1)}) custom-call(bf16[1024,128]{1,0:T(8,128)(2,1)S(1)} %shard_map.104.own_ref, bf16[1024,128]{1,0:T(8,128)(2,1)S(1)} %collective-permute-done.10.other_ref, f32[4096,128]{1,0:T(8,128)} %table_ref.5, ...), custom_call_target="tpu_custom_call", output_to_operand_aliasing={{0}: (4, {})} | custom-call | tf_op jit(solution)/shard_map/pallas_call | solution.py:216
  86.3 2.4 %shard_map.110.refs_0_ = f32[512,512]{1,0:T(8,128)} custom-call(s32[8,512]{1,0:T(8,128)S(1)} %reshape.99.slot_ref, s32[8,512]{1,0:T(8,128)S(1)} %collective-permute-done.13.peer_slot_ref, bf16[1024,128]{1,0:T(8,128)(2,1)S(1)} %get-tuple-element.29.delta_ref, bf16[1024,128]{1,0:T(8,128)(2,1)S(1)} %collective-permute-done.16.peer_delta_ref), custom_call_target="tpu_custom_call" | custom-call | tf_op jit(solution)/shard_map/pallas_call | solution.py:282
  88.7 4.5 %shard_map.111.refs_0_ = f32[512,512]{1,0:T(8,128)} custom-call(s32[8,512]{1,0:T(8,128)S(1)} %reshape.99.slot_ref, s32[8,512]{1,0:T(8,128)S(1)} %collective-permute-done.13.peer_slot_ref, bf16[2048,128]{1,0:T(8,128)(2,1)S(1)} %get-tuple-element.28.delta_ref, bf16[2048,128]{1,0:T(8,128)(2,1)S(1)} %collective-permute-done.15.peer_delta_ref, ...), custom_call_target="tpu_custom_call" | custom-call | tf_op jit(solution)/shard_map/pallas_call | solution.py:282
  93.2 2.4 %shard_map.112 = (bf16[256,128]{1,0:T(8,128)(2,1)S(1)}, bf16[256,128]{1,0:T(8,128)(2,1)S(1)}, bf16[256,128]{1,0:T(8,128)(2,1)S(1)}, bf16[256,128]{1,0:T(8,128)(2...) custom-call(s32[8,512]{1,0:T(8,128)S(1)} %reshape.99.slot_ref, ...), custom_call_target="tpu_custom_call" | custom-call | tf_op jit(solution)/shard_map/pallas_call | solution.py:282
  95.6 4.5 %collective-permute-start.23 = (bf16[256,128]{1,0:T(8,128)(2,1)S(1)}, bf16[256,128]{1,0:T(8,128)(2,1)S(1)}, u32[]{:S(2)}, u32[]{:S(2)}) collective-permute-start(bf16[256,128]{1,0:T(8,128)(2,1)S(1)} %get-tuple-element.37), channel_id=1, source_target_pairs={{0,28},{2,30},{4,24},{6,26},{8,20},{10,22},{12,16},{14,18},{16,12}... | collective-permute-start | bytes 196616 | tf_op jit(solution)/shard_map/ppermute | solution.py:308
  101.3 2.1 %collective-permute-start.20 = (bf16[256,128]{1,0:T(8,128)(2,1)S(1)}, bf16[256,128]{1,0:T(8,128)(2,1)S(1)}, u32[]{:S(2)}, u32[]{:S(2)}) collective-permute-start(bf16[256,128]{1,0:T(8,128)(2,1)S(1)} %get-tuple-element.34), channel_id=1, source_target_pairs={{0,16},{2,18},{4,20},{6,22},{8,24},{10,26},{12,28},{14,30},{16,0},... | collective-permute-start | bytes 196616 | tf_op jit(solution)/shard_map/ppermute | solution.py:308
  103.4 2.1 %collective-permute-start.19 = (bf16[256,128]{1,0:T(8,128)(2,1)S(1)}, bf16[256,128]{1,0:T(8,128)(2,1)S(1)}, u32[]{:S(2)}, u32[]{:S(2)}) collective-permute-start(bf16[256,128]{1,0:T(8,128)(2,1)S(1)} %get-tuple-element.33), channel_id=1, source_target_pairs={{0,12},{2,14},{4,8},{6,10},{8,4},{10,6},{12,0},{14,2},{16,28},{18,... | collective-permute-start | bytes 196616 | tf_op jit(solution)/shard_map/ppermute | solution.py:308
  107.7 2.6 %collective-permute-done.21 = bf16[256,128]{1,0:T(8,128)(2,1)S(1)} collective-permute-done((bf16[256,128]{1,0:T(8,128)(2,1)S(1)}, bf16[256,128]{1,0:T(8,128)(2,1)S(1)}, u32[]{:S(2)}, u32[]{:S(2)}) %collective-permute-start.21) | collective-permute-done | bytes 65568 | tf_op jit(solution)/shard_map/ppermute | solution.py:308
  110.3 1.7 %collective-permute-done.20 = bf16[256,128]{1,0:T(8,128)(2,1)S(1)} collective-permute-done((bf16[256,128]{1,0:T(8,128)(2,1)S(1)}, bf16[256,128]{1,0:T(8,128)(2,1)S(1)}, u32[]{:S(2)}, u32[]{:S(2)}) %collective-permute-start.20) | collective-permute-done | bytes 65568 | tf_op jit(solution)/shard_map/ppermute | solution.py:308
  113.4 3.1 %collective-permute-done.24 = bf16[256,128]{1,0:T(8,128)(2,1)S(1)} collective-permute-done((bf16[256,128]{1,0:T(8,128)(2,1)S(1)}, bf16[256,128]{1,0:T(8,128)(2,1)S(1)}, u32[]{:S(2)}, u32[]{:S(2)}) %collective-permute-start.24) | collective-permute-done | bytes 65568 | tf_op jit(solution)/shard_map/ppermute | solution.py:375
  117.3 2.1 %reduce_sum.12 = bf16[512,128]{1,0:T(8,128)(2,1)} reduce(bf16[8,512,128]{2,1,0:T(8,128)(2,1)} %all-to-all-done.1, bf16[]{:T(256)} %constant.5.clone.1), dimensions={0}, to_apply=%region_1.2 | reduce | flops 458752 | bytes 1179650 | tf_op jit(solution)/shard_map/reduce_sum | solution.py:371
  (93 shorter events, 18.8 us)
Async XLA Ops:
  3.3 40.5 %collective-permute-start = (bf16[4096,128]{1,0:T(8,128)(2,1)}, bf16[4096,128]{1,0:T(8,128)(2,1)}, u32[]{:S(2)}, u32[]{:S(2)}) collective-permute-start(bf16[4096,128]{1,0:T(8,128)(2,1)} %shard_map.102.own_ref), channel_id=1, source_target_pairs={{0,2},{2,0},{4,6},{6,4},{8,10},{10,8},{12,14},{14,12},{16,18},{18,... | collective-permute-start | bytes 3145736 | tf_op jit(solution)/shard_map/ppermute | solution.py:308
  3.8 10.6 %collective-permute-start.2 = (bf16[512,128]{1,0:T(8,128)(2,1)S(1)}, bf16[512,128]{1,0:T(8,128)(2,1)S(1)}, u32[]{:S(2)}, u32[]{:S(2)}) collective-permute-start(bf16[512,128]{1,0:T(8,128)(2,1)S(1)} %copy-done.12), channel_id=1, source_target_pairs={{0,16},{2,18},{4,20},{6,22},{8,24},{10,26},{12,28},{14,30},{16,0},... | collective-permute-start | bytes 393224 | tf_op jit(solution)/shard_map/ppermute | solution.py:308
  14.4 18.9 %collective-permute-start.3 = (bf16[1024,128]{1,0:T(8,128)(2,1)S(1)}, bf16[1024,128]{1,0:T(8,128)(2,1)S(1)}, u32[]{:S(2)}, u32[]{:S(2)}) collective-permute-start(bf16[1024,128]{1,0:T(8,128)(2,1)S(1)} %constant_dynamic-update-slice_fusion.refs_0_), channel_id=1, source_target_pairs={{0,4},{2,6},{4,0},{6,2},{8,12},{10,14},{12,8},{14,10},{16,20},{18,... | collective-permute-start | bytes 786440 | tf_op jit(solution)/shard_map/ppermute | solution.py:308
  16.0 17.7 %collective-permute-start.4 = (bf16[1024,128]{1,0:T(8,128)(2,1)S(1)}, bf16[1024,128]{1,0:T(8,128)(2,1)S(1)}, u32[]{:S(2)}, u32[]{:S(2)}) collective-permute-start(bf16[1024,128]{1,0:T(8,128)(2,1)S(1)} %constant_dynamic-update-slice_fusion.refs_0_), channel_id=1, source_target_pairs={{0,8},{2,10},{4,12},{6,14},{8,0},{10,2},{12,4},{14,6},{16,24},{18,... | collective-permute-start | bytes 786440 | tf_op jit(solution)/shard_map/ppermute | solution.py:308
  16.7 17.1 %collective-permute-start.5 = (bf16[1024,128]{1,0:T(8,128)(2,1)S(1)}, bf16[1024,128]{1,0:T(8,128)(2,1)S(1)}, u32[]{:S(2)}, u32[]{:S(2)}) collective-permute-start(bf16[1024,128]{1,0:T(8,128)(2,1)S(1)} %constant_dynamic-update-slice_fusion.refs_0_), channel_id=1, source_target_pairs={{0,12},{2,14},{4,8},{6,10},{8,4},{10,6},{12,0},{14,2},{16,28},{18,... | collective-permute-start | bytes 786440 | tf_op jit(solution)/shard_map/ppermute | solution.py:308
  33.2 1.5 %collective-permute-start.6 = (bf16[1024,128]{1,0:T(8,128)(2,1)S(1)}, bf16[1024,128]{1,0:T(8,128)(2,1)S(1)}, u32[]{:S(2)}, u32[]{:S(2)}) collective-permute-start(bf16[1024,128]{1,0:T(8,128)(2,1)S(1)} %constant_dynamic-update-slice_fusion.refs_0_), channel_id=1, source_target_pairs={{0,2},{2,0},{4,6},{6,4},{8,10},{10,8},{12,14},{14,12},{16,18},{18,... | collective-permute-start | bytes 786440 | tf_op jit(solution)/shard_map/ppermute | solution.py:308
  33.4 1.7 %collective-permute-start.7 = (bf16[1024,128]{1,0:T(8,128)(2,1)S(1)}, bf16[1024,128]{1,0:T(8,128)(2,1)S(1)}, u32[]{:S(2)}, u32[]{:S(2)}) collective-permute-start(bf16[1024,128]{1,0:T(8,128)(2,1)S(1)} %collective-permute-done.3.refs_1_), channel_id=1, source_target_pairs={{0,2},{2,0},{4,6},{6,4},{8,10},{10,8},{12,14},{14,12},{16,18},{18,... | collective-permute-start | bytes 786440 | tf_op jit(solution)/shard_map/ppermute | solution.py:308
  33.7 1.8 %collective-permute-start.8 = (bf16[1024,128]{1,0:T(8,128)(2,1)S(1)}, bf16[1024,128]{1,0:T(8,128)(2,1)S(1)}, u32[]{:S(2)}, u32[]{:S(2)}) collective-permute-start(bf16[1024,128]{1,0:T(8,128)(2,1)S(1)} %collective-permute-done.4.refs_2_), channel_id=1, source_target_pairs={{0,2},{2,0},{4,6},{6,4},{8,10},{10,8},{12,14},{14,12},{16,18},{18,... | collective-permute-start | bytes 786440 | tf_op jit(solution)/shard_map/ppermute | solution.py:308
  33.9 2.0 %collective-permute-start.9 = (bf16[1024,128]{1,0:T(8,128)(2,1)S(1)}, bf16[1024,128]{1,0:T(8,128)(2,1)S(1)}, u32[]{:S(2)}, u32[]{:S(2)}) collective-permute-start(bf16[1024,128]{1,0:T(8,128)(2,1)S(1)} %collective-permute-done.5.refs_3_), channel_id=1, source_target_pairs={{0,2},{2,0},{4,6},{6,4},{8,10},{10,8},{12,14},{14,12},{16,18},{18,... | collective-permute-start | bytes 786440 | tf_op jit(solution)/shard_map/ppermute | solution.py:308
  42.3 33.0 %collective-permute-start.11 = (bf16[2048,128]{1,0:T(8,128)(2,1)}, bf16[2048,128]{1,0:T(8,128)(2,1)}, u32[]{:S(2)}, u32[]{:S(2)}) collective-permute-start(bf16[2048,128]{1,0:T(8,128)(2,1)} %shard_map.105.own_ref), channel_id=1, source_target_pairs={{0,1},{1,0},{2,3},{3,2},{4,5},{5,4},{6,7},{7,6},{8,9},{9,8},{10,11... | collective-permute-start | bytes 1572872 | tf_op jit(solution)/shard_map/ppermute | solution.py:346
  55.7 61.6 %all-to-all-start.1 = ((bf16[8,512,128]{2,1,0:T(8,128)(2,1)}), bf16[8,512,128]{2,1,0:T(8,128)(2,1)}, u32[]{:S(2)}, u32[]{:S(2)}) async-start(bf16[8,512,128]{2,1,0:T(8,128)(2,1)} %bitcast.16), calls=%async_computation.1 | async-start | bytes 2097152 | tf_op jit(solution)/shard_map/all_to_all | solution.py:311
  62.8 9.2 %collective-permute-start.12 = (bf16[1024,128]{1,0:T(8,128)(2,1)S(1)}, bf16[1024,128]{1,0:T(8,128)(2,1)S(1)}, u32[]{:S(2)}, u32[]{:S(2)}) collective-permute-start(bf16[1024,128]{1,0:T(8,128)(2,1)S(1)} %shard_map.106.own_ref), channel_id=1, source_target_pairs={{0,1},{1,0},{2,3},{3,2},{4,5},{5,4},{6,7},{7,6},{8,9},{9,8},{10,11... | collective-permute-start | bytes 786440 | tf_op jit(solution)/shard_map/ppermute | solution.py:346
  66.1 15.3 %collective-permute-start.10 = (bf16[1024,128]{1,0:T(8,128)(2,1)S(1)}, bf16[1024,128]{1,0:T(8,128)(2,1)S(1)}, u32[]{:S(2)}, u32[]{:S(2)}) collective-permute-start(bf16[1024,128]{1,0:T(8,128)(2,1)S(1)} %shard_map.104.own_ref), channel_id=1, source_target_pairs={{0,1},{1,0},{2,3},{3,2},{4,5},{5,4},{6,7},{7,6},{8,9},{9,8},{10,11... | collective-permute-start | bytes 786440 | tf_op jit(solution)/shard_map/ppermute | solution.py:346
  80.8 7.9 %collective-permute-start.15 = (bf16[2048,128]{1,0:T(8,128)(2,1)S(1)}, bf16[2048,128]{1,0:T(8,128)(2,1)S(1)}, u32[]{:S(2)}, u32[]{:S(2)}) collective-permute-start(bf16[2048,128]{1,0:T(8,128)(2,1)S(1)} %get-tuple-element.28.delta_ref), channel_id=1, source_target_pairs={{0,2},{2,0},{4,6},{6,4},{8,10},{10,8},{12,14},{14,12},{16,18},{18,... | collective-permute-start | bytes 1572872 | tf_op jit(solution)/shard_map/ppermute | solution.py:308
  80.9 5.4 %collective-permute-start.16 = (bf16[1024,128]{1,0:T(8,128)(2,1)S(1)}, bf16[1024,128]{1,0:T(8,128)(2,1)S(1)}, u32[]{:S(2)}, u32[]{:S(2)}) collective-permute-start(bf16[1024,128]{1,0:T(8,128)(2,1)S(1)} %get-tuple-element.29.delta_ref), channel_id=1, source_target_pairs={{0,2},{2,0},{4,6},{6,4},{8,10},{10,8},{12,14},{14,12},{16,18},{18,... | collective-permute-start | bytes 786440 | tf_op jit(solution)/shard_map/ppermute | solution.py:308
  84.6 8.6 %collective-permute-start.14 = (bf16[1024,128]{1,0:T(8,128)(2,1)S(1)}, bf16[1024,128]{1,0:T(8,128)(2,1)S(1)}, u32[]{:S(2)}, u32[]{:S(2)}) collective-permute-start(bf16[1024,128]{1,0:T(8,128)(2,1)S(1)} %get-tuple-element.27.delta_ref), channel_id=1, source_target_pairs={{0,2},{2,0},{4,6},{6,4},{8,10},{10,8},{12,14},{14,12},{16,18},{18,... | collective-permute-start | bytes 786440 | tf_op jit(solution)/shard_map/ppermute | solution.py:308
  95.6 9.8 %collective-permute-start.23 = (bf16[256,128]{1,0:T(8,128)(2,1)S(1)}, bf16[256,128]{1,0:T(8,128)(2,1)S(1)}, u32[]{:S(2)}, u32[]{:S(2)}) collective-permute-start(bf16[256,128]{1,0:T(8,128)(2,1)S(1)} %get-tuple-element.37), channel_id=1, source_target_pairs={{0,28},{2,30},{4,24},{6,26},{8,20},{10,22},{12,16},{14,18},{16,12}... | collective-permute-start | bytes 196616 | tf_op jit(solution)/shard_map/ppermute | solution.py:308
  100.1 6.9 %collective-permute-start.22 = (bf16[256,128]{1,0:T(8,128)(2,1)S(1)}, bf16[256,128]{1,0:T(8,128)(2,1)S(1)}, u32[]{:S(2)}, u32[]{:S(2)}) collective-permute-start(bf16[256,128]{1,0:T(8,128)(2,1)S(1)} %get-tuple-element.36), channel_id=1, source_target_pairs={{0,24},{2,26},{4,28},{6,30},{8,16},{10,18},{12,20},{14,22},{16,8},... | collective-permute-start | bytes 196616 | tf_op jit(solution)/shard_map/ppermute | solution.py:308
  100.7 9.6 %collective-permute-start.21 = (bf16[256,128]{1,0:T(8,128)(2,1)S(1)}, bf16[256,128]{1,0:T(8,128)(2,1)S(1)}, u32[]{:S(2)}, u32[]{:S(2)}) collective-permute-start(bf16[256,128]{1,0:T(8,128)(2,1)S(1)} %get-tuple-element.35), channel_id=1, source_target_pairs={{0,20},{2,22},{4,16},{6,18},{8,28},{10,30},{12,24},{14,26},{16,4},... | collective-permute-start | bytes 196616 | tf_op jit(solution)/shard_map/ppermute | solution.py:308
  101.3 10.7 %collective-permute-start.20 = (bf16[256,128]{1,0:T(8,128)(2,1)S(1)}, bf16[256,128]{1,0:T(8,128)(2,1)S(1)}, u32[]{:S(2)}, u32[]{:S(2)}) collective-permute-start(bf16[256,128]{1,0:T(8,128)(2,1)S(1)} %get-tuple-element.34), channel_id=1, source_target_pairs={{0,16},{2,18},{4,20},{6,22},{8,24},{10,26},{12,28},{14,30},{16,0},... | collective-permute-start | bytes 196616 | tf_op jit(solution)/shard_map/ppermute | solution.py:308
  103.4 8.6 %collective-permute-start.19 = (bf16[256,128]{1,0:T(8,128)(2,1)S(1)}, bf16[256,128]{1,0:T(8,128)(2,1)S(1)}, u32[]{:S(2)}, u32[]{:S(2)}) collective-permute-start(bf16[256,128]{1,0:T(8,128)(2,1)S(1)} %get-tuple-element.33), channel_id=1, source_target_pairs={{0,12},{2,14},{4,8},{6,10},{8,4},{10,6},{12,0},{14,2},{16,28},{18,... | collective-permute-start | bytes 196616 | tf_op jit(solution)/shard_map/ppermute | solution.py:308
  105.4 6.7 %collective-permute-start.18 = (bf16[256,128]{1,0:T(8,128)(2,1)S(1)}, bf16[256,128]{1,0:T(8,128)(2,1)S(1)}, u32[]{:S(2)}, u32[]{:S(2)}) collective-permute-start(bf16[256,128]{1,0:T(8,128)(2,1)S(1)} %get-tuple-element.32), channel_id=1, source_target_pairs={{0,8},{2,10},{4,12},{6,14},{8,0},{10,2},{12,4},{14,6},{16,24},{18,... | collective-permute-start | bytes 196616 | tf_op jit(solution)/shard_map/ppermute | solution.py:308
  107.0 5.1 %collective-permute-start.17 = (bf16[256,128]{1,0:T(8,128)(2,1)S(1)}, bf16[256,128]{1,0:T(8,128)(2,1)S(1)}, u32[]{:S(2)}, u32[]{:S(2)}) collective-permute-start(bf16[256,128]{1,0:T(8,128)(2,1)S(1)} %get-tuple-element.31), channel_id=1, source_target_pairs={{0,4},{2,6},{4,0},{6,2},{8,12},{10,14},{12,8},{14,10},{16,20},{18,... | collective-permute-start | bytes 196616 | tf_op jit(solution)/shard_map/ppermute | solution.py:308
  112.2 4.3 %collective-permute-start.24 = (bf16[256,128]{1,0:T(8,128)(2,1)S(1)}, bf16[256,128]{1,0:T(8,128)(2,1)S(1)}, u32[]{:S(2)}, u32[]{:S(2)}) collective-permute-start(bf16[256,128]{1,0:T(8,128)(2,1)S(1)} %add_convert_fusion), channel_id=1, source_target_pairs={{0,1},{1,0},{2,3},{3,2},{4,5},{5,4},{6,7},{7,6},{8,9},{9,8},{10,11... | collective-permute-start | bytes 196616 | tf_op jit(solution)/shard_map/ppermute | solution.py:375
  (21 other events, 266.1 us)

commit v6 on v4

v6 whole, which is shorter than its diff:
```python
import functools
import jax
import jax.numpy as jnp
from jax import lax
from jax.experimental import pallas as pl
from jax.experimental.pallas import tpu as pltpu
from jax.sharding import PartitionSpec as P

LEARN = 0.5
EPSILON = 1e-06
SPLIT = 4
PARTS = (2, 2)
NEAR_BYTES = 1 << 21
VMEM = pl.BlockSpec(memory_space=pltpu.VMEM)


def near(values, copies=1):
    if copies * values.size * values.dtype.itemsize > NEAR_BYTES:
        return values
    return pltpu.with_memory_space_constraint(values, pltpu.MemorySpace.VMEM)


def column_of(row, lanes):
    return jnp.broadcast_to(row, (lanes, row.shape[1])).T


def bits_of(count):
    assert count & (count - 1) == 0
    return count.bit_length() - 1


def split_index(index, low_count):
    return lax.shift_right_arithmetic(index, bits_of(low_count)), lax.bitwise_and(index, low_count - 1)


def position():
    device = lax.axis_index("table")
    return lax.bitwise_and(device, 1), lax.shift_right_logical(device, 1), lax.axis_index("dp")


def add_segments(total_ref, index, rows, first):
    low_count, spread_width = total_ref.shape
    width = rows.shape[1]
    split = spread_width // width
    block, low = split_index(index, low_count)
    low = jnp.where((block < 0) | (block >= split), -1, low)
    hits = (
        (lax.broadcasted_iota(jnp.int32, (low_count, index.shape[1]), 0) == low)
        .astype(jnp.float32)
        .astype(jnp.bfloat16)
    )
    block_column = column_of(block, width)
    rows = rows.astype(jnp.float32)
    spread = jnp.concatenate(
        [jnp.where(block_column == i, rows, 0.0).astype(jnp.bfloat16) for i in range(split)], axis=1
    )
    part = jnp.dot(hits, spread, preferred_element_type=jnp.float32)
    if first:
        total_ref[...] = part
    else:
        total_ref[...] += part


def put_segments(out_ref, total_ref):
    low_count, width = total_ref.shape[0], out_ref.shape[1]
    for i in range(total_ref.shape[1] // width):
        out_ref[i * low_count : (i + 1) * low_count, :] = total_ref[
            :, i * width : (i + 1) * width
        ].astype(out_ref.dtype)


def segment_kernel(asked_ref, *refs, base):
    out_ref, total_ref = refs[-2:]
    count = (len(refs) - 2) // 2
    core, chip, _ = position()
    for k in range(count):
        sources = [2 * (chip ^ k ^ far) + (core ^ side) for side in range(2) for far in (0, count)]
        index = jnp.concatenate([asked_ref[source] for source in sources], axis=1) - base
        rows = jnp.concatenate([refs[k][...], refs[count + k][...]], axis=0)
        add_segments(total_ref, index, rows, k == 0)
    put_segments(out_ref, total_ref)


def row_gradients(asked, grads, peer_grads, base, row_count):
    width = grads[0].shape[1]
    split = SPLIT if row_count > 4 * 256 else SPLIT // 2
    return pl.pallas_call(
        functools.partial(segment_kernel, base=base),
        in_specs=[VMEM] * (1 + 2 * len(grads)),
        out_specs=VMEM,
        out_shape=pltpu.VMEM((row_count, width), jnp.bfloat16),
        scratch_shapes=[pltpu.VMEM((row_count // split, split * width), jnp.float32)],
    )(near(asked), *[near(g, 2 * len(grads)) for g in (*grads, *peer_grads)])


def gather_kernel(asked_ref, table_ref, *refs, together):
    out_refs, (arrived_ref, held_ref, sems) = refs[:2], refs[2:]
    low_count, width = held_ref.shape[0], table_ref.shape[1]
    bags = asked_ref.shape[2]
    core, _, _ = position()
    copies = []
    for i in range(SPLIT):
        at = pl.ds(i * low_count, low_count)
        copies.append(pltpu.make_async_copy(table_ref.at[at, :], arrived_ref.at[at, :], sems.at[i]))
        copies[i].start()
    for i in range(SPLIT):
        copies[i].wait()
        rows = arrived_ref[i * low_count : (i + 1) * low_count, :]
        held_ref[:, i * width : (i + 1) * width] = rows.astype(jnp.bfloat16)
    lane = lax.broadcasted_iota(jnp.int32, (together * bags, width), 1)
    for side in (1, 0):
        for j in range(0, asked_ref.shape[0] // 2, together):
            index = jnp.concatenate(
                [asked_ref[2 * (j + i) + (core ^ side)] for i in range(together)], axis=1
            )
            block, low = split_index(column_of(index, width), low_count)
            hits = jnp.concatenate(
                [
                    (lane == low - first).astype(jnp.float32).astype(jnp.bfloat16)
                    for first in range(0, low_count, width)
                ],
                axis=1,
            )
            found = jnp.dot(hits, held_ref[...], preferred_element_type=jnp.float32)
            row = jnp.where(block == 0, found[:, :width], 0.0)
            for i in range(1, SPLIT):
                row = jnp.where(block == i, found[:, i * width : (i + 1) * width], row)
            out_refs[side][j * bags : (j + together) * bags, :] = row.astype(jnp.bfloat16)


def named_rows(asked, table):
    row_count, width = table.shape
    sources, _, bags = asked.shape
    rows = jax.ShapeDtypeStruct((sources // 2 * bags, width), jnp.bfloat16)
    return pl.pallas_call(
        functools.partial(gather_kernel, together=2),
        in_specs=[VMEM, pl.BlockSpec(memory_space=pl.ANY)],
        out_specs=[VMEM, VMEM],
        out_shape=[rows, rows],
        scratch_shapes=[
            pltpu.VMEM(table.shape, table.dtype),
            pltpu.VMEM((row_count // SPLIT, SPLIT * width), jnp.bfloat16),
            pltpu.SemaphoreType.DMA((SPLIT,)),
        ],
    )(near(asked), table)


def diagonal_of(width):
    rows = lax.broadcasted_iota(jnp.int32, (width, width), 0)
    return rows == lax.broadcasted_iota(jnp.int32, (width, width), 1)


def fresh_accum_of(grads, accum_line, diagonal):
    width = grads.shape[1]
    rest, terms = grads * grads + jnp.where(diagonal, accum_line * width, 0.0), []
    for _ in range(3):
        terms.append(rest.astype(jnp.bfloat16))
        rest = rest - terms[-1].astype(jnp.float32)
    ones = jnp.ones((3 * width, width), jnp.bfloat16)
    sums = jnp.dot(jnp.concatenate(terms, axis=1), ones, preferred_element_type=jnp.float32)
    return sums * (1.0 / width)


def change_kernel(own_ref, other_ref, accum_ref, new_accum_ref, delta_ref, *, base):
    rows, width = own_ref.shape
    diagonal = diagonal_of(width)
    for j in range(rows // width):
        at = slice(j * width, (j + 1) * width)
        line = base // width + j
        grads = own_ref[at, :].astype(jnp.float32) + other_ref[at, :].astype(jnp.float32)
        fresh_accum = fresh_accum_of(grads, accum_ref[line : line + 1, :], diagonal)
        delta_ref[at, :] = (-LEARN * grads / jnp.sqrt(fresh_accum + EPSILON)).astype(jnp.bfloat16)
        new_accum_ref[j : j + 1, :] = jnp.sum(
            jnp.where(diagonal, fresh_accum, 0.0), axis=0, keepdims=True
        )


def changes_of(own, other, accum, base):
    rows, width = own.shape
    return pl.pallas_call(
        functools.partial(change_kernel, base=base),
        in_specs=[VMEM] * 3,
        out_specs=[VMEM, VMEM],
        out_shape=[
            jax.ShapeDtypeStruct((rows // width, width), jnp.float32),
            pltpu.VMEM((rows, width), jnp.bfloat16),
        ],
    )(*map(near, (own, other, accum)))


def finish_kernel(*refs, parts):
    accum_ref, table_ref, out_ref = refs[2 * parts :]
    step = pl.program_id(0)
    part = step // (pl.num_programs(0) // parts)
    rows, width = out_ref.shape
    lines = rows // width
    diagonal = diagonal_of(width)
    for j in range(lines):
        at = slice(j * width, (j + 1) * width)
        grads = refs[0][at, :].astype(jnp.float32) + refs[1][at, :].astype(jnp.float32)
        for i in range(1, parts):
            later = refs[2 * i][at, :].astype(jnp.float32) + refs[2 * i + 1][at, :].astype(jnp.float32)
            grads = jnp.where(part >= i, later, grads)
        fresh_accum = fresh_accum_of(grads, accum_ref[pl.ds(step * lines + j, 1), :], diagonal)
        out_ref[at, :] = table_ref[at, :] - LEARN * grads / jnp.sqrt(fresh_accum + EPSILON)


def finished_table(halves, accum, table):
    row_count, width = table.shape
    parts = len(halves)
    tile = min(512, row_count // parts)
    per_part = row_count // parts // tile
    specs = [
        pl.BlockSpec((tile, width), functools.partial(lambda i, k: (jnp.clip(k - i * per_part, 0, per_part - 1), 0), i))
        for i in range(parts)
    ]
    rows_spec = pl.BlockSpec((tile, width), lambda k: (k, 0))
    return pl.pallas_call(
        functools.partial(finish_kernel, parts=parts),
        grid=(row_count // tile,),
        in_specs=[spec for spec in specs for _ in range(2)]
        + [pl.BlockSpec(accum.shape, lambda k: (0, 0)), rows_spec],
        out_specs=rows_spec,
        out_shape=jax.ShapeDtypeStruct(table.shape, jnp.float32),
    )(*[term for pair in halves for term in pair], accum, table)


def parity_kernel(slot_ref, peer_slot_ref, delta_ref, peer_delta_ref, *refs, base, holder_rows, dp_count, tile, last):
    refs, total_ref = refs[:-1], refs[-1]
    if base > 0:
        start_ref, refs, held_ref, sem = refs[0], refs[1:-2], refs[-2], refs[-1]
        copy = pltpu.make_async_copy(start_ref, held_ref, sem)
        copy.start()
    core, chip, dp_index = position()
    part_count = holder_rows // dp_count
    line_width = slot_ref.shape[1]
    width = delta_ref.shape[1]
    for k in range(delta_ref.shape[0] // tile):
        first = (base + k * tile) // line_width
        slot = jnp.concatenate(
            [
                ref[first + i : first + i + 1, :]
                for ref in (slot_ref, peer_slot_ref)
                for i in range(tile // line_width)
            ],
            axis=1,
        )
        holder, offset = split_index(slot, holder_rows)
        part, offset = split_index(offset, part_count)
        mine = (lax.bitwise_and(holder, 1) == core) & (part == dp_index)
        target = lax.bitwise_xor(lax.shift_right_arithmetic(holder, 1), chip) * part_count + offset
        at = slice(k * tile, (k + 1) * tile)
        rows = jnp.concatenate([delta_ref[at, :], peer_delta_ref[at, :]], axis=0)
        add_segments(total_ref, jnp.where(mine, target, -1), rows, k == 0)
    if base > 0:
        copy.wait()
        total_ref[...] += held_ref[...]
    if not last:
        refs[-1][...] = total_ref[...]
        return
    low_count = total_ref.shape[0]
    out_refs = refs[-(low_count * SPLIT // part_count) :]
    for i, out_ref in enumerate(out_refs):
        block, low = divmod(i * part_count, low_count)
        out_ref[...] = total_ref[
            low : low + part_count, block * width : (block + 1) * width
        ].astype(out_ref.dtype)


def parity_changes(slot, peer_slot, delta, peer_delta, base, holder_rows, dp_count, chip_count, start, last):
    width = delta.shape[1]
    part_count = holder_rows // dp_count
    segment_count = chip_count * part_count
    held = pltpu.VMEM((segment_count // SPLIT, SPLIT * width), jnp.float32)
    return pl.pallas_call(
        functools.partial(
            parity_kernel, base=base, holder_rows=holder_rows, dp_count=dp_count,
            tile=min(1024, delta.shape[0]), last=last,
        ),
        in_specs=[VMEM] * 4 + [pl.BlockSpec(memory_space=pl.ANY)] * len(start),
        out_specs=[VMEM] * chip_count if last else VMEM,
        out_shape=[pltpu.VMEM((part_count, width), jnp.bfloat16)] * chip_count
        if last
        else jax.ShapeDtypeStruct(held.shape, held.dtype),
        scratch_shapes=([held, pltpu.SemaphoreType.DMA] if start else []) + [held],
    )(*map(near, (slot, peer_slot, delta, peer_delta)), *start)


def on_device(owners, local_rows, grad_pooled, table, accum, parity, parity_slot):
    table_count = lax.axis_size("table")
    dp_count = lax.axis_size("dp")
    chip_count = table_count // 2
    half = table_count // 2
    bag_count, _ = owners.shape
    row_count, width = table.shape
    parity_count = parity.shape[0]
    dp_index = lax.axis_index("dp")
    same_core = [list(range(c, table_count, 2)) for c in range(2)]

    def swap(values, distance):
        return lax.ppermute(values, "table", [(i, i ^ distance) for i in range(table_count)])

    def exchange(values):
        return lax.all_to_all(
            values, "table", split_axis=0, concat_axis=0, axis_index_groups=same_core, tiled=True
        )

    far_grads = swap(grad_pooled, half)

    devices = jnp.arange(table_count, dtype=jnp.int32)[:, None, None, None]
    named = owners.T[None, None] == devices
    requests = jnp.max(jnp.where(named, local_rows.T[None, None], -1), axis=2)
    asked = lax.all_to_all(requests, "table", split_axis=0, concat_axis=0, tiled=True)
    line_width = 4 * width
    slot_lines = parity_slot.reshape(-1, line_width)
    peer_slot_lines = swap(slot_lines, 1)

    grads = [jnp.concatenate([grad_pooled, far_grads], axis=0)]
    for k in range(1, chip_count // 2):
        grads.append(swap(grads[0], 2 * k))
    peer_grads = []
    for values in grads:
        peer_grads.append(swap(values, 1))

    own_named, peer_named = named_rows(asked, table)
    found = swap(peer_named, 1)
    fetched = (own_named.astype(jnp.float32) + found.astype(jnp.float32)).astype(jnp.bfloat16)

    halves, bases = [], []
    for part, share in enumerate(PARTS):
        part_rows = row_count // share
        bases.append(sum(row_count // other for other in PARTS[:part]))
        mine = row_gradients(asked, grads, peer_grads, bases[part], part_rows)
        distance = 1
        other = lax.ppermute(mine, "dp", [(i, i ^ 1) for i in range(dp_count)])
        while 2 * distance < dp_count:
            distance *= 2
            mine = (mine.astype(jnp.float32) + other.astype(jnp.float32)).astype(jnp.bfloat16)
            other = lax.ppermute(mine, "dp", [(i, i ^ distance) for i in range(dp_count)])
        halves.append((mine, other))

    returned = exchange(fetched.reshape(chip_count, bag_count, width))

    accums, changes = [], []
    accum_lines = accum.reshape(-1, width)
    for part, (mine, other) in enumerate(halves):
        fresh_accum, delta = changes_of(mine, other, accum_lines, bases[part])
        accums.append(fresh_accum)
        peer_delta = swap(delta, 1)
        changes = parity_changes(
            slot_lines, peer_slot_lines, delta, peer_delta, bases[part],
            parity_count, dp_count, chip_count, changes, part == len(PARTS) - 1,
        )
        if part < len(PARTS) - 1:
            changes = [changes]
    arrived = [changes[0]]
    for k in range(1, chip_count):
        arrived.append(swap(changes[k], 2 * k))
    pooled = jnp.sum(returned.astype(jnp.float32), axis=0).astype(jnp.bfloat16)
    new_table = finished_table(halves, accum_lines, table)
    new_accum = jnp.concatenate(accums, axis=0).reshape(row_count)
    part = sum(values.astype(jnp.float32) for values in arrived).astype(jnp.bfloat16)
    if dp_count == 2:
        other = lax.ppermute(part, "dp", [(0, 1), (1, 0)])
        parts = jnp.where(dp_index == 0, jnp.stack([part, other]), jnp.stack([other, part]))
    else:
        parts = lax.all_gather(part, "dp", axis=0)
    new_parity = parity + parts.reshape(parity_count, width).astype(jnp.float32)
    return (pooled, new_table, new_accum, new_parity)


def solution(mesh):
    in_specs = (
        P(("table", "dp"), None),
        P(("table", "dp"), None),
        P(("table", "dp"), None),
        P("table", None),
        P("table"),
        P("table", None),
        P("table"),
    )
    out_specs = (P(("table", "dp"), None), P("table", None), P("table"), P("table", None))

    return jax.shard_map(on_device, mesh=mesh, in_specs=in_specs, out_specs=out_specs, check_vma=False)
```

time: 111 us -> 122 us (1.099)
  waiting for transfers between devices: 16.7 us -> 34 us
  starting transfers between devices: 34.9 us -> 24 us
  other arithmetic: 3.68 us -> 7.17 us
  local copies, waits for them, and re-layouts: 0.1 us -> 1.92 us
    ppermute x20 -> x19, starting transfers between devices: 26.9 us -> 15.7 us  [swap(): lax.ppermute(values, 'table', [(i, i ^ distance) for i in range(table_cou...]
    ppermute x20 -> x19, waiting for transfers between devices: 14.5 us -> 23.5 us  [swap(): lax.ppermute(values, 'table', [(i, i ^ distance) for i in range(table_cou...]
    ppermute x2, waiting for transfers between devices: 0.01 us -> 8.33 us  [on_device(): other = lax.ppermute(mine, 'dp', [(i, i ^ 1) for i in range(dp_count)])]
    convert_element_type x1, other arithmetic: 0.01 us -> 2.8 us  [on_device(): (own_named.astype(jnp.float32) + found.astype(jnp.float32)).astype(jnp.bf...]
    unnamed x17 -> x23, local copies, waits for them, and re-layouts: 0.05 us -> 1.88 us
  transfers between devices with their start and end apart: 24 -> 23, of which waited for: 11 -> 10; matrix products, arithmetic and copies ran while one was open for 2% -> 4% of each run, Pallas kernels for 34% -> 23%
where the time goes in v6:
time: 122 us
  Pallas kernels  40 us (33%)
  waiting for transfers between devices  34 us (28%)
  starting transfers between devices  24 us (20%)
  blocking collectives  13.8 us (11%)
  other arithmetic  7.17 us (6%)
  local copies, waits for them, and re-layouts  1.92 us (2%)
    ppermute x19, waiting for transfers between devices, swap(): lax.ppermute(values, 'table', [(i, i ^ distance) for i in range(table_cou...  23.5 us
    ppermute x19, starting transfers between devices, swap(): lax.ppermute(values, 'table', [(i, i ^ distance) for i in range(table_cou...  15.7 us
    all_to_all x1, blocking collectives, on_device(): lax.all_to_all(requests, 'table', split_axis=0, concat_axis=0, tiled=True)  13.8 us
    pallas_call x1, Pallas kernels, named_rows(): pl.pallas_call(functools.partial(gather_kernel, together=2), in_specs=[VM...  11.5 us
    pallas_call x2, Pallas kernels, row_gradients(): pl.pallas_call(functools.partial(segment_kernel, base=base), in_specs=[VM...  9.8 us
    ppermute x2, waiting for transfers between devices, on_device(): other = lax.ppermute(mine, 'dp', [(i, i ^ 1) for i in range(dp_count)])  8.33 us
    pallas_call x1, Pallas kernels, finished_table(): pl.pallas_call(functools.partial(finish_kernel, parts=parts), grid=(row_c...  7.34 us
    pallas_call x2, Pallas kernels, parity_changes(): pl.pallas_call(functools.partial(parity_kernel, base=base, holder_rows=ho...  7.1 us
  transfers between devices with their start and end apart: 23, of which 10 were waited for; matrix products, arithmetic and copies ran while one was open for 4% of the time, Pallas kernels for 23%

profile of v6, /device:TPU:0, one launch (start us, length us, event | category | flops | bytes accessed | tf_op | source)
XLA Modules:
  0.0 121.8 jit_solution(17000983135806484334)
XLA Ops:
  1.6 13.8 %all_to_all.10.asked_ref = s32[16,1,512]{2,1,0:T(1,128)S(1)} all-to-all(s32[16,1,512]{2,1,0:T(1,128)S(1)} %reduce_max.12), channel_id=1, replica_groups=mesh['table'=16,'dp'=2] {'table'}, dimensions={0} | all-to-all | bytes 65536 | tf_op jit(solution)/shard_map/all_to_all | solution.py:313
  15.4 11.5 %shard_map.102 = (bf16[4096,128]{1,0:T(8,128)(2,1)}, bf16[4096,128]{1,0:T(8,128)(2,1)}) custom-call(s32[16,1,512]{2,1,0:T(1,128)S(1)} %all_to_all.10.asked_ref, f32[4096,128]{1,0:T(8,128)} %refs_5_.1), custom_call_target="tpu_custom_call" | custom-call | tf_op jit(solution)/shard_map/pallas_call | solution.py:135
  27.5 8.9 %collective-permute-done.1 = bf16[512,128]{1,0:T(8,128)(2,1)S(1)} collective-permute-done((bf16[512,128]{1,0:T(8,128)(2,1)S(1)}, bf16[512,128]{1,0:T(8,128)(2,1)S(1)}, u32[]{:S(2)}, u32[]{:S(2)}) %collective-permute-start.1) | collective-permute-done | bytes 131104 | tf_op jit(solution)/shard_map/ppermute | solution.py:301
  37.0 2.9 %collective-permute-start.4 = (bf16[1024,128]{1,0:T(8,128)(2,1)S(1)}, bf16[1024,128]{1,0:T(8,128)(2,1)S(1)}, u32[]{:S(2)}, u32[]{:S(2)}) collective-permute-start(bf16[1024,128]{1,0:T(8,128)(2,1)S(1)} %constant_dynamic-update-slice_fusion.refs_0_), channel_id=1, source_target_pairs={{0,12},{2,14},{4,8},{6,10},{8,4},{10,6},{12,0},{14,2},{16,28},{18,... | collective-permute-start | bytes 786440 | tf_op jit(solution)/shard_map/ppermute | solution.py:301
  39.9 4.8 %collective-permute-done.2.refs_1_ = bf16[1024,128]{1,0:T(8,128)(2,1)S(1)} collective-permute-done((bf16[1024,128]{1,0:T(8,128)(2,1)S(1)}, bf16[1024,128]{1,0:T(8,128)(2,1)S(1)}, u32[]{:S(2)}, u32[]{:S(2)}) %collective-permute-start.2) | collective-permute-done | bytes 262176 | tf_op jit(solution)/shard_map/ppermute | solution.py:301
  46.2 5.3 %collective-permute-done.4.refs_3_ = bf16[1024,128]{1,0:T(8,128)(2,1)S(1)} collective-permute-done((bf16[1024,128]{1,0:T(8,128)(2,1)S(1)}, bf16[1024,128]{1,0:T(8,128)(2,1)S(1)}, u32[]{:S(2)}, u32[]{:S(2)}) %collective-permute-start.4) | collective-permute-done | bytes 262176 | tf_op jit(solution)/shard_map/ppermute | solution.py:301
  53.0 4.9 %shard_map.103.refs_0_.own_ref = bf16[2048,128]{1,0:T(8,128)(2,1)S(1)} custom-call(s32[16,1,512]{2,1,0:T(1,128)S(1)} %all_to_all.10.asked_ref, bf16[1024,128]{1,0:T(8,128)(2,1)S(1)} %constant_dynamic-update-slice_fusion.refs_0_, bf16[1024,128]{1,0:T(8,128)(2,1)S(1)} %collective-permute-done.2.refs_1_, bf16[1024,128]{1,0:T(8,128)(2,1)S(1)} %collective-permute-done.3.refs_2_, ...), custom_call_target="tpu_custom_call" | custom-call | tf_op jit(solution)/shard_map/pallas_call | solution.py:87
  58.0 1.7 %collective-permute-start.9 = (bf16[2048,128]{1,0:T(8,128)(2,1)S(1)}, bf16[2048,128]{1,0:T(8,128)(2,1)}, u32[]{:S(2)}, u32[]{:S(2)}) collective-permute-start(bf16[2048,128]{1,0:T(8,128)(2,1)S(1)} %shard_map.103.refs_0_.own_ref), channel_id=1, source_target_pairs={{0,1},{1,0},{2,3},{3,2},{4,5},{5,4},{6,7},{7,6},{8,9},{9,8},{10,11... | collective-permute-start | bytes 1572872 | tf_op jit(solution)/shard_map/ppermute | solution.py:335
  59.7 4.9 %shard_map.104.refs_2_.own_ref = bf16[2048,128]{1,0:T(8,128)(2,1)S(1)} custom-call(s32[16,1,512]{2,1,0:T(1,128)S(1)} %all_to_all.10.asked_ref, bf16[1024,128]{1,0:T(8,128)(2,1)S(1)} %constant_dynamic-update-slice_fusion.refs_0_, bf16[1024,128]{1,0:T(8,128)(2,1)S(1)} %collective-permute-done.2.refs_1_, bf16[1024,128]{1,0:T(8,128)(2,1)S(1)} %collective-permute-done.3.refs_2_, ...), custom_call_target="tpu_custom_call" | custom-call | tf_op jit(solution)/shard_map/pallas_call | solution.py:87
  65.2 2.8 %add_convert_fusion = bf16[4096,128]{1,0:T(8,128)(2,1)} fusion(bf16[4096,128]{1,0:T(8,128)(2,1)} %collective-permute-done, bf16[4096,128]{1,0:T(8,128)(2,1)} %get-tuple-element.18), kind=kLoop, calls=%fused_computation | loop fusion | flops 2097152 | bytes 3145728 | tf_op jit(solution)/shard_map/convert_element_type | solution.py:327
  68.0 4.4 %all-to-all-start.1 = ((bf16[8,512,128]{2,1,0:T(8,128)(2,1)}), bf16[8,512,128]{2,1,0:T(8,128)(2,1)}, u32[]{:S(2)}, u32[]{:S(2)}) async-start(bf16[8,512,128]{2,1,0:T(8,128)(2,1)} %bitcast.2), calls=%async_computation.1 | async-start | bytes 2097152 | tf_op jit(solution)/shard_map/all_to_all | solution.py:304
  73.1 2.7 %shard_map.106 = (f32[16,128]{1,0:T(8,128)}, bf16[2048,128]{1,0:T(8,128)(2,1)S(1)}) custom-call(bf16[2048,128]{1,0:T(8,128)(2,1)S(1)} %shard_map.103.refs_0_.own_ref, bf16[2048,128]{1,0:T(8,128)(2,1)} %collective-permute-done.9.refs_1_.other_ref, f32[32,128]{1,0:T(8,128)S(1)} %bitcast.12), custom_call_target="tpu_custom_call" | custom-call | tf_op jit(solution)/shard_map/pallas_call | solution.py:180
  75.8 7.6 %collective-permute-done.10.refs_3_.other_ref = bf16[2048,128]{1,0:T(8,128)(2,1)S(1)} collective-permute-done((bf16[2048,128]{1,0:T(8,128)(2,1)S(1)}, bf16[2048,128]{1,0:T(8,128)(2,1)S(1)}, u32[]{:S(2)}, u32[]{:S(2)}) %collective-permute-start.10) | collective-permute-done | bytes 524320 | tf_op jit(solution)/shard_map/ppermute | solution.py:335
  83.4 1.6 %shard_map.107 = (f32[16,128]{1,0:T(8,128)}, bf16[2048,128]{1,0:T(8,128)(2,1)S(1)}) custom-call(bf16[2048,128]{1,0:T(8,128)(2,1)S(1)} %shard_map.104.refs_2_.own_ref, bf16[2048,128]{1,0:T(8,128)(2,1)S(1)} %collective-permute-done.10.refs_3_.other_ref, f32[32,128]{1,0:T(8,128)S(1)} %bitcast.13), custom_call_target="tpu_custom_call" | custom-call | tf_op jit(solution)/shard_map/pallas_call | solution.py:180
  88.8 3.5 %shard_map.108.refs_0_ = f32[512,512]{1,0:T(8,128)} custom-call(s32[8,512]{1,0:T(8,128)S(1)} %reshape.55.slot_ref, s32[8,512]{1,0:T(8,128)S(1)} %collective-permute-done.11.peer_slot_ref, bf16[2048,128]{1,0:T(8,128)(2,1)S(1)} %get-tuple-element.23.delta_ref, bf16[2048,128]{1,0:T(8,128)(2,1)S(1)} %copy-done.4), custom_call_target="tpu_custom_call" | custom-call | tf_op jit(solution)/shard_map/pallas_call | solution.py:275
  92.4 3.6 %shard_map.109 = (bf16[256,128]{1,0:T(8,128)(2,1)S(1)}, bf16[256,128]{1,0:T(8,128)(2,1)S(1)}, bf16[256,128]{1,0:T(8,128)(2,1)S(1)}, bf16[256,128]{1,0:T(8,128)(2...) custom-call(s32[8,512]{1,0:T(8,128)S(1)} %reshape.55.slot_ref, ...), custom_call_target="tpu_custom_call" | custom-call | tf_op jit(solution)/shard_map/pallas_call | solution.py:275
  96.1 3.6 %collective-permute-start.19 = (bf16[256,128]{1,0:T(8,128)(2,1)S(1)}, bf16[256,128]{1,0:T(8,128)(2,1)S(1)}, u32[]{:S(2)}, u32[]{:S(2)}) collective-permute-start(bf16[256,128]{1,0:T(8,128)(2,1)S(1)} %get-tuple-element.30), channel_id=1, source_target_pairs={{0,24},{2,26},{4,28},{6,30},{8,16},{10,18},{12,20},{14,22},{16,8},... | collective-permute-start | bytes 196616 | tf_op jit(solution)/shard_map/ppermute | solution.py:301
  99.7 3.9 %collective-permute-start.17 = (bf16[256,128]{1,0:T(8,128)(2,1)S(1)}, bf16[256,128]{1,0:T(8,128)(2,1)S(1)}, u32[]{:S(2)}, u32[]{:S(2)}) collective-permute-start(bf16[256,128]{1,0:T(8,128)(2,1)S(1)} %get-tuple-element.28), channel_id=1, source_target_pairs={{0,16},{2,18},{4,20},{6,22},{8,24},{10,26},{12,28},{14,30},{16,0},... | collective-permute-start | bytes 196616 | tf_op jit(solution)/shard_map/ppermute | solution.py:301
  103.8 1.8 %collective-permute-start.15 = (bf16[256,128]{1,0:T(8,128)(2,1)S(1)}, bf16[256,128]{1,0:T(8,128)(2,1)S(1)}, u32[]{:S(2)}, u32[]{:S(2)}) collective-permute-start(bf16[256,128]{1,0:T(8,128)(2,1)S(1)} %get-tuple-element.26), channel_id=1, source_target_pairs={{0,8},{2,10},{4,12},{6,14},{8,0},{10,2},{12,4},{14,6},{16,24},{18,... | collective-permute-start | bytes 196616 | tf_op jit(solution)/shard_map/ppermute | solution.py:301
  105.6 1.6 %collective-permute-start.14 = (bf16[256,128]{1,0:T(8,128)(2,1)S(1)}, bf16[256,128]{1,0:T(8,128)(2,1)S(1)}, u32[]{:S(2)}, u32[]{:S(2)}) collective-permute-start(bf16[256,128]{1,0:T(8,128)(2,1)S(1)} %get-tuple-element.25), channel_id=1, source_target_pairs={{0,4},{2,6},{4,0},{6,2},{8,12},{10,14},{12,8},{14,10},{16,20},{18,... | collective-permute-start | bytes 196616 | tf_op jit(solution)/shard_map/ppermute | solution.py:301
  107.2 7.3 %shard_map.105 = f32[4096,128]{1,0:T(8,128)} custom-call(bf16[2048,128]{1,0:T(8,128)(2,1)} %copy-done, bf16[2048,128]{1,0:T(8,128)(2,1)} %collective-permute-done.9.refs_1_.other_ref, bf16[2048,128]{1,0:T(8,128)(2,1)} %copy-done.1, bf16[2048,128]{1,0:T(8,128)(2,1)} %copy-done.2, f32[32,128]{1,0:T(8,128)} %bitcast.11, f32[4096,128]{1,0:T(8,128)} %refs_5_.1), custom_call_target="tpu_custom_call" | custom-call | tf_op jit(solution)/shard_map/pallas_call | solution.py:218
  114.6 1.6 %collective-permute-start.21 = (bf16[256,128]{1,0:T(8,128)(2,1)S(1)}, bf16[256,128]{1,0:T(8,128)(2,1)S(1)}, u32[]{:S(2)}, u32[]{:S(2)}) collective-permute-start(bf16[256,128]{1,0:T(8,128)(2,1)S(1)} %add_convert_fusion.1), channel_id=1, source_target_pairs={{0,1},{1,0},{2,3},{3,2},{4,5},{5,4},{6,7},{7,6},{8,9},{9,8},{10,11... | collective-permute-start | bytes 196616 | tf_op jit(solution)/shard_map/ppermute | solution.py:364
  116.8 2.2 %collective-permute-done.21 = bf16[256,128]{1,0:T(8,128)(2,1)S(1)} collective-permute-done((bf16[256,128]{1,0:T(8,128)(2,1)S(1)}, bf16[256,128]{1,0:T(8,128)(2,1)S(1)}, u32[]{:S(2)}, u32[]{:S(2)}) %collective-permute-start.21) | collective-permute-done | bytes 65568 | tf_op jit(solution)/shard_map/ppermute | solution.py:364
  119.7 2.1 %reduce_sum.12 = bf16[512,128]{1,0:T(8,128)(2,1)} reduce(bf16[8,512,128]{2,1,0:T(8,128)(2,1)} %all-to-all-done.1, bf16[]{:T(256)} %constant.3.clone.1), dimensions={0}, to_apply=%region_1.2 | reduce | flops 458752 | bytes 1179650 | tf_op jit(solution)/shard_map/reduce_sum | solution.py:359
  (64 shorter events, 12.0 us)
Async XLA Ops:
  0.6 26.3 %copy-start.7 = (bf16[512,128]{1,0:T(8,128)(2,1)S(1)}, bf16[512,128]{1,0:T(8,128)(2,1)}, u32[]{:S(2)}) copy-start(bf16[512,128]{1,0:T(8,128)(2,1)} %param.9) | copy-start | bytes 393220
  26.9 38.3 %collective-permute-start = (bf16[4096,128]{1,0:T(8,128)(2,1)}, bf16[4096,128]{1,0:T(8,128)(2,1)}, u32[]{:S(2)}, u32[]{:S(2)}) collective-permute-start(bf16[4096,128]{1,0:T(8,128)(2,1)} %get-tuple-element.19), channel_id=1, source_target_pairs={{0,2},{2,0},{4,6},{6,4},{8,10},{10,8},{12,14},{14,12},{16,18},{18,... | collective-permute-start | bytes 3145736 | tf_op jit(solution)/shard_map/ppermute | solution.py:301
  27.0 9.4 %collective-permute-start.1 = (bf16[512,128]{1,0:T(8,128)(2,1)S(1)}, bf16[512,128]{1,0:T(8,128)(2,1)S(1)}, u32[]{:S(2)}, u32[]{:S(2)}) collective-permute-start(bf16[512,128]{1,0:T(8,128)(2,1)S(1)} %copy-done.7), channel_id=1, source_target_pairs={{0,16},{2,18},{4,20},{6,22},{8,24},{10,26},{12,28},{14,30},{16,0},... | collective-permute-start | bytes 393224 | tf_op jit(solution)/shard_map/ppermute | solution.py:301
  36.4 8.3 %collective-permute-start.2 = (bf16[1024,128]{1,0:T(8,128)(2,1)S(1)}, bf16[1024,128]{1,0:T(8,128)(2,1)S(1)}, u32[]{:S(2)}, u32[]{:S(2)}) collective-permute-start(bf16[1024,128]{1,0:T(8,128)(2,1)S(1)} %constant_dynamic-update-slice_fusion.refs_0_), channel_id=1, source_target_pairs={{0,4},{2,6},{4,0},{6,2},{8,12},{10,14},{12,8},{14,10},{16,20},{18,... | collective-permute-start | bytes 786440 | tf_op jit(solution)/shard_map/ppermute | solution.py:301
  37.0 9.2 %collective-permute-start.3 = (bf16[1024,128]{1,0:T(8,128)(2,1)S(1)}, bf16[1024,128]{1,0:T(8,128)(2,1)S(1)}, u32[]{:S(2)}, u32[]{:S(2)}) collective-permute-start(bf16[1024,128]{1,0:T(8,128)(2,1)S(1)} %constant_dynamic-update-slice_fusion.refs_0_), channel_id=1, source_target_pairs={{0,8},{2,10},{4,12},{6,14},{8,0},{10,2},{12,4},{14,6},{16,24},{18,... | collective-permute-start | bytes 786440 | tf_op jit(solution)/shard_map/ppermute | solution.py:301
  37.0 14.5 %collective-permute-start.4 = (bf16[1024,128]{1,0:T(8,128)(2,1)S(1)}, bf16[1024,128]{1,0:T(8,128)(2,1)S(1)}, u32[]{:S(2)}, u32[]{:S(2)}) collective-permute-start(bf16[1024,128]{1,0:T(8,128)(2,1)S(1)} %constant_dynamic-update-slice_fusion.refs_0_), channel_id=1, source_target_pairs={{0,12},{2,14},{4,8},{6,10},{8,4},{10,6},{12,0},{14,2},{16,28},{18,... | collective-permute-start | bytes 786440 | tf_op jit(solution)/shard_map/ppermute | solution.py:301
  39.9 11.6 %collective-permute-start.5 = (bf16[1024,128]{1,0:T(8,128)(2,1)S(1)}, bf16[1024,128]{1,0:T(8,128)(2,1)S(1)}, u32[]{:S(2)}, u32[]{:S(2)}) collective-permute-start(bf16[1024,128]{1,0:T(8,128)(2,1)S(1)} %constant_dynamic-update-slice_fusion.refs_0_), channel_id=1, source_target_pairs={{0,2},{2,0},{4,6},{6,4},{8,10},{10,8},{12,14},{14,12},{16,18},{18,... | collective-permute-start | bytes 786440 | tf_op jit(solution)/shard_map/ppermute | solution.py:301
  44.7 6.8 %collective-permute-start.6 = (bf16[1024,128]{1,0:T(8,128)(2,1)S(1)}, bf16[1024,128]{1,0:T(8,128)(2,1)S(1)}, u32[]{:S(2)}, u32[]{:S(2)}) collective-permute-start(bf16[1024,128]{1,0:T(8,128)(2,1)S(1)} %collective-permute-done.2.refs_1_), channel_id=1, source_target_pairs={{0,2},{2,0},{4,6},{6,4},{8,10},{10,8},{12,14},{14,12},{16,18},{18,... | collective-permute-start | bytes 786440 | tf_op jit(solution)/shard_map/ppermute | solution.py:301
  46.2 5.3 %collective-permute-start.7 = (bf16[1024,128]{1,0:T(8,128)(2,1)S(1)}, bf16[1024,128]{1,0:T(8,128)(2,1)S(1)}, u32[]{:S(2)}, u32[]{:S(2)}) collective-permute-start(bf16[1024,128]{1,0:T(8,128)(2,1)S(1)} %collective-permute-done.3.refs_2_), channel_id=1, source_target_pairs={{0,2},{2,0},{4,6},{6,4},{8,10},{10,8},{12,14},{14,12},{16,18},{18,... | collective-permute-start | bytes 786440 | tf_op jit(solution)/shard_map/ppermute | solution.py:301
  51.5 1.5 %collective-permute-start.8 = (bf16[1024,128]{1,0:T(8,128)(2,1)S(1)}, bf16[1024,128]{1,0:T(8,128)(2,1)S(1)}, u32[]{:S(2)}, u32[]{:S(2)}) collective-permute-start(bf16[1024,128]{1,0:T(8,128)(2,1)S(1)} %collective-permute-done.4.refs_3_), channel_id=1, source_target_pairs={{0,2},{2,0},{4,6},{6,4},{8,10},{10,8},{12,14},{14,12},{16,18},{18,... | collective-permute-start | bytes 786440 | tf_op jit(solution)/shard_map/ppermute | solution.py:301
  58.0 15.1 %collective-permute-start.9 = (bf16[2048,128]{1,0:T(8,128)(2,1)S(1)}, bf16[2048,128]{1,0:T(8,128)(2,1)}, u32[]{:S(2)}, u32[]{:S(2)}) collective-permute-start(bf16[2048,128]{1,0:T(8,128)(2,1)S(1)} %shard_map.103.refs_0_.own_ref), channel_id=1, source_target_pairs={{0,1},{1,0},{2,3},{3,2},{4,5},{5,4},{6,7},{7,6},{8,9},{9,8},{10,11... | collective-permute-start | bytes 1572872 | tf_op jit(solution)/shard_map/ppermute | solution.py:335
  64.6 18.8 %collective-permute-start.10 = (bf16[2048,128]{1,0:T(8,128)(2,1)S(1)}, bf16[2048,128]{1,0:T(8,128)(2,1)S(1)}, u32[]{:S(2)}, u32[]{:S(2)}) collective-permute-start(bf16[2048,128]{1,0:T(8,128)(2,1)S(1)} %shard_map.104.refs_2_.own_ref), channel_id=1, source_target_pairs={{0,1},{1,0},{2,3},{3,2},{4,5},{5,4},{6,7},{7,6},{8,9},{9,8},{10,11... | collective-permute-start | bytes 1572872 | tf_op jit(solution)/shard_map/ppermute | solution.py:335
  68.0 51.7 %all-to-all-start.1 = ((bf16[8,512,128]{2,1,0:T(8,128)(2,1)}), bf16[8,512,128]{2,1,0:T(8,128)(2,1)}, u32[]{:S(2)}, u32[]{:S(2)}) async-start(bf16[8,512,128]{2,1,0:T(8,128)(2,1)} %bitcast.2), calls=%async_computation.1 | async-start | bytes 2097152 | tf_op jit(solution)/shard_map/all_to_all | solution.py:304
  75.8 11.2 %collective-permute-start.13 = (bf16[2048,128]{1,0:T(8,128)(2,1)S(1)}, bf16[2048,128]{1,0:T(8,128)(2,1)S(1)}, u32[]{:S(2)}, u32[]{:S(2)}) collective-permute-start(bf16[2048,128]{1,0:T(8,128)(2,1)S(1)} %get-tuple-element.23.delta_ref), channel_id=1, source_target_pairs={{0,2},{2,0},{4,6},{6,4},{8,10},{10,8},{12,14},{14,12},{16,18},{18,... | collective-permute-start | bytes 1572872 | tf_op jit(solution)/shard_map/ppermute | solution.py:301
  85.0 7.3 %collective-permute-start.12 = (bf16[2048,128]{1,0:T(8,128)(2,1)S(1)}, bf16[2048,128]{1,0:T(8,128)(2,1)S(1)}, u32[]{:S(2)}, u32[]{:S(2)}) collective-permute-start(bf16[2048,128]{1,0:T(8,128)(2,1)S(1)} %get-tuple-element.22.delta_ref), channel_id=1, source_target_pairs={{0,2},{2,0},{4,6},{6,4},{8,10},{10,8},{12,14},{14,12},{16,18},{18,... | collective-permute-start | bytes 1572872 | tf_op jit(solution)/shard_map/ppermute | solution.py:301
  85.0 1.9 %collective-permute-start.11 = (s32[8,512]{1,0:T(8,128)S(1)}, s32[8,512]{1,0:T(8,128)S(1)}, u32[]{:S(2)}, u32[]{:S(2)}) collective-permute-start(s32[8,512]{1,0:T(8,128)S(1)} %reshape.55.slot_ref), channel_id=1, source_target_pairs={{0,2},{2,0},{4,6},{6,4},{8,10},{10,8},{12,14},{14,12},{16,18},{18,... | collective-permute-start | bytes 49160 | tf_op jit(solution)/shard_map/ppermute | solution.py:301
  95.9 7.8 %collective-permute-start.20 = (bf16[256,128]{1,0:T(8,128)(2,1)S(1)}, bf16[256,128]{1,0:T(8,128)(2,1)S(1)}, u32[]{:S(2)}, u32[]{:S(2)}) collective-permute-start(bf16[256,128]{1,0:T(8,128)(2,1)S(1)} %get-tuple-element.31), channel_id=1, source_target_pairs={{0,28},{2,30},{4,24},{6,26},{8,20},{10,22},{12,16},{14,18},{16,12}... | collective-permute-start | bytes 196616 | tf_op jit(solution)/shard_map/ppermute | solution.py:301
  96.1 9.4 %collective-permute-start.19 = (bf16[256,128]{1,0:T(8,128)(2,1)S(1)}, bf16[256,128]{1,0:T(8,128)(2,1)S(1)}, u32[]{:S(2)}, u32[]{:S(2)}) collective-permute-start(bf16[256,128]{1,0:T(8,128)(2,1)S(1)} %get-tuple-element.30), channel_id=1, source_target_pairs={{0,24},{2,26},{4,28},{6,30},{8,16},{10,18},{12,20},{14,22},{16,8},... | collective-permute-start | bytes 196616 | tf_op jit(solution)/shard_map/ppermute | solution.py:301
  99.7 14.8 %collective-permute-start.18 = (bf16[256,128]{1,0:T(8,128)(2,1)S(1)}, bf16[256,128]{1,0:T(8,128)(2,1)S(1)}, u32[]{:S(2)}, u32[]{:S(2)}) collective-permute-start(bf16[256,128]{1,0:T(8,128)(2,1)S(1)} %get-tuple-element.29), channel_id=1, source_target_pairs={{0,20},{2,22},{4,16},{6,18},{8,28},{10,30},{12,24},{14,26},{16,4},... | collective-permute-start | bytes 196616 | tf_op jit(solution)/shard_map/ppermute | solution.py:301
  99.7 14.8 %collective-permute-start.17 = (bf16[256,128]{1,0:T(8,128)(2,1)S(1)}, bf16[256,128]{1,0:T(8,128)(2,1)S(1)}, u32[]{:S(2)}, u32[]{:S(2)}) collective-permute-start(bf16[256,128]{1,0:T(8,128)(2,1)S(1)} %get-tuple-element.28), channel_id=1, source_target_pairs={{0,16},{2,18},{4,20},{6,22},{8,24},{10,26},{12,28},{14,30},{16,0},... | collective-permute-start | bytes 196616 | tf_op jit(solution)/shard_map/ppermute | solution.py:301
  103.6 10.9 %collective-permute-start.16 = (bf16[256,128]{1,0:T(8,128)(2,1)S(1)}, bf16[256,128]{1,0:T(8,128)(2,1)S(1)}, u32[]{:S(2)}, u32[]{:S(2)}) collective-permute-start(bf16[256,128]{1,0:T(8,128)(2,1)S(1)} %get-tuple-element.27), channel_id=1, source_target_pairs={{0,12},{2,14},{4,8},{6,10},{8,4},{10,6},{12,0},{14,2},{16,28},{18,... | collective-permute-start | bytes 196616 | tf_op jit(solution)/shard_map/ppermute | solution.py:301
  103.8 10.8 %collective-permute-start.15 = (bf16[256,128]{1,0:T(8,128)(2,1)S(1)}, bf16[256,128]{1,0:T(8,128)(2,1)S(1)}, u32[]{:S(2)}, u32[]{:S(2)}) collective-permute-start(bf16[256,128]{1,0:T(8,128)(2,1)S(1)} %get-tuple-element.26), channel_id=1, source_target_pairs={{0,8},{2,10},{4,12},{6,14},{8,0},{10,2},{12,4},{14,6},{16,24},{18,... | collective-permute-start | bytes 196616 | tf_op jit(solution)/shard_map/ppermute | solution.py:301
  105.6 8.9 %collective-permute-start.14 = (bf16[256,128]{1,0:T(8,128)(2,1)S(1)}, bf16[256,128]{1,0:T(8,128)(2,1)S(1)}, u32[]{:S(2)}, u32[]{:S(2)}) collective-permute-start(bf16[256,128]{1,0:T(8,128)(2,1)S(1)} %get-tuple-element.25), channel_id=1, source_target_pairs={{0,4},{2,6},{4,0},{6,2},{8,12},{10,14},{12,8},{14,10},{16,20},{18,... | collective-permute-start | bytes 196616 | tf_op jit(solution)/shard_map/ppermute | solution.py:301
  114.6 4.3 %collective-permute-start.21 = (bf16[256,128]{1,0:T(8,128)(2,1)S(1)}, bf16[256,128]{1,0:T(8,128)(2,1)S(1)}, u32[]{:S(2)}, u32[]{:S(2)}) collective-permute-start(bf16[256,128]{1,0:T(8,128)(2,1)S(1)} %add_convert_fusion.1), channel_id=1, source_target_pairs={{0,1},{1,0},{2,3},{3,2},{4,5},{5,4},{6,7},{7,6},{8,9},{9,8},{10,11... | collective-permute-start | bytes 196616 | tf_op jit(solution)/shard_map/ppermute | solution.py:364
  (10 other events, 103.1 us)

commit v7 on v6

--- a/solution.py
+++ b/solution.py
@@ -10,6 +10,7 @@
 EPSILON = 1e-06
 SPLIT = 4
 PARTS = (2, 2)
+SUM_PART = 1
 NEAR_BYTES = 1 << 21
 VMEM = pl.BlockSpec(memory_space=pltpu.VMEM)
 
@@ -69,28 +70,69 @@
         ].astype(out_ref.dtype)
 
 
-def segment_kernel(asked_ref, *refs, base):
-    out_ref, total_ref = refs[-2:]
-    count = (len(refs) - 2) // 2
+def segment_kernel(asked_ref, *refs, base, count):
+    grad_refs, refs = refs[: 2 * count], refs[2 * count :]
+    if len(refs) > 2:
+        first_ref, second_ref, out_ref, sum_ref, total_ref, terms_ref, sums_ref, in_sems, out_sems = refs
+        chunk = sums_ref.shape[0] // count
+        at = [pl.ds(k * chunk, chunk) for k in range(count)]
+        loads = [
+            [
+                pltpu.make_async_copy(ref.at[at[k], :], terms_ref.at[i, at[k], :], in_sems.at[i, k])
+                for i, ref in enumerate((first_ref, second_ref))
+            ]
+            for k in range(count)
+        ]
+        stores = [
+            pltpu.make_async_copy(sums_ref.at[at[k], :], sum_ref.at[at[k], :], out_sems.at[k])
+            for k in range(count)
+        ]
+        for pair in loads:
+            for copy in pair:
+                copy.start()
+    else:
+        (out_ref, total_ref), stores = refs, []
     core, chip, _ = position()
     for k in range(count):
         sources = [2 * (chip ^ k ^ far) + (core ^ side) for side in range(2) for far in (0, count)]
         index = jnp.concatenate([asked_ref[source] for source in sources], axis=1) - base
-        rows = jnp.concatenate([refs[k][...], refs[count + k][...]], axis=0)
+        rows = jnp.concatenate([grad_refs[k][...], grad_refs[count + k][...]], axis=0)
         add_segments(total_ref, index, rows, k == 0)
+        if stores:
+            for copy in loads[k]:
+                copy.wait()
+            here = slice(k * chunk, (k + 1) * chunk)
+            terms = [terms_ref[i, here, :].astype(jnp.float32) for i in range(2)]
+            sums_ref[here, :] = (terms[0] + terms[1]).astype(jnp.bfloat16)
+            stores[k].start()
     put_segments(out_ref, total_ref)
-
-
-def row_gradients(asked, grads, peer_grads, base, row_count):
+    for copy in stores:
+        copy.wait()
+
+
+def row_gradients(asked, grads, peer_grads, base, row_count, terms=()):
     width = grads[0].shape[1]
+    count = len(grads)
     split = SPLIT if row_count > 4 * 256 else SPLIT // 2
+    anywhere = pl.BlockSpec(memory_space=pl.ANY)
+    out_shape = [pltpu.VMEM((row_count, width), jnp.bfloat16)]
+    scratch_shapes = [pltpu.VMEM((row_count // split, split * width), jnp.float32)]
+    if terms:
+        shape = terms[0].shape
+        out_shape.append(jax.ShapeDtypeStruct(shape, jnp.bfloat16))
+        scratch_shapes += [
+            pltpu.VMEM((2,) + shape, jnp.bfloat16),
+            pltpu.VMEM(shape, jnp.bfloat16),
+            pltpu.SemaphoreType.DMA((2, count)),
+            pltpu.SemaphoreType.DMA((count,)),
+        ]
     return pl.pallas_call(
-        functools.partial(segment_kernel, base=base),
-        in_specs=[VMEM] * (1 + 2 * len(grads)),
-        out_specs=VMEM,
-        out_shape=pltpu.VMEM((row_count, width), jnp.bfloat16),
-        scratch_shapes=[pltpu.VMEM((row_count // split, split * width), jnp.float32)],
-    )(near(asked), *[near(g, 2 * len(grads)) for g in (*grads, *peer_grads)])
+        functools.partial(segment_kernel, base=base, count=count),
+        in_specs=[VMEM] * (1 + 2 * count) + [anywhere] * len(terms),
+        out_specs=[VMEM] + [anywhere] * (1 if terms else 0),
+        out_shape=out_shape,
+        scratch_shapes=scratch_shapes,
+    )(near(asked), *[near(g, 2 * count) for g in (*grads, *peer_grads)], *terms)
 
 
 def gather_kernel(asked_ref, table_ref, *refs, together):
@@ -188,54 +230,29 @@
     )(*map(near, (own, other, accum)))
 
 
-def finish_kernel(*refs, parts):
-    accum_ref, table_ref, out_ref = refs[2 * parts :]
-    step = pl.program_id(0)
-    part = step // (pl.num_programs(0) // parts)
-    rows, width = out_ref.shape
-    lines = rows // width
-    diagonal = diagonal_of(width)
-    for j in range(lines):
-        at = slice(j * width, (j + 1) * width)
-        grads = refs[0][at, :].astype(jnp.float32) + refs[1][at, :].astype(jnp.float32)
-        for i in range(1, parts):
-            later = refs[2 * i][at, :].astype(jnp.float32) + refs[2 * i + 1][at, :].astype(jnp.float32)
-            grads = jnp.where(part >= i, later, grads)
-        fresh_accum = fresh_accum_of(grads, accum_ref[pl.ds(step * lines + j, 1), :], diagonal)
-        out_ref[at, :] = table_ref[at, :] - LEARN * grads / jnp.sqrt(fresh_accum + EPSILON)
-
-
-def finished_table(halves, accum, table):
-    row_count, width = table.shape
-    parts = len(halves)
-    tile = min(512, row_count // parts)
-    per_part = row_count // parts // tile
-    specs = [
-        pl.BlockSpec((tile, width), functools.partial(lambda i, k: (jnp.clip(k - i * per_part, 0, per_part - 1), 0), i))
-        for i in range(parts)
-    ]
-    rows_spec = pl.BlockSpec((tile, width), lambda k: (k, 0))
-    return pl.pallas_call(
-        functools.partial(finish_kernel, parts=parts),
-        grid=(row_count // tile,),
-        in_specs=[spec for spec in specs for _ in range(2)]
-        + [pl.BlockSpec(accum.shape, lambda k: (0, 0)), rows_spec],
-        out_specs=rows_spec,
-        out_shape=jax.ShapeDtypeStruct(table.shape, jnp.float32),
-    )(*[term for pair in halves for term in pair], accum, table)
-
-
-def parity_kernel(slot_ref, peer_slot_ref, delta_ref, peer_delta_ref, *refs, base, holder_rows, dp_count, tile, last):
-    refs, total_ref = refs[:-1], refs[-1]
+def parity_kernel(*refs, base, holder_rows, dp_count, tile, last):
+    slot_ref, peer_slot_ref, delta_ref, peer_delta_ref, table_ref = refs[:5]
+    scratch, refs = refs[-5:], refs[5:-5]
+    total_ref, old_ref, fresh_ref, load_sems, store_sems = scratch
+    steps = delta_ref.shape[0] // tile
     if base > 0:
-        start_ref, refs, held_ref, sem = refs[0], refs[1:-2], refs[-2], refs[-1]
+        start_ref, refs, held_ref, sem = refs[0], refs[2:-2], refs[-2], refs[-1]
         copy = pltpu.make_async_copy(start_ref, held_ref, sem)
         copy.start()
+    new_table_ref, out_refs = refs[0], refs[1:]
+    loads, stores = [], []
+    for k in range(steps):
+        here, there = pl.ds(k * tile, tile), pl.ds(base + k * tile, tile)
+        loads.append(pltpu.make_async_copy(table_ref.at[there, :], old_ref.at[here, :], load_sems.at[k]))
+        stores.append(
+            pltpu.make_async_copy(fresh_ref.at[here, :], new_table_ref.at[there, :], store_sems.at[k])
+        )
+        loads[k].start()
     core, chip, dp_index = position()
     part_count = holder_rows // dp_count
     line_width = slot_ref.shape[1]
     width = delta_ref.shape[1]
-    for k in range(delta_ref.shape[0] // tile):
+    for k in range(steps):
         first = (base + k * tile) // line_width
         slot = jnp.concatenate(
             [
@@ -252,38 +269,52 @@
         at = slice(k * tile, (k + 1) * tile)
         rows = jnp.concatenate([delta_ref[at, :], peer_delta_ref[at, :]], axis=0)
         add_segments(total_ref, jnp.where(mine, target, -1), rows, k == 0)
+        loads[k].wait()
+        fresh_ref[at, :] = old_ref[at, :] + delta_ref[at, :].astype(jnp.float32)
+        stores[k].start()
     if base > 0:
         copy.wait()
         total_ref[...] += held_ref[...]
-    if not last:
-        refs[-1][...] = total_ref[...]
-        return
-    low_count = total_ref.shape[0]
-    out_refs = refs[-(low_count * SPLIT // part_count) :]
-    for i, out_ref in enumerate(out_refs):
-        block, low = divmod(i * part_count, low_count)
-        out_ref[...] = total_ref[
-            low : low + part_count, block * width : (block + 1) * width
-        ].astype(out_ref.dtype)
-
-
-def parity_changes(slot, peer_slot, delta, peer_delta, base, holder_rows, dp_count, chip_count, start, last):
-    width = delta.shape[1]
+    if last:
+        low_count = total_ref.shape[0]
+        for i, out_ref in enumerate(out_refs):
+            block, low = divmod(i * part_count, low_count)
+            out_ref[...] = total_ref[
+                low : low + part_count, block * width : (block + 1) * width
+            ].astype(out_ref.dtype)
+    else:
+        out_refs[0][...] = total_ref[...]
+    for store in stores:
+        store.wait()
+
+
+def parity_changes(slot, peer_slot, delta, peer_delta, table, base, holder_rows, dp_count, chip_count, start, new_table, last):
+    rows, width = delta.shape
     part_count = holder_rows // dp_count
     segment_count = chip_count * part_count
     held = pltpu.VMEM((segment_count // SPLIT, SPLIT * width), jnp.float32)
+    anywhere = pl.BlockSpec(memory_space=pl.ANY)
+    tile = min(1024, rows)
+    changes = [pltpu.VMEM((part_count, width), jnp.bfloat16)] * chip_count
+    if not last:
+        changes = [jax.ShapeDtypeStruct(held.shape, held.dtype)]
     return pl.pallas_call(
         functools.partial(
-            parity_kernel, base=base, holder_rows=holder_rows, dp_count=dp_count,
-            tile=min(1024, delta.shape[0]), last=last,
+            parity_kernel, base=base, holder_rows=holder_rows, dp_count=dp_count, tile=tile, last=last
         ),
-        in_specs=[VMEM] * 4 + [pl.BlockSpec(memory_space=pl.ANY)] * len(start),
-        out_specs=[VMEM] * chip_count if last else VMEM,
-        out_shape=[pltpu.VMEM((part_count, width), jnp.bfloat16)] * chip_count
-        if last
-        else jax.ShapeDtypeStruct(held.shape, held.dtype),
-        scratch_shapes=([held, pltpu.SemaphoreType.DMA] if start else []) + [held],
-    )(*map(near, (slot, peer_slot, delta, peer_delta)), *start)
+        in_specs=[VMEM] * 4 + [anywhere] * (1 + len(start) + len(new_table)),
+        out_specs=[anywhere] + [VMEM] * len(changes),
+        out_shape=[jax.ShapeDtypeStruct(table.shape, jnp.float32)] + changes,
+        scratch_shapes=([held, pltpu.SemaphoreType.DMA] if start else [])
+        + [
+            held,
+            pltpu.VMEM((rows, width), jnp.float32),
+            pltpu.VMEM((rows, width), jnp.float32),
+            pltpu.SemaphoreType.DMA((rows // tile,)),
+            pltpu.SemaphoreType.DMA((rows // tile,)),
+        ],
+        input_output_aliases={6: 0} if new_table else {},
+    )(*map(near, (slot, peer_slot, delta, peer_delta)), table, *start, *new_table)
 
 
 def on_device(owners, local_rows, grad_pooled, table, accum, parity, parity_slot):
@@ -324,13 +355,15 @@
 
     own_named, peer_named = named_rows(asked, table)
     found = swap(peer_named, 1)
-    fetched = (own_named.astype(jnp.float32) + found.astype(jnp.float32)).astype(jnp.bfloat16)
 
     halves, bases = [], []
     for part, share in enumerate(PARTS):
         part_rows = row_count // share
         bases.append(sum(row_count // other for other in PARTS[:part]))
-        mine = row_gradients(asked, grads, peer_grads, bases[part], part_rows)
+        terms = (own_named, found) if part == SUM_PART else ()
+        mine, *sums = row_gradients(asked, grads, peer_grads, bases[part], part_rows, terms)
+        if sums:
+            fetched = sums[0]
         distance = 1
         other = lax.ppermute(mine, "dp", [(i, i ^ 1) for i in range(dp_count)])
         while 2 * distance < dp_count:
@@ -341,23 +374,21 @@
 
     returned = exchange(fetched.reshape(chip_count, bag_count, width))
 
-    accums, changes = [], []
+    accums, changes, new_table = [], [], []
     accum_lines = accum.reshape(-1, width)
     for part, (mine, other) in enumerate(halves):
         fresh_accum, delta = changes_of(mine, other, accum_lines, bases[part])
         accums.append(fresh_accum)
         peer_delta = swap(delta, 1)
-        changes = parity_changes(
-            slot_lines, peer_slot_lines, delta, peer_delta, bases[part],
-            parity_count, dp_count, chip_count, changes, part == len(PARTS) - 1,
+        new_table, *changes = parity_changes(
+            slot_lines, peer_slot_lines, delta, peer_delta, table, bases[part],
+            parity_count, dp_count, chip_count, changes, new_table, part == len(PARTS) - 1,
         )
-        if part < len(PARTS) - 1:
-            changes = [changes]
+        new_table = [new_table]
     arrived = [changes[0]]
     for k in range(1, chip_count):
         arrived.append(swap(changes[k], 2 * k))
     pooled = jnp.sum(returned.astype(jnp.float32), axis=0).astype(jnp.bfloat16)
-    new_table = finished_table(halves, accum_lines, table)
     new_accum = jnp.concatenate(accums, axis=0).reshape(row_count)
     part = sum(values.astype(jnp.float32) for values in arrived).astype(jnp.bfloat16)
     if dp_count == 2:
@@ -366,7 +397,7 @@
     else:
         parts = lax.all_gather(part, "dp", axis=0)
     new_parity = parity + parts.reshape(parity_count, width).astype(jnp.float32)
-    return (pooled, new_table, new_accum, new_parity)
+    return (pooled, new_table[0], new_accum, new_parity)
 
 
 def solution(mesh):

time: 122 us -> 121 us (level)
  waiting for transfers between devices: 34 us -> 37.7 us
  other arithmetic: 7.17 us -> 4.37 us
  Pallas kernels: 40 us -> 38.1 us
    pallas_call x3 -> x2, Pallas kernels: 17.1 us -> 12.9 us  [row_gradients(): pl.pallas_call(functools.partial(segment_kernel, base=base, count=count),...]
    ppermute x19, waiting for transfers between devices: 23.5 us -> 27.5 us  [swap(): lax.ppermute(values, 'table', [(i, i ^ distance) for i in range(table_cou...]
    convert_element_type x1 -> x0, other arithmetic: 2.8 us -> none  [on_device(): (own_named.astype(jnp.float32) + found.astype(jnp.float32)).astype(jnp.bf...]
    pallas_call x2, Pallas kernels: 7.1 us -> 8.45 us  [parity_changes(): pl.pallas_call(functools.partial(parity_kernel, base=base, holder_rows=ho...]
  transfers between devices with their start and end apart: 23 -> 23, of which waited for: 10 -> 12; matrix products, arithmetic and copies ran while one was open for 4% -> 1% of each run, Pallas kernels for 23% -> 22%
where the time goes in v7:
time: 121 us
  Pallas kernels  38.1 us (31%)
  waiting for transfers between devices  37.7 us (31%)
  starting transfers between devices  23.8 us (20%)
  blocking collectives  13.8 us (11%)
  other arithmetic  4.37 us (4%)
  local copies, waits for them, and re-layouts  1.92 us (2%)
    ppermute x19, waiting for transfers between devices, swap(): lax.ppermute(values, 'table', [(i, i ^ distance) for i in range(table_cou...  27.5 us
    ppermute x19, starting transfers between devices, swap(): lax.ppermute(values, 'table', [(i, i ^ distance) for i in range(table_cou...  15.7 us
    all_to_all x1, blocking collectives, on_device(): lax.all_to_all(requests, 'table', split_axis=0, concat_axis=0, tiled=True)  13.8 us
    pallas_call x2, Pallas kernels, row_gradients(): pl.pallas_call(functools.partial(segment_kernel, base=base, count=count),...  12.9 us
    pallas_call x1, Pallas kernels, named_rows(): pl.pallas_call(functools.partial(gather_kernel, together=2), in_specs=[VM...  11.5 us
    pallas_call x2, Pallas kernels, parity_changes(): pl.pallas_call(functools.partial(parity_kernel, base=base, holder_rows=ho...  8.45 us
    ppermute x2, waiting for transfers between devices, on_device(): other = lax.ppermute(mine, 'dp', [(i, i ^ 1) for i in range(dp_count)])  8.06 us
    pallas_call x2, Pallas kernels, changes_of(): pl.pallas_call(functools.partial(change_kernel, base=base), in_specs=[VME...  5.31 us
  transfers between devices with their start and end apart: 23, of which 12 were waited for; matrix products, arithmetic and copies ran while one was open for 1% of the time, Pallas kernels for 22%

profile of v7, /device:TPU:0, one launch (start us, length us, event | category | flops | bytes accessed | tf_op | source)
XLA Modules:
  0.0 120.6 jit_solution(16868328237071694136)
XLA Ops:
  1.6 13.8 %all_to_all.10.asked_ref = s32[16,1,512]{2,1,0:T(1,128)S(1)} all-to-all(s32[16,1,512]{2,1,0:T(1,128)S(1)} %reduce_max.12), channel_id=1, replica_groups=mesh['table'=16,'dp'=2] {'table'}, dimensions={0} | all-to-all | bytes 65536 | tf_op jit(solution)/shard_map/all_to_all | solution.py:344
  15.4 11.5 %shard_map.102 = (bf16[4096,128]{1,0:T(8,128)(2,1)}, bf16[4096,128]{1,0:T(8,128)(2,1)}) custom-call(s32[16,1,512]{2,1,0:T(1,128)S(1)} %all_to_all.10.asked_ref, f32[4096,128]{1,0:T(8,128)} %refs_4_.3), custom_call_target="tpu_custom_call" | custom-call | tf_op jit(solution)/shard_map/pallas_call | solution.py:177
  27.5 8.9 %collective-permute-done = bf16[512,128]{1,0:T(8,128)(2,1)S(1)} collective-permute-done((bf16[512,128]{1,0:T(8,128)(2,1)S(1)}, bf16[512,128]{1,0:T(8,128)(2,1)S(1)}, u32[]{:S(2)}, u32[]{:S(2)}) %collective-permute-start) | collective-permute-done | bytes 131104 | tf_op jit(solution)/shard_map/ppermute | solution.py:332
  37.0 2.9 %collective-permute-start.3 = (bf16[1024,128]{1,0:T(8,128)(2,1)S(1)}, bf16[1024,128]{1,0:T(8,128)(2,1)S(1)}, u32[]{:S(2)}, u32[]{:S(2)}) collective-permute-start(bf16[1024,128]{1,0:T(8,128)(2,1)S(1)} %constant_dynamic-update-slice_fusion.refs_0_), channel_id=1, source_target_pairs={{0,12},{2,14},{4,8},{6,10},{8,4},{10,6},{12,0},{14,2},{16,28},{18,... | collective-permute-start | bytes 786440 | tf_op jit(solution)/shard_map/ppermute | solution.py:332
  39.9 4.8 %collective-permute-done.1.refs_1_ = bf16[1024,128]{1,0:T(8,128)(2,1)S(1)} collective-permute-done((bf16[1024,128]{1,0:T(8,128)(2,1)S(1)}, bf16[1024,128]{1,0:T(8,128)(2,1)S(1)}, u32[]{:S(2)}, u32[]{:S(2)}) %collective-permute-start.1) | collective-permute-done | bytes 262176 | tf_op jit(solution)/shard_map/ppermute | solution.py:332
  46.2 5.3 %collective-permute-done.3.refs_3_ = bf16[1024,128]{1,0:T(8,128)(2,1)S(1)} collective-permute-done((bf16[1024,128]{1,0:T(8,128)(2,1)S(1)}, bf16[1024,128]{1,0:T(8,128)(2,1)S(1)}, u32[]{:S(2)}, u32[]{:S(2)}) %collective-permute-start.3) | collective-permute-done | bytes 262176 | tf_op jit(solution)/shard_map/ppermute | solution.py:332
  51.5 1.5 %collective-permute-done.7.refs_7_ = bf16[1024,128]{1,0:T(8,128)(2,1)S(1)} collective-permute-done((bf16[1024,128]{1,0:T(8,128)(2,1)S(1)}, bf16[1024,128]{1,0:T(8,128)(2,1)S(1)}, u32[]{:S(2)}, u32[]{:S(2)}) %collective-permute-start.7) | collective-permute-done | bytes 262176 | tf_op jit(solution)/shard_map/ppermute | solution.py:332
  53.0 4.9 %shard_map.105.own_ref = bf16[2048,128]{1,0:T(8,128)(2,1)S(1)} custom-call(s32[16,1,512]{2,1,0:T(1,128)S(1)} %all_to_all.10.asked_ref, bf16[1024,128]{1,0:T(8,128)(2,1)S(1)} %constant_dynamic-update-slice_fusion.refs_0_, bf16[1024,128]{1,0:T(8,128)(2,1)S(1)} %collective-permute-done.1.refs_1_, bf16[1024,128]{1,0:T(8,128)(2,1)S(1)} %collective-permute-done.2.refs_2_, ...), custom_call_target="tpu_custom_call" | custom-call | tf_op jit(solution)/shard_map/pallas_call | solution.py:129
  58.0 1.6 %collective-permute-start.12 = (bf16[2048,128]{1,0:T(8,128)(2,1)S(1)}, bf16[2048,128]{1,0:T(8,128)(2,1)}, u32[]{:S(2)}, u32[]{:S(2)}) collective-permute-start(bf16[2048,128]{1,0:T(8,128)(2,1)S(1)} %shard_map.105.own_ref), channel_id=1, source_target_pairs={{0,1},{1,0},{2,3},{3,2},{4,5},{5,4},{6,7},{7,6},{8,9},{9,8},{10,11... | collective-permute-start | bytes 1572872 | tf_op jit(solution)/shard_map/ppermute | solution.py:368
  59.5 8.0 %shard_map.103 = (bf16[2048,128]{1,0:T(8,128)(2,1)}, bf16[4096,128]{1,0:T(8,128)(2,1)}) custom-call(s32[16,1,512]{2,1,0:T(1,128)S(1)} %all_to_all.10.asked_ref, bf16[1024,128]{1,0:T(8,128)(2,1)S(1)} %constant_dynamic-update-slice_fusion.refs_0_, bf16[1024,128]{1,0:T(8,128)(2,1)S(1)} %collective-permute-done.1.refs_1_, ...), custom_call_target="tpu_custom_call" | custom-call | tf_op jit(solution)/shard_map/pallas_call | solution.py:129
  68.1 4.4 %all-to-all-start.1 = ((bf16[8,512,128]{2,1,0:T(8,128)(2,1)}), bf16[8,512,128]{2,1,0:T(8,128)(2,1)}, u32[]{:S(2)}, u32[]{:S(2)}) async-start(bf16[8,512,128]{2,1,0:T(8,128)(2,1)} %bitcast.13), calls=%async_computation.1 | async-start | bytes 2097152 | tf_op jit(solution)/shard_map/all_to_all | solution.py:335
  72.9 2.7 %shard_map.106 = (f32[16,128]{1,0:T(8,128)}, bf16[2048,128]{1,0:T(8,128)(2,1)S(1)}) custom-call(bf16[2048,128]{1,0:T(8,128)(2,1)S(1)} %shard_map.105.own_ref, bf16[2048,128]{1,0:T(8,128)(2,1)} %collective-permute-done.12.other_ref, f32[32,128]{1,0:T(8,128)S(1)} %bitcast.11), custom_call_target="tpu_custom_call" | custom-call | tf_op jit(solution)/shard_map/pallas_call | solution.py:222
  75.6 7.6 %collective-permute-done.10.other_ref = bf16[2048,128]{1,0:T(8,128)(2,1)S(1)} collective-permute-done((bf16[2048,128]{1,0:T(8,128)(2,1)}, bf16[2048,128]{1,0:T(8,128)(2,1)S(1)}, u32[]{:S(2)}, u32[]{:S(2)}) %collective-permute-start.10) | collective-permute-done | bytes 524320 | tf_op jit(solution)/shard_map/ppermute | solution.py:368
  85.1 2.7 %shard_map.104 = (f32[16,128]{1,0:T(8,128)}, bf16[2048,128]{1,0:T(8,128)(2,1)S(1)}) custom-call(bf16[2048,128]{1,0:T(8,128)(2,1)} %get-tuple-element.26.own_ref, bf16[2048,128]{1,0:T(8,128)(2,1)S(1)} %copy-done.1, f32[32,128]{1,0:T(8,128)S(1)} %bitcast.12), custom_call_target="tpu_custom_call" | custom-call | tf_op jit(solution)/shard_map/pallas_call | solution.py:222
  89.6 4.7 %shard_map.107 = (f32[4096,128]{1,0:T(8,128)}, f32[512,512]{1,0:T(8,128)}) custom-call(s32[8,512]{1,0:T(8,128)S(1)} %reshape.53.refs_0_, s32[8,512]{1,0:T(8,128)S(1)} %collective-permute-done.9.refs_1_, bf16[2048,128]{1,0:T(8,128)(2,1)S(1)} %get-tuple-element.28.refs_2_, bf16[2048,128]{1,0:T(8,128)(2,1)S(1)} %collective-permute-done.13.refs_3_, ...), custom_call_target="tpu_custom_call" | custom-call | tf_op jit(solution)/shard_map/pallas_call | solution.py:301
  94.4 3.7 %shard_map.108 = (f32[4096,128]{1,0:T(8,128)}, bf16[256,128]{1,0:T(8,128)(2,1)S(1)}, bf16[256,128]{1,0:T(8,128)(2,1)S(1)}, bf16[256,128]{1,0:T(8,128)(2,1)S(1)},...) custom-call(s32[8,512]{1,0:T(8,128)S(1)} %reshape.53.refs_0_, ...), custom_call_target="tpu_custom_call", output_to_operand_aliasing={{0}: (6, {})} | custom-call | tf_op jit(solution)/shard_map/pallas_call | solution.py:301
  98.4 3.6 %collective-permute-start.19 = (bf16[256,128]{1,0:T(8,128)(2,1)S(1)}, bf16[256,128]{1,0:T(8,128)(2,1)S(1)}, u32[]{:S(2)}, u32[]{:S(2)}) collective-permute-start(bf16[256,128]{1,0:T(8,128)(2,1)S(1)} %get-tuple-element.40), channel_id=1, source_target_pairs={{0,24},{2,26},{4,28},{6,30},{8,16},{10,18},{12,20},{14,22},{16,8},... | collective-permute-start | bytes 196616 | tf_op jit(solution)/shard_map/ppermute | solution.py:332
  102.0 3.9 %collective-permute-start.17 = (bf16[256,128]{1,0:T(8,128)(2,1)S(1)}, bf16[256,128]{1,0:T(8,128)(2,1)S(1)}, u32[]{:S(2)}, u32[]{:S(2)}) collective-permute-start(bf16[256,128]{1,0:T(8,128)(2,1)S(1)} %get-tuple-element.38), channel_id=1, source_target_pairs={{0,16},{2,18},{4,20},{6,22},{8,24},{10,26},{12,28},{14,30},{16,0},... | collective-permute-start | bytes 196616 | tf_op jit(solution)/shard_map/ppermute | solution.py:332
  106.0 1.8 %collective-permute-start.15 = (bf16[256,128]{1,0:T(8,128)(2,1)S(1)}, bf16[256,128]{1,0:T(8,128)(2,1)S(1)}, u32[]{:S(2)}, u32[]{:S(2)}) collective-permute-start(bf16[256,128]{1,0:T(8,128)(2,1)S(1)} %get-tuple-element.36), channel_id=1, source_target_pairs={{0,8},{2,10},{4,12},{6,14},{8,0},{10,2},{12,4},{14,6},{16,24},{18,... | collective-permute-start | bytes 196616 | tf_op jit(solution)/shard_map/ppermute | solution.py:332
  107.8 1.6 %collective-permute-start.14 = (bf16[256,128]{1,0:T(8,128)(2,1)S(1)}, bf16[256,128]{1,0:T(8,128)(2,1)S(1)}, u32[]{:S(2)}, u32[]{:S(2)}) collective-permute-start(bf16[256,128]{1,0:T(8,128)(2,1)S(1)} %get-tuple-element.35), channel_id=1, source_target_pairs={{0,4},{2,6},{4,0},{6,2},{8,12},{10,14},{12,8},{14,10},{16,20},{18,... | collective-permute-start | bytes 196616 | tf_op jit(solution)/shard_map/ppermute | solution.py:332
  109.4 2.8 %collective-permute-done.18 = bf16[256,128]{1,0:T(8,128)(2,1)S(1)} collective-permute-done((bf16[256,128]{1,0:T(8,128)(2,1)S(1)}, bf16[256,128]{1,0:T(8,128)(2,1)S(1)}, u32[]{:S(2)}, u32[]{:S(2)}) %collective-permute-start.18) | collective-permute-done | bytes 65568 | tf_op jit(solution)/shard_map/ppermute | solution.py:332
  113.5 1.6 %collective-permute-start.21 = (bf16[256,128]{1,0:T(8,128)(2,1)S(1)}, bf16[256,128]{1,0:T(8,128)(2,1)S(1)}, u32[]{:S(2)}, u32[]{:S(2)}) collective-permute-start(bf16[256,128]{1,0:T(8,128)(2,1)S(1)} %add_convert_fusion), channel_id=1, source_target_pairs={{0,1},{1,0},{2,3},{3,2},{4,5},{5,4},{6,7},{7,6},{8,9},{9,8},{10,11... | collective-permute-start | bytes 196616 | tf_op jit(solution)/shard_map/ppermute | solution.py:395
  115.6 2.2 %collective-permute-done.21 = bf16[256,128]{1,0:T(8,128)(2,1)S(1)} collective-permute-done((bf16[256,128]{1,0:T(8,128)(2,1)S(1)}, bf16[256,128]{1,0:T(8,128)(2,1)S(1)}, u32[]{:S(2)}, u32[]{:S(2)}) %collective-permute-start.21) | collective-permute-done | bytes 65568 | tf_op jit(solution)/shard_map/ppermute | solution.py:395
  118.5 2.1 %reduce_sum.12 = bf16[512,128]{1,0:T(8,128)(2,1)} reduce(bf16[8,512,128]{2,1,0:T(8,128)(2,1)} %all-to-all-done.1, bf16[]{:T(256)} %constant.3.clone.1), dimensions={0}, to_apply=%region_1.2 | reduce | flops 458752 | bytes 1179650 | tf_op jit(solution)/shard_map/reduce_sum | solution.py:391
  (56 shorter events, 11.4 us)
Async XLA Ops:
  0.6 26.3 %copy-start.4 = (bf16[512,128]{1,0:T(8,128)(2,1)S(1)}, bf16[512,128]{1,0:T(8,128)(2,1)}, u32[]{:S(2)}) copy-start(bf16[512,128]{1,0:T(8,128)(2,1)} %param.9) | copy-start | bytes 393220
  26.9 32.6 %collective-permute-start.8 = (bf16[4096,128]{1,0:T(8,128)(2,1)}, bf16[4096,128]{1,0:T(8,128)(2,1)}, u32[]{:S(2)}, u32[]{:S(2)}) collective-permute-start(bf16[4096,128]{1,0:T(8,128)(2,1)} %get-tuple-element.24), channel_id=1, source_target_pairs={{0,2},{2,0},{4,6},{6,4},{8,10},{10,8},{12,14},{14,12},{16,18},{18,... | collective-permute-start | bytes 3145736 | tf_op jit(solution)/shard_map/ppermute | solution.py:332
  27.0 9.4 %collective-permute-start = (bf16[512,128]{1,0:T(8,128)(2,1)S(1)}, bf16[512,128]{1,0:T(8,128)(2,1)S(1)}, u32[]{:S(2)}, u32[]{:S(2)}) collective-permute-start(bf16[512,128]{1,0:T(8,128)(2,1)S(1)} %copy-done.4), channel_id=1, source_target_pairs={{0,16},{2,18},{4,20},{6,22},{8,24},{10,26},{12,28},{14,30},{16,0},... | collective-permute-start | bytes 393224 | tf_op jit(solution)/shard_map/ppermute | solution.py:332
  36.4 8.3 %collective-permute-start.1 = (bf16[1024,128]{1,0:T(8,128)(2,1)S(1)}, bf16[1024,128]{1,0:T(8,128)(2,1)S(1)}, u32[]{:S(2)}, u32[]{:S(2)}) collective-permute-start(bf16[1024,128]{1,0:T(8,128)(2,1)S(1)} %constant_dynamic-update-slice_fusion.refs_0_), channel_id=1, source_target_pairs={{0,4},{2,6},{4,0},{6,2},{8,12},{10,14},{12,8},{14,10},{16,20},{18,... | collective-permute-start | bytes 786440 | tf_op jit(solution)/shard_map/ppermute | solution.py:332
  37.0 9.2 %collective-permute-start.2 = (bf16[1024,128]{1,0:T(8,128)(2,1)S(1)}, bf16[1024,128]{1,0:T(8,128)(2,1)S(1)}, u32[]{:S(2)}, u32[]{:S(2)}) collective-permute-start(bf16[1024,128]{1,0:T(8,128)(2,1)S(1)} %constant_dynamic-update-slice_fusion.refs_0_), channel_id=1, source_target_pairs={{0,8},{2,10},{4,12},{6,14},{8,0},{10,2},{12,4},{14,6},{16,24},{18,... | collective-permute-start | bytes 786440 | tf_op jit(solution)/shard_map/ppermute | solution.py:332
  37.0 14.5 %collective-permute-start.3 = (bf16[1024,128]{1,0:T(8,128)(2,1)S(1)}, bf16[1024,128]{1,0:T(8,128)(2,1)S(1)}, u32[]{:S(2)}, u32[]{:S(2)}) collective-permute-start(bf16[1024,128]{1,0:T(8,128)(2,1)S(1)} %constant_dynamic-update-slice_fusion.refs_0_), channel_id=1, source_target_pairs={{0,12},{2,14},{4,8},{6,10},{8,4},{10,6},{12,0},{14,2},{16,28},{18,... | collective-permute-start | bytes 786440 | tf_op jit(solution)/shard_map/ppermute | solution.py:332
  39.9 11.6 %collective-permute-start.4 = (bf16[1024,128]{1,0:T(8,128)(2,1)S(1)}, bf16[1024,128]{1,0:T(8,128)(2,1)S(1)}, u32[]{:S(2)}, u32[]{:S(2)}) collective-permute-start(bf16[1024,128]{1,0:T(8,128)(2,1)S(1)} %constant_dynamic-update-slice_fusion.refs_0_), channel_id=1, source_target_pairs={{0,2},{2,0},{4,6},{6,4},{8,10},{10,8},{12,14},{14,12},{16,18},{18,... | collective-permute-start | bytes 786440 | tf_op jit(solution)/shard_map/ppermute | solution.py:332
  44.7 6.8 %collective-permute-start.5 = (bf16[1024,128]{1,0:T(8,128)(2,1)S(1)}, bf16[1024,128]{1,0:T(8,128)(2,1)S(1)}, u32[]{:S(2)}, u32[]{:S(2)}) collective-permute-start(bf16[1024,128]{1,0:T(8,128)(2,1)S(1)} %collective-permute-done.1.refs_1_), channel_id=1, source_target_pairs={{0,2},{2,0},{4,6},{6,4},{8,10},{10,8},{12,14},{14,12},{16,18},{18,... | collective-permute-start | bytes 786440 | tf_op jit(solution)/shard_map/ppermute | solution.py:332
  46.2 5.3 %collective-permute-start.6 = (bf16[1024,128]{1,0:T(8,128)(2,1)S(1)}, bf16[1024,128]{1,0:T(8,128)(2,1)S(1)}, u32[]{:S(2)}, u32[]{:S(2)}) collective-permute-start(bf16[1024,128]{1,0:T(8,128)(2,1)S(1)} %collective-permute-done.2.refs_2_), channel_id=1, source_target_pairs={{0,2},{2,0},{4,6},{6,4},{8,10},{10,8},{12,14},{14,12},{16,18},{18,... | collective-permute-start | bytes 786440 | tf_op jit(solution)/shard_map/ppermute | solution.py:332
  51.5 1.5 %collective-permute-start.7 = (bf16[1024,128]{1,0:T(8,128)(2,1)S(1)}, bf16[1024,128]{1,0:T(8,128)(2,1)S(1)}, u32[]{:S(2)}, u32[]{:S(2)}) collective-permute-start(bf16[1024,128]{1,0:T(8,128)(2,1)S(1)} %collective-permute-done.3.refs_3_), channel_id=1, source_target_pairs={{0,2},{2,0},{4,6},{6,4},{8,10},{10,8},{12,14},{14,12},{16,18},{18,... | collective-permute-start | bytes 786440 | tf_op jit(solution)/shard_map/ppermute | solution.py:332
  58.0 15.0 %collective-permute-start.12 = (bf16[2048,128]{1,0:T(8,128)(2,1)S(1)}, bf16[2048,128]{1,0:T(8,128)(2,1)}, u32[]{:S(2)}, u32[]{:S(2)}) collective-permute-start(bf16[2048,128]{1,0:T(8,128)(2,1)S(1)} %shard_map.105.own_ref), channel_id=1, source_target_pairs={{0,1},{1,0},{2,3},{3,2},{4,5},{5,4},{6,7},{7,6},{8,9},{9,8},{10,11... | collective-permute-start | bytes 1572872 | tf_op jit(solution)/shard_map/ppermute | solution.py:368
  67.5 15.7 %collective-permute-start.10 = (bf16[2048,128]{1,0:T(8,128)(2,1)}, bf16[2048,128]{1,0:T(8,128)(2,1)S(1)}, u32[]{:S(2)}, u32[]{:S(2)}) collective-permute-start(bf16[2048,128]{1,0:T(8,128)(2,1)} %get-tuple-element.26.own_ref), channel_id=1, source_target_pairs={{0,1},{1,0},{2,3},{3,2},{4,5},{5,4},{6,7},{7,6},{8,9},{9,8},{10,11... | collective-permute-start | bytes 1572872 | tf_op jit(solution)/shard_map/ppermute | solution.py:368
  68.1 50.4 %all-to-all-start.1 = ((bf16[8,512,128]{2,1,0:T(8,128)(2,1)}), bf16[8,512,128]{2,1,0:T(8,128)(2,1)}, u32[]{:S(2)}, u32[]{:S(2)}) async-start(bf16[8,512,128]{2,1,0:T(8,128)(2,1)} %bitcast.13), calls=%async_computation.1 | async-start | bytes 2097152 | tf_op jit(solution)/shard_map/all_to_all | solution.py:335
  75.6 14.1 %collective-permute-start.13 = (bf16[2048,128]{1,0:T(8,128)(2,1)S(1)}, bf16[2048,128]{1,0:T(8,128)(2,1)S(1)}, u32[]{:S(2)}, u32[]{:S(2)}) collective-permute-start(bf16[2048,128]{1,0:T(8,128)(2,1)S(1)} %get-tuple-element.28.refs_2_), channel_id=1, source_target_pairs={{0,2},{2,0},{4,6},{6,4},{8,10},{10,8},{12,14},{14,12},{16,18},{18,... | collective-permute-start | bytes 1572872 | tf_op jit(solution)/shard_map/ppermute | solution.py:332
  87.7 6.7 %collective-permute-start.11 = (bf16[2048,128]{1,0:T(8,128)(2,1)S(1)}, bf16[2048,128]{1,0:T(8,128)(2,1)S(1)}, u32[]{:S(2)}, u32[]{:S(2)}) collective-permute-start(bf16[2048,128]{1,0:T(8,128)(2,1)S(1)} %get-tuple-element.27.refs_2_), channel_id=1, source_target_pairs={{0,2},{2,0},{4,6},{6,4},{8,10},{10,8},{12,14},{14,12},{16,18},{18,... | collective-permute-start | bytes 1572872 | tf_op jit(solution)/shard_map/ppermute | solution.py:332
  87.7 1.9 %collective-permute-start.9 = (s32[8,512]{1,0:T(8,128)S(1)}, s32[8,512]{1,0:T(8,128)S(1)}, u32[]{:S(2)}, u32[]{:S(2)}) collective-permute-start(s32[8,512]{1,0:T(8,128)S(1)} %reshape.53.refs_0_), channel_id=1, source_target_pairs={{0,2},{2,0},{4,6},{6,4},{8,10},{10,8},{12,14},{14,12},{16,18},{18,... | collective-permute-start | bytes 49160 | tf_op jit(solution)/shard_map/ppermute | solution.py:332
  98.2 7.8 %collective-permute-start.20 = (bf16[256,128]{1,0:T(8,128)(2,1)S(1)}, bf16[256,128]{1,0:T(8,128)(2,1)S(1)}, u32[]{:S(2)}, u32[]{:S(2)}) collective-permute-start(bf16[256,128]{1,0:T(8,128)(2,1)S(1)} %get-tuple-element.41), channel_id=1, source_target_pairs={{0,28},{2,30},{4,24},{6,26},{8,20},{10,22},{12,16},{14,18},{16,12}... | collective-permute-start | bytes 196616 | tf_op jit(solution)/shard_map/ppermute | solution.py:332
  98.4 9.4 %collective-permute-start.19 = (bf16[256,128]{1,0:T(8,128)(2,1)S(1)}, bf16[256,128]{1,0:T(8,128)(2,1)S(1)}, u32[]{:S(2)}, u32[]{:S(2)}) collective-permute-start(bf16[256,128]{1,0:T(8,128)(2,1)S(1)} %get-tuple-element.40), channel_id=1, source_target_pairs={{0,24},{2,26},{4,28},{6,30},{8,16},{10,18},{12,20},{14,22},{16,8},... | collective-permute-start | bytes 196616 | tf_op jit(solution)/shard_map/ppermute | solution.py:332
  102.0 10.2 %collective-permute-start.18 = (bf16[256,128]{1,0:T(8,128)(2,1)S(1)}, bf16[256,128]{1,0:T(8,128)(2,1)S(1)}, u32[]{:S(2)}, u32[]{:S(2)}) collective-permute-start(bf16[256,128]{1,0:T(8,128)(2,1)S(1)} %get-tuple-element.39), channel_id=1, source_target_pairs={{0,20},{2,22},{4,16},{6,18},{8,28},{10,30},{12,24},{14,26},{16,4},... | collective-permute-start | bytes 196616 | tf_op jit(solution)/shard_map/ppermute | solution.py:332
  102.0 10.2 %collective-permute-start.17 = (bf16[256,128]{1,0:T(8,128)(2,1)S(1)}, bf16[256,128]{1,0:T(8,128)(2,1)S(1)}, u32[]{:S(2)}, u32[]{:S(2)}) collective-permute-start(bf16[256,128]{1,0:T(8,128)(2,1)S(1)} %get-tuple-element.38), channel_id=1, source_target_pairs={{0,16},{2,18},{4,20},{6,22},{8,24},{10,26},{12,28},{14,30},{16,0},... | collective-permute-start | bytes 196616 | tf_op jit(solution)/shard_map/ppermute | solution.py:332
  105.9 7.5 %collective-permute-start.16 = (bf16[256,128]{1,0:T(8,128)(2,1)S(1)}, bf16[256,128]{1,0:T(8,128)(2,1)S(1)}, u32[]{:S(2)}, u32[]{:S(2)}) collective-permute-start(bf16[256,128]{1,0:T(8,128)(2,1)S(1)} %get-tuple-element.37), channel_id=1, source_target_pairs={{0,12},{2,14},{4,8},{6,10},{8,4},{10,6},{12,0},{14,2},{16,28},{18,... | collective-permute-start | bytes 196616 | tf_op jit(solution)/shard_map/ppermute | solution.py:332
  106.0 7.4 %collective-permute-start.15 = (bf16[256,128]{1,0:T(8,128)(2,1)S(1)}, bf16[256,128]{1,0:T(8,128)(2,1)S(1)}, u32[]{:S(2)}, u32[]{:S(2)}) collective-permute-start(bf16[256,128]{1,0:T(8,128)(2,1)S(1)} %get-tuple-element.36), channel_id=1, source_target_pairs={{0,8},{2,10},{4,12},{6,14},{8,0},{10,2},{12,4},{14,6},{16,24},{18,... | collective-permute-start | bytes 196616 | tf_op jit(solution)/shard_map/ppermute | solution.py:332
  107.8 5.6 %collective-permute-start.14 = (bf16[256,128]{1,0:T(8,128)(2,1)S(1)}, bf16[256,128]{1,0:T(8,128)(2,1)S(1)}, u32[]{:S(2)}, u32[]{:S(2)}) collective-permute-start(bf16[256,128]{1,0:T(8,128)(2,1)S(1)} %get-tuple-element.35), channel_id=1, source_target_pairs={{0,4},{2,6},{4,0},{6,2},{8,12},{10,14},{12,8},{14,10},{16,20},{18,... | collective-permute-start | bytes 196616 | tf_op jit(solution)/shard_map/ppermute | solution.py:332
  113.5 4.3 %collective-permute-start.21 = (bf16[256,128]{1,0:T(8,128)(2,1)S(1)}, bf16[256,128]{1,0:T(8,128)(2,1)S(1)}, u32[]{:S(2)}, u32[]{:S(2)}) collective-permute-start(bf16[256,128]{1,0:T(8,128)(2,1)S(1)} %add_convert_fusion), channel_id=1, source_target_pairs={{0,1},{1,0},{2,3},{3,2},{4,5},{5,4},{6,7},{7,6},{8,9},{9,8},{10,11... | collective-permute-start | bytes 196616 | tf_op jit(solution)/shard_map/ppermute | solution.py:395
  (7 other events, 91.5 us)

commit v8 on v7

--- a/solution.py
+++ b/solution.py
@@ -10,6 +10,7 @@
 EPSILON = 1e-06
 SPLIT = 4
 PARTS = (2, 2)
+GRANT = pltpu.CompilerParams(vmem_limit_bytes=56 << 20)
 SUM_PART = 1
 NEAR_BYTES = 1 << 21
 VMEM = pl.BlockSpec(memory_space=pltpu.VMEM)
@@ -114,7 +115,7 @@
     width = grads[0].shape[1]
     count = len(grads)
     split = SPLIT if row_count > 4 * 256 else SPLIT // 2
-    anywhere = pl.BlockSpec(memory_space=pl.ANY)
+    anywhere = pl.BlockSpec(memory_space=pltpu.HBM)
     out_shape = [pltpu.VMEM((row_count, width), jnp.bfloat16)]
     scratch_shapes = [pltpu.VMEM((row_count // split, split * width), jnp.float32)]
     if terms:
@@ -128,6 +129,7 @@
         ]
     return pl.pallas_call(
         functools.partial(segment_kernel, base=base, count=count),
+        compiler_params=GRANT,
         in_specs=[VMEM] * (1 + 2 * count) + [anywhere] * len(terms),
         out_specs=[VMEM] + [anywhere] * (1 if terms else 0),
         out_shape=out_shape,
@@ -176,7 +178,8 @@
     rows = jax.ShapeDtypeStruct((sources // 2 * bags, width), jnp.bfloat16)
     return pl.pallas_call(
         functools.partial(gather_kernel, together=2),
-        in_specs=[VMEM, pl.BlockSpec(memory_space=pl.ANY)],
+        compiler_params=GRANT,
+        in_specs=[VMEM, pl.BlockSpec(memory_space=pltpu.HBM)],
         out_specs=[VMEM, VMEM],
         out_shape=[rows, rows],
         scratch_shapes=[
@@ -221,6 +224,7 @@
     rows, width = own.shape
     return pl.pallas_call(
         functools.partial(change_kernel, base=base),
+        compiler_params=GRANT,
         in_specs=[VMEM] * 3,
         out_specs=[VMEM, VMEM],
         out_shape=[
@@ -293,7 +297,7 @@
     part_count = holder_rows // dp_count
     segment_count = chip_count * part_count
     held = pltpu.VMEM((segment_count // SPLIT, SPLIT * width), jnp.float32)
-    anywhere = pl.BlockSpec(memory_space=pl.ANY)
+    anywhere = pl.BlockSpec(memory_space=pltpu.HBM)
     tile = min(1024, rows)
     changes = [pltpu.VMEM((part_count, width), jnp.bfloat16)] * chip_count
     if not last:
@@ -302,6 +306,7 @@
         functools.partial(
             parity_kernel, base=base, holder_rows=holder_rows, dp_count=dp_count, tile=tile, last=last
         ),
+        compiler_params=GRANT,
         in_specs=[VMEM] * 4 + [anywhere] * (1 + len(start) + len(new_table)),
         out_specs=[anywhere] + [VMEM] * len(changes),
         out_shape=[jax.ShapeDtypeStruct(table.shape, jnp.float32)] + changes,

time: 121 us -> 119 us (0.983)
  Pallas kernels: 38.1 us -> 35.2 us
  starting transfers between devices: 23.8 us -> 25.1 us
    pallas_call x3, Pallas kernels: 16.8 us -> 14.7 us  [the longest x1 11.5 us: named_rows(): pl.pallas_call(functools.partial(gather_kernel, together=2), compiler_par...]
    ppermute x19, starting transfers between devices: 15.7 us -> 17 us  [swap(): lax.ppermute(values, 'table', [(i, i ^ distance) for i in range(table_cou...]
  transfers between devices with their start and end apart: 23 -> 23, of which waited for: 12 -> 14; matrix products, arithmetic and copies ran while one was open for 1% -> 1% of each run, Pallas kernels for 22% -> 20%
where the time goes in v8:
time: 119 us
  waiting for transfers between devices  38.2 us (32%)
  Pallas kernels  35.2 us (30%)
  starting transfers between devices  25.1 us (21%)
  blocking collectives  13.8 us (12%)
  other arithmetic  4.37 us (4%)
    ppermute x19, waiting for transfers between devices, swap(): lax.ppermute(values, 'table', [(i, i ^ distance) for i in range(table_cou...  27.1 us
    ppermute x19, starting transfers between devices, swap(): lax.ppermute(values, 'table', [(i, i ^ distance) for i in range(table_cou...  17 us
    all_to_all x1, blocking collectives, on_device(): lax.all_to_all(requests, 'table', split_axis=0, concat_axis=0, tiled=True)  13.8 us
    pallas_call x2, Pallas kernels, row_gradients(): pl.pallas_call(functools.partial(segment_kernel, base=base, count=count),...  12.1 us
    pallas_call x1, Pallas kernels, named_rows(): pl.pallas_call(functools.partial(gather_kernel, together=2), compiler_par...  11.5 us
    ppermute x2, waiting for transfers between devices, on_device(): other = lax.ppermute(mine, 'dp', [(i, i ^ 1) for i in range(dp_count)])  8.93 us
    pallas_call x2, Pallas kernels, parity_changes(): pl.pallas_call(functools.partial(parity_kernel, base=base, holder_rows=ho...  8.46 us
    all_to_all x1, starting transfers between devices, exchange(): lax.all_to_all(values, 'table', split_axis=0, concat_axis=0, axis_index_g...  4.37 us
  transfers between devices with their start and end apart: 23, of which 14 were waited for; matrix products, arithmetic and copies ran while one was open for 1% of the time, Pallas kernels for 20%

profile of v8, /device:TPU:0, one launch (start us, length us, event | category | flops | bytes accessed | tf_op | source)
XLA Modules:
  0.0 118.7 jit_solution(18352749806483161476)
XLA Ops:
  1.6 13.8 %all_to_all.10.asked_ref = s32[16,1,512]{2,1,0:T(1,128)S(1)} all-to-all(s32[16,1,512]{2,1,0:T(1,128)S(1)} %reduce_max.12), channel_id=1, replica_groups=mesh['table'=16,'dp'=2] {'table'}, dimensions={0} | all-to-all | bytes 65536 | tf_op jit(solution)/shard_map/all_to_all | solution.py:349
  15.4 11.5 %shard_map.102 = (bf16[4096,128]{1,0:T(8,128)(2,1)}, bf16[4096,128]{1,0:T(8,128)(2,1)}) custom-call(s32[16,1,512]{2,1,0:T(1,128)S(1)} %all_to_all.10.asked_ref, f32[4096,128]{1,0:T(8,128)} %refs_4_.3), custom_call_target="tpu_custom_call" | custom-call | tf_op jit(solution)/shard_map/pallas_call | solution.py:179
  27.5 8.9 %collective-permute-done = bf16[512,128]{1,0:T(8,128)(2,1)S(1)} collective-permute-done((bf16[512,128]{1,0:T(8,128)(2,1)S(1)}, bf16[512,128]{1,0:T(8,128)(2,1)S(1)}, u32[]{:S(2)}, u32[]{:S(2)}) %collective-permute-start) | collective-permute-done | bytes 131104 | tf_op jit(solution)/shard_map/ppermute | solution.py:337
  37.0 2.9 %collective-permute-start.3 = (bf16[1024,128]{1,0:T(8,128)(2,1)S(1)}, bf16[1024,128]{1,0:T(8,128)(2,1)S(1)}, u32[]{:S(2)}, u32[]{:S(2)}) collective-permute-start(bf16[1024,128]{1,0:T(8,128)(2,1)S(1)} %constant_dynamic-update-slice_fusion.refs_0_), channel_id=1, source_target_pairs={{0,12},{2,14},{4,8},{6,10},{8,4},{10,6},{12,0},{14,2},{16,28},{18,... | collective-permute-start | bytes 786440 | tf_op jit(solution)/shard_map/ppermute | solution.py:337
  39.9 4.8 %collective-permute-done.1.refs_1_ = bf16[1024,128]{1,0:T(8,128)(2,1)S(1)} collective-permute-done((bf16[1024,128]{1,0:T(8,128)(2,1)S(1)}, bf16[1024,128]{1,0:T(8,128)(2,1)S(1)}, u32[]{:S(2)}, u32[]{:S(2)}) %collective-permute-start.1) | collective-permute-done | bytes 262176 | tf_op jit(solution)/shard_map/ppermute | solution.py:337
  44.7 1.5 %collective-permute-done.2.refs_2_ = bf16[1024,128]{1,0:T(8,128)(2,1)S(1)} collective-permute-done((bf16[1024,128]{1,0:T(8,128)(2,1)S(1)}, bf16[1024,128]{1,0:T(8,128)(2,1)S(1)}, u32[]{:S(2)}, u32[]{:S(2)}) %collective-permute-start.2) | collective-permute-done | bytes 262176 | tf_op jit(solution)/shard_map/ppermute | solution.py:337
  46.2 5.3 %collective-permute-done.3.refs_3_ = bf16[1024,128]{1,0:T(8,128)(2,1)S(1)} collective-permute-done((bf16[1024,128]{1,0:T(8,128)(2,1)S(1)}, bf16[1024,128]{1,0:T(8,128)(2,1)S(1)}, u32[]{:S(2)}, u32[]{:S(2)}) %collective-permute-start.3) | collective-permute-done | bytes 262176 | tf_op jit(solution)/shard_map/ppermute | solution.py:337
  51.5 1.5 %collective-permute-done.7.refs_7_ = bf16[1024,128]{1,0:T(8,128)(2,1)S(1)} collective-permute-done((bf16[1024,128]{1,0:T(8,128)(2,1)S(1)}, bf16[1024,128]{1,0:T(8,128)(2,1)S(1)}, u32[]{:S(2)}, u32[]{:S(2)}) %collective-permute-start.7) | collective-permute-done | bytes 262176 | tf_op jit(solution)/shard_map/ppermute | solution.py:337
  53.0 4.9 %shard_map.105.own_ref = bf16[2048,128]{1,0:T(8,128)(2,1)S(1)} custom-call(s32[16,1,512]{2,1,0:T(1,128)S(1)} %all_to_all.10.asked_ref, bf16[1024,128]{1,0:T(8,128)(2,1)S(1)} %constant_dynamic-update-slice_fusion.refs_0_, bf16[1024,128]{1,0:T(8,128)(2,1)S(1)} %collective-permute-done.1.refs_1_, bf16[1024,128]{1,0:T(8,128)(2,1)S(1)} %collective-permute-done.2.refs_2_, ...), custom_call_target="tpu_custom_call" | custom-call | tf_op jit(solution)/shard_map/pallas_call | solution.py:130
  58.0 1.6 %collective-permute-start.12 = (bf16[2048,128]{1,0:T(8,128)(2,1)S(1)}, bf16[2048,128]{1,0:T(8,128)(2,1)S(1)}, u32[]{:S(2)}, u32[]{:S(2)}) collective-permute-start(bf16[2048,128]{1,0:T(8,128)(2,1)S(1)} %shard_map.105.own_ref), channel_id=1, source_target_pairs={{0,1},{1,0},{2,3},{3,2},{4,5},{5,4},{6,7},{7,6},{8,9},{9,8},{10,11... | collective-permute-start | bytes 1572872 | tf_op jit(solution)/shard_map/ppermute | solution.py:373
  60.5 7.2 %shard_map.103 = (bf16[2048,128]{1,0:T(8,128)(2,1)S(1)}, bf16[4096,128]{1,0:T(8,128)(2,1)}) custom-call(s32[16,1,512]{2,1,0:T(1,128)S(1)} %all_to_all.10.asked_ref, bf16[1024,128]{1,0:T(8,128)(2,1)S(1)} %constant_dynamic-update-slice_fusion.refs_0_, bf16[1024,128]{1,0:T(8,128)(2,1)S(1)} %collective-permute-done.1.refs_1_, ...), custom_call_target="tpu_custom_call" | custom-call | tf_op jit(solution)/shard_map/pallas_call | solution.py:130
  68.3 4.4 %all-to-all-start.1 = ((bf16[8,512,128]{2,1,0:T(8,128)(2,1)}), bf16[8,512,128]{2,1,0:T(8,128)(2,1)}, u32[]{:S(2)}, u32[]{:S(2)}) async-start(bf16[8,512,128]{2,1,0:T(8,128)(2,1)} %bitcast.13), calls=%async_computation.1 | async-start | bytes 2097152 | tf_op jit(solution)/shard_map/all_to_all | solution.py:340
  72.8 1.6 %shard_map.106 = (f32[16,128]{1,0:T(8,128)}, bf16[2048,128]{1,0:T(8,128)(2,1)S(1)}) custom-call(bf16[2048,128]{1,0:T(8,128)(2,1)S(1)} %shard_map.105.own_ref, bf16[2048,128]{1,0:T(8,128)(2,1)S(1)} %collective-permute-done.12.other_ref, f32[32,128]{1,0:T(8,128)S(1)} %bitcast.11), custom_call_target="tpu_custom_call" | custom-call | tf_op jit(solution)/shard_map/pallas_call | solution.py:225
  74.4 8.8 %collective-permute-done.10.other_ref = bf16[2048,128]{1,0:T(8,128)(2,1)S(1)} collective-permute-done((bf16[2048,128]{1,0:T(8,128)(2,1)S(1)}, bf16[2048,128]{1,0:T(8,128)(2,1)S(1)}, u32[]{:S(2)}, u32[]{:S(2)}) %collective-permute-start.10) | collective-permute-done | bytes 524320 | tf_op jit(solution)/shard_map/ppermute | solution.py:373
  83.2 1.6 %shard_map.104 = (f32[16,128]{1,0:T(8,128)}, bf16[2048,128]{1,0:T(8,128)(2,1)S(1)}) custom-call(bf16[2048,128]{1,0:T(8,128)(2,1)S(1)} %get-tuple-element.26.own_ref, bf16[2048,128]{1,0:T(8,128)(2,1)S(1)} %collective-permute-done.10.other_ref, f32[32,128]{1,0:T(8,128)S(1)} %bitcast.12), custom_call_target="tpu_custom_call" | custom-call | tf_op jit(solution)/shard_map/pallas_call | solution.py:225
  86.8 4.7 %shard_map.107 = (f32[4096,128]{1,0:T(8,128)}, f32[512,512]{1,0:T(8,128)}) custom-call(s32[8,512]{1,0:T(8,128)S(1)} %reshape.53.refs_0_, s32[8,512]{1,0:T(8,128)S(1)} %collective-permute-done.9.refs_1_, bf16[2048,128]{1,0:T(8,128)(2,1)S(1)} %get-tuple-element.28.refs_2_, bf16[2048,128]{1,0:T(8,128)(2,1)S(1)} %collective-permute-done.13.refs_3_, ...), custom_call_target="tpu_custom_call" | custom-call | tf_op jit(solution)/shard_map/pallas_call | solution.py:305
  91.5 3.7 %shard_map.108 = (f32[4096,128]{1,0:T(8,128)}, bf16[256,128]{1,0:T(8,128)(2,1)S(1)}, bf16[256,128]{1,0:T(8,128)(2,1)S(1)}, bf16[256,128]{1,0:T(8,128)(2,1)S(1)},...) custom-call(s32[8,512]{1,0:T(8,128)S(1)} %reshape.53.refs_0_, ...), custom_call_target="tpu_custom_call", output_to_operand_aliasing={{0}: (6, {})} | custom-call | tf_op jit(solution)/shard_map/pallas_call | solution.py:305
  95.5 3.6 %collective-permute-start.19 = (bf16[256,128]{1,0:T(8,128)(2,1)S(1)}, bf16[256,128]{1,0:T(8,128)(2,1)S(1)}, u32[]{:S(2)}, u32[]{:S(2)}) collective-permute-start(bf16[256,128]{1,0:T(8,128)(2,1)S(1)} %get-tuple-element.40), channel_id=1, source_target_pairs={{0,24},{2,26},{4,28},{6,30},{8,16},{10,18},{12,20},{14,22},{16,8},... | collective-permute-start | bytes 196616 | tf_op jit(solution)/shard_map/ppermute | solution.py:337
  99.1 3.9 %collective-permute-start.17 = (bf16[256,128]{1,0:T(8,128)(2,1)S(1)}, bf16[256,128]{1,0:T(8,128)(2,1)S(1)}, u32[]{:S(2)}, u32[]{:S(2)}) collective-permute-start(bf16[256,128]{1,0:T(8,128)(2,1)S(1)} %get-tuple-element.38), channel_id=1, source_target_pairs={{0,16},{2,18},{4,20},{6,22},{8,24},{10,26},{12,28},{14,30},{16,0},... | collective-permute-start | bytes 196616 | tf_op jit(solution)/shard_map/ppermute | solution.py:337
  103.1 3.8 %collective-permute-start.15 = (bf16[256,128]{1,0:T(8,128)(2,1)S(1)}, bf16[256,128]{1,0:T(8,128)(2,1)S(1)}, u32[]{:S(2)}, u32[]{:S(2)}) collective-permute-start(bf16[256,128]{1,0:T(8,128)(2,1)S(1)} %get-tuple-element.36), channel_id=1, source_target_pairs={{0,8},{2,10},{4,12},{6,14},{8,0},{10,2},{12,4},{14,6},{16,24},{18,... | collective-permute-start | bytes 196616 | tf_op jit(solution)/shard_map/ppermute | solution.py:337
  107.8 1.8 %collective-permute-done.18 = bf16[256,128]{1,0:T(8,128)(2,1)S(1)} collective-permute-done((bf16[256,128]{1,0:T(8,128)(2,1)S(1)}, bf16[256,128]{1,0:T(8,128)(2,1)S(1)}, u32[]{:S(2)}, u32[]{:S(2)}) %collective-permute-start.18) | collective-permute-done | bytes 65568 | tf_op jit(solution)/shard_map/ppermute | solution.py:337
  111.5 1.6 %collective-permute-start.21 = (bf16[256,128]{1,0:T(8,128)(2,1)S(1)}, bf16[256,128]{1,0:T(8,128)(2,1)S(1)}, u32[]{:S(2)}, u32[]{:S(2)}) collective-permute-start(bf16[256,128]{1,0:T(8,128)(2,1)S(1)} %add_convert_fusion), channel_id=1, source_target_pairs={{0,1},{1,0},{2,3},{3,2},{4,5},{5,4},{6,7},{7,6},{8,9},{9,8},{10,11... | collective-permute-start | bytes 196616 | tf_op jit(solution)/shard_map/ppermute | solution.py:400
  113.7 2.2 %collective-permute-done.21 = bf16[256,128]{1,0:T(8,128)(2,1)S(1)} collective-permute-done((bf16[256,128]{1,0:T(8,128)(2,1)S(1)}, bf16[256,128]{1,0:T(8,128)(2,1)S(1)}, u32[]{:S(2)}, u32[]{:S(2)}) %collective-permute-start.21) | collective-permute-done | bytes 65568 | tf_op jit(solution)/shard_map/ppermute | solution.py:400
  116.6 2.1 %reduce_sum.12 = bf16[512,128]{1,0:T(8,128)(2,1)} reduce(bf16[8,512,128]{2,1,0:T(8,128)(2,1)} %all-to-all-done.1, bf16[]{:T(256)} %constant.3.clone.1), dimensions={0}, to_apply=%region_1.2 | reduce | flops 458752 | bytes 1179650 | tf_op jit(solution)/shard_map/reduce_sum | solution.py:396
  (54 shorter events, 10.3 us)
Async XLA Ops:
  0.6 26.3 %copy-start.3 = (bf16[512,128]{1,0:T(8,128)(2,1)S(1)}, bf16[512,128]{1,0:T(8,128)(2,1)}, u32[]{:S(2)}) copy-start(bf16[512,128]{1,0:T(8,128)(2,1)} %param.9) | copy-start | bytes 393220
  26.9 32.6 %collective-permute-start.8 = (bf16[4096,128]{1,0:T(8,128)(2,1)}, bf16[4096,128]{1,0:T(8,128)(2,1)S(1)}, u32[]{:S(2)}, u32[]{:S(2)}) collective-permute-start(bf16[4096,128]{1,0:T(8,128)(2,1)} %get-tuple-element.24), channel_id=1, source_target_pairs={{0,2},{2,0},{4,6},{6,4},{8,10},{10,8},{12,14},{14,12},{16,18},{18,... | collective-permute-start | bytes 3145736 | tf_op jit(solution)/shard_map/ppermute | solution.py:337
  27.0 9.4 %collective-permute-start = (bf16[512,128]{1,0:T(8,128)(2,1)S(1)}, bf16[512,128]{1,0:T(8,128)(2,1)S(1)}, u32[]{:S(2)}, u32[]{:S(2)}) collective-permute-start(bf16[512,128]{1,0:T(8,128)(2,1)S(1)} %copy-done.3), channel_id=1, source_target_pairs={{0,16},{2,18},{4,20},{6,22},{8,24},{10,26},{12,28},{14,30},{16,0},... | collective-permute-start | bytes 393224 | tf_op jit(solution)/shard_map/ppermute | solution.py:337
  36.4 8.3 %collective-permute-start.1 = (bf16[1024,128]{1,0:T(8,128)(2,1)S(1)}, bf16[1024,128]{1,0:T(8,128)(2,1)S(1)}, u32[]{:S(2)}, u32[]{:S(2)}) collective-permute-start(bf16[1024,128]{1,0:T(8,128)(2,1)S(1)} %constant_dynamic-update-slice_fusion.refs_0_), channel_id=1, source_target_pairs={{0,4},{2,6},{4,0},{6,2},{8,12},{10,14},{12,8},{14,10},{16,20},{18,... | collective-permute-start | bytes 786440 | tf_op jit(solution)/shard_map/ppermute | solution.py:337
  37.0 9.2 %collective-permute-start.2 = (bf16[1024,128]{1,0:T(8,128)(2,1)S(1)}, bf16[1024,128]{1,0:T(8,128)(2,1)S(1)}, u32[]{:S(2)}, u32[]{:S(2)}) collective-permute-start(bf16[1024,128]{1,0:T(8,128)(2,1)S(1)} %constant_dynamic-update-slice_fusion.refs_0_), channel_id=1, source_target_pairs={{0,8},{2,10},{4,12},{6,14},{8,0},{10,2},{12,4},{14,6},{16,24},{18,... | collective-permute-start | bytes 786440 | tf_op jit(solution)/shard_map/ppermute | solution.py:337
  37.0 14.5 %collective-permute-start.3 = (bf16[1024,128]{1,0:T(8,128)(2,1)S(1)}, bf16[1024,128]{1,0:T(8,128)(2,1)S(1)}, u32[]{:S(2)}, u32[]{:S(2)}) collective-permute-start(bf16[1024,128]{1,0:T(8,128)(2,1)S(1)} %constant_dynamic-update-slice_fusion.refs_0_), channel_id=1, source_target_pairs={{0,12},{2,14},{4,8},{6,10},{8,4},{10,6},{12,0},{14,2},{16,28},{18,... | collective-permute-start | bytes 786440 | tf_op jit(solution)/shard_map/ppermute | solution.py:337
  39.9 11.6 %collective-permute-start.4 = (bf16[1024,128]{1,0:T(8,128)(2,1)S(1)}, bf16[1024,128]{1,0:T(8,128)(2,1)S(1)}, u32[]{:S(2)}, u32[]{:S(2)}) collective-permute-start(bf16[1024,128]{1,0:T(8,128)(2,1)S(1)} %constant_dynamic-update-slice_fusion.refs_0_), channel_id=1, source_target_pairs={{0,2},{2,0},{4,6},{6,4},{8,10},{10,8},{12,14},{14,12},{16,18},{18,... | collective-permute-start | bytes 786440 | tf_op jit(solution)/shard_map/ppermute | solution.py:337
  44.7 6.8 %collective-permute-start.5 = (bf16[1024,128]{1,0:T(8,128)(2,1)S(1)}, bf16[1024,128]{1,0:T(8,128)(2,1)S(1)}, u32[]{:S(2)}, u32[]{:S(2)}) collective-permute-start(bf16[1024,128]{1,0:T(8,128)(2,1)S(1)} %collective-permute-done.1.refs_1_), channel_id=1, source_target_pairs={{0,2},{2,0},{4,6},{6,4},{8,10},{10,8},{12,14},{14,12},{16,18},{18,... | collective-permute-start | bytes 786440 | tf_op jit(solution)/shard_map/ppermute | solution.py:337
  46.2 5.3 %collective-permute-start.6 = (bf16[1024,128]{1,0:T(8,128)(2,1)S(1)}, bf16[1024,128]{1,0:T(8,128)(2,1)S(1)}, u32[]{:S(2)}, u32[]{:S(2)}) collective-permute-start(bf16[1024,128]{1,0:T(8,128)(2,1)S(1)} %collective-permute-done.2.refs_2_), channel_id=1, source_target_pairs={{0,2},{2,0},{4,6},{6,4},{8,10},{10,8},{12,14},{14,12},{16,18},{18,... | collective-permute-start | bytes 786440 | tf_op jit(solution)/shard_map/ppermute | solution.py:337
  51.5 1.5 %collective-permute-start.7 = (bf16[1024,128]{1,0:T(8,128)(2,1)S(1)}, bf16[1024,128]{1,0:T(8,128)(2,1)S(1)}, u32[]{:S(2)}, u32[]{:S(2)}) collective-permute-start(bf16[1024,128]{1,0:T(8,128)(2,1)S(1)} %collective-permute-done.3.refs_3_), channel_id=1, source_target_pairs={{0,2},{2,0},{4,6},{6,4},{8,10},{10,8},{12,14},{14,12},{16,18},{18,... | collective-permute-start | bytes 786440 | tf_op jit(solution)/shard_map/ppermute | solution.py:337
  58.0 14.9 %collective-permute-start.12 = (bf16[2048,128]{1,0:T(8,128)(2,1)S(1)}, bf16[2048,128]{1,0:T(8,128)(2,1)S(1)}, u32[]{:S(2)}, u32[]{:S(2)}) collective-permute-start(bf16[2048,128]{1,0:T(8,128)(2,1)S(1)} %shard_map.105.own_ref), channel_id=1, source_target_pairs={{0,1},{1,0},{2,3},{3,2},{4,5},{5,4},{6,7},{7,6},{8,9},{9,8},{10,11... | collective-permute-start | bytes 1572872 | tf_op jit(solution)/shard_map/ppermute | solution.py:373
  67.7 15.5 %collective-permute-start.10 = (bf16[2048,128]{1,0:T(8,128)(2,1)S(1)}, bf16[2048,128]{1,0:T(8,128)(2,1)S(1)}, u32[]{:S(2)}, u32[]{:S(2)}) collective-permute-start(bf16[2048,128]{1,0:T(8,128)(2,1)S(1)} %get-tuple-element.26.own_ref), channel_id=1, source_target_pairs={{0,1},{1,0},{2,3},{3,2},{4,5},{5,4},{6,7},{7,6},{8,9},{9,8},{10,11... | collective-permute-start | bytes 1572872 | tf_op jit(solution)/shard_map/ppermute | solution.py:373
  68.3 48.3 %all-to-all-start.1 = ((bf16[8,512,128]{2,1,0:T(8,128)(2,1)}), bf16[8,512,128]{2,1,0:T(8,128)(2,1)}, u32[]{:S(2)}, u32[]{:S(2)}) async-start(bf16[8,512,128]{2,1,0:T(8,128)(2,1)} %bitcast.13), calls=%async_computation.1 | async-start | bytes 2097152 | tf_op jit(solution)/shard_map/all_to_all | solution.py:340
  74.4 12.3 %collective-permute-start.13 = (bf16[2048,128]{1,0:T(8,128)(2,1)S(1)}, bf16[2048,128]{1,0:T(8,128)(2,1)S(1)}, u32[]{:S(2)}, u32[]{:S(2)}) collective-permute-start(bf16[2048,128]{1,0:T(8,128)(2,1)S(1)} %get-tuple-element.28.refs_2_), channel_id=1, source_target_pairs={{0,2},{2,0},{4,6},{6,4},{8,10},{10,8},{12,14},{14,12},{16,18},{18,... | collective-permute-start | bytes 1572872 | tf_op jit(solution)/shard_map/ppermute | solution.py:337
  84.8 6.7 %collective-permute-start.11 = (bf16[2048,128]{1,0:T(8,128)(2,1)S(1)}, bf16[2048,128]{1,0:T(8,128)(2,1)S(1)}, u32[]{:S(2)}, u32[]{:S(2)}) collective-permute-start(bf16[2048,128]{1,0:T(8,128)(2,1)S(1)} %get-tuple-element.27.refs_2_), channel_id=1, source_target_pairs={{0,2},{2,0},{4,6},{6,4},{8,10},{10,8},{12,14},{14,12},{16,18},{18,... | collective-permute-start | bytes 1572872 | tf_op jit(solution)/shard_map/ppermute | solution.py:337
  84.9 1.9 %collective-permute-start.9 = (s32[8,512]{1,0:T(8,128)S(1)}, s32[8,512]{1,0:T(8,128)S(1)}, u32[]{:S(2)}, u32[]{:S(2)}) collective-permute-start(s32[8,512]{1,0:T(8,128)S(1)} %reshape.53.refs_0_), channel_id=1, source_target_pairs={{0,2},{2,0},{4,6},{6,4},{8,10},{10,8},{12,14},{14,12},{16,18},{18,... | collective-permute-start | bytes 49160 | tf_op jit(solution)/shard_map/ppermute | solution.py:337
  95.3 7.8 %collective-permute-start.20 = (bf16[256,128]{1,0:T(8,128)(2,1)S(1)}, bf16[256,128]{1,0:T(8,128)(2,1)S(1)}, u32[]{:S(2)}, u32[]{:S(2)}) collective-permute-start(bf16[256,128]{1,0:T(8,128)(2,1)S(1)} %get-tuple-element.41), channel_id=1, source_target_pairs={{0,28},{2,30},{4,24},{6,26},{8,20},{10,22},{12,16},{14,18},{16,12}... | collective-permute-start | bytes 196616 | tf_op jit(solution)/shard_map/ppermute | solution.py:337
  95.5 11.4 %collective-permute-start.19 = (bf16[256,128]{1,0:T(8,128)(2,1)S(1)}, bf16[256,128]{1,0:T(8,128)(2,1)S(1)}, u32[]{:S(2)}, u32[]{:S(2)}) collective-permute-start(bf16[256,128]{1,0:T(8,128)(2,1)S(1)} %get-tuple-element.40), channel_id=1, source_target_pairs={{0,24},{2,26},{4,28},{6,30},{8,16},{10,18},{12,20},{14,22},{16,8},... | collective-permute-start | bytes 196616 | tf_op jit(solution)/shard_map/ppermute | solution.py:337
  99.1 10.5 %collective-permute-start.18 = (bf16[256,128]{1,0:T(8,128)(2,1)S(1)}, bf16[256,128]{1,0:T(8,128)(2,1)S(1)}, u32[]{:S(2)}, u32[]{:S(2)}) collective-permute-start(bf16[256,128]{1,0:T(8,128)(2,1)S(1)} %get-tuple-element.39), channel_id=1, source_target_pairs={{0,20},{2,22},{4,16},{6,18},{8,28},{10,30},{12,24},{14,26},{16,4},... | collective-permute-start | bytes 196616 | tf_op jit(solution)/shard_map/ppermute | solution.py:337
  99.1 10.6 %collective-permute-start.17 = (bf16[256,128]{1,0:T(8,128)(2,1)S(1)}, bf16[256,128]{1,0:T(8,128)(2,1)S(1)}, u32[]{:S(2)}, u32[]{:S(2)}) collective-permute-start(bf16[256,128]{1,0:T(8,128)(2,1)S(1)} %get-tuple-element.38), channel_id=1, source_target_pairs={{0,16},{2,18},{4,20},{6,22},{8,24},{10,26},{12,28},{14,30},{16,0},... | collective-permute-start | bytes 196616 | tf_op jit(solution)/shard_map/ppermute | solution.py:337
  103.0 7.9 %collective-permute-start.16 = (bf16[256,128]{1,0:T(8,128)(2,1)S(1)}, bf16[256,128]{1,0:T(8,128)(2,1)S(1)}, u32[]{:S(2)}, u32[]{:S(2)}) collective-permute-start(bf16[256,128]{1,0:T(8,128)(2,1)S(1)} %get-tuple-element.37), channel_id=1, source_target_pairs={{0,12},{2,14},{4,8},{6,10},{8,4},{10,6},{12,0},{14,2},{16,28},{18,... | collective-permute-start | bytes 196616 | tf_op jit(solution)/shard_map/ppermute | solution.py:337
  103.1 7.8 %collective-permute-start.15 = (bf16[256,128]{1,0:T(8,128)(2,1)S(1)}, bf16[256,128]{1,0:T(8,128)(2,1)S(1)}, u32[]{:S(2)}, u32[]{:S(2)}) collective-permute-start(bf16[256,128]{1,0:T(8,128)(2,1)S(1)} %get-tuple-element.36), channel_id=1, source_target_pairs={{0,8},{2,10},{4,12},{6,14},{8,0},{10,2},{12,4},{14,6},{16,24},{18,... | collective-permute-start | bytes 196616 | tf_op jit(solution)/shard_map/ppermute | solution.py:337
  106.9 4.6 %collective-permute-start.14 = (bf16[256,128]{1,0:T(8,128)(2,1)S(1)}, bf16[256,128]{1,0:T(8,128)(2,1)S(1)}, u32[]{:S(2)}, u32[]{:S(2)}) collective-permute-start(bf16[256,128]{1,0:T(8,128)(2,1)S(1)} %get-tuple-element.35), channel_id=1, source_target_pairs={{0,4},{2,6},{4,0},{6,2},{8,12},{10,14},{12,8},{14,10},{16,20},{18,... | collective-permute-start | bytes 196616 | tf_op jit(solution)/shard_map/ppermute | solution.py:337
  111.5 4.3 %collective-permute-start.21 = (bf16[256,128]{1,0:T(8,128)(2,1)S(1)}, bf16[256,128]{1,0:T(8,128)(2,1)S(1)}, u32[]{:S(2)}, u32[]{:S(2)}) collective-permute-start(bf16[256,128]{1,0:T(8,128)(2,1)S(1)} %add_convert_fusion), channel_id=1, source_target_pairs={{0,1},{1,0},{2,3},{3,2},{4,5},{5,4},{6,7},{7,6},{8,9},{9,8},{10,11... | collective-permute-start | bytes 196616 | tf_op jit(solution)/shard_map/ppermute | solution.py:400
  (6 other events, 90.1 us)

commit v9 on v8

--- a/solution.py
+++ b/solution.py
@@ -11,7 +11,6 @@
 SPLIT = 4
 PARTS = (2, 2)
 GRANT = pltpu.CompilerParams(vmem_limit_bytes=56 << 20)
-SUM_PART = 1
 NEAR_BYTES = 1 << 21
 VMEM = pl.BlockSpec(memory_space=pltpu.VMEM)
 
@@ -361,14 +360,13 @@
     own_named, peer_named = named_rows(asked, table)
     found = swap(peer_named, 1)
 
+    fetched = (own_named.astype(jnp.float32) + found.astype(jnp.float32)).astype(jnp.bfloat16)
+
     halves, bases = [], []
     for part, share in enumerate(PARTS):
         part_rows = row_count // share
         bases.append(sum(row_count // other for other in PARTS[:part]))
-        terms = (own_named, found) if part == SUM_PART else ()
-        mine, *sums = row_gradients(asked, grads, peer_grads, bases[part], part_rows, terms)
-        if sums:
-            fetched = sums[0]
+        mine = row_gradients(asked, grads, peer_grads, bases[part], part_rows)[0]
         distance = 1
         other = lax.ppermute(mine, "dp", [(i, i ^ 1) for i in range(dp_count)])
         while 2 * distance < dp_count:

time: 119 us -> 118 us (level)
  Pallas kernels: 35.2 us -> 33 us
  waiting for transfers between devices: 38.2 us -> 40.2 us
  other arithmetic: 4.37 us -> 5.61 us
    pallas_call x2, Pallas kernels: 12.1 us -> 9.8 us  [row_gradients(): pl.pallas_call(functools.partial(segment_kernel, base=base, count=count),...]
    ppermute x2, waiting for transfers between devices: 8.93 us -> 10.9 us  [on_device(): other = lax.ppermute(mine, 'dp', [(i, i ^ 1) for i in range(dp_count)])]
    convert_element_type x0 -> x1, other arithmetic: none -> 1.24 us  [on_device(): (own_named.astype(jnp.float32) + found.astype(jnp.float32)).astype(jnp.bf...]
  transfers between devices with their start and end apart: 23 -> 23, of which waited for: 14 -> 11; matrix products, arithmetic and copies ran while one was open for 1% -> 2% of each run, Pallas kernels for 20% -> 18%
where the time goes in v9:
time: 118 us
  waiting for transfers between devices  40.2 us (34%)
  Pallas kernels  33 us (28%)
  starting transfers between devices  24.1 us (20%)
  blocking collectives  13.8 us (12%)
  other arithmetic  5.61 us (5%)
    ppermute x19, waiting for transfers between devices, swap(): lax.ppermute(values, 'table', [(i, i ^ distance) for i in range(table_cou...  27.1 us
    ppermute x19, starting transfers between devices, swap(): lax.ppermute(values, 'table', [(i, i ^ distance) for i in range(table_cou...  15.8 us
    all_to_all x1, blocking collectives, on_device(): lax.all_to_all(requests, 'table', split_axis=0, concat_axis=0, tiled=True)  13.8 us
    pallas_call x1, Pallas kernels, named_rows(): pl.pallas_call(functools.partial(gather_kernel, together=2), compiler_par...  11.5 us
    ppermute x2, waiting for transfers between devices, on_device(): other = lax.ppermute(mine, 'dp', [(i, i ^ 1) for i in range(dp_count)])  10.9 us
    pallas_call x2, Pallas kernels, row_gradients(): pl.pallas_call(functools.partial(segment_kernel, base=base, count=count),...  9.8 us
    pallas_call x2, Pallas kernels, parity_changes(): pl.pallas_call(functools.partial(parity_kernel, base=base, holder_rows=ho...  8.44 us
    all_to_all x1, starting transfers between devices, exchange(): lax.all_to_all(values, 'table', split_axis=0, concat_axis=0, axis_index_g...  4.37 us
  transfers between devices with their start and end apart: 23, of which 11 were waited for; matrix products, arithmetic and copies ran while one was open for 2% of the time, Pallas kernels for 18%

profile of v9, /device:TPU:0, one launch (start us, length us, event | category | flops | bytes accessed | tf_op | source)
XLA Modules:
  0.0 117.6 jit_solution(16204539297977556422)
XLA Ops:
  1.6 13.8 %all_to_all.10.asked_ref = s32[16,1,512]{2,1,0:T(1,128)S(1)} all-to-all(s32[16,1,512]{2,1,0:T(1,128)S(1)} %reduce_max.12), channel_id=1, replica_groups=mesh['table'=16,'dp'=2] {'table'}, dimensions={0} | all-to-all | bytes 65536 | tf_op jit(solution)/shard_map/all_to_all | solution.py:348
  15.4 11.5 %shard_map.102 = (bf16[4096,128]{1,0:T(8,128)(2,1)}, bf16[4096,128]{1,0:T(8,128)(2,1)}) custom-call(s32[16,1,512]{2,1,0:T(1,128)S(1)} %all_to_all.10.asked_ref, f32[4096,128]{1,0:T(8,128)} %refs_4_.3), custom_call_target="tpu_custom_call" | custom-call | tf_op jit(solution)/shard_map/pallas_call | solution.py:178
  27.5 8.9 %collective-permute-done.2 = bf16[512,128]{1,0:T(8,128)(2,1)S(1)} collective-permute-done((bf16[512,128]{1,0:T(8,128)(2,1)S(1)}, bf16[512,128]{1,0:T(8,128)(2,1)S(1)}, u32[]{:S(2)}, u32[]{:S(2)}) %collective-permute-start.2) | collective-permute-done | bytes 131104 | tf_op jit(solution)/shard_map/ppermute | solution.py:336
  37.0 2.9 %collective-permute-start.5 = (bf16[1024,128]{1,0:T(8,128)(2,1)S(1)}, bf16[1024,128]{1,0:T(8,128)(2,1)S(1)}, u32[]{:S(2)}, u32[]{:S(2)}) collective-permute-start(bf16[1024,128]{1,0:T(8,128)(2,1)S(1)} %constant_dynamic-update-slice_fusion.refs_0_), channel_id=1, source_target_pairs={{0,12},{2,14},{4,8},{6,10},{8,4},{10,6},{12,0},{14,2},{16,28},{18,... | collective-permute-start | bytes 786440 | tf_op jit(solution)/shard_map/ppermute | solution.py:336
  39.9 4.8 %collective-permute-done.3.refs_1_ = bf16[1024,128]{1,0:T(8,128)(2,1)S(1)} collective-permute-done((bf16[1024,128]{1,0:T(8,128)(2,1)S(1)}, bf16[1024,128]{1,0:T(8,128)(2,1)S(1)}, u32[]{:S(2)}, u32[]{:S(2)}) %collective-permute-start.3) | collective-permute-done | bytes 262176 | tf_op jit(solution)/shard_map/ppermute | solution.py:336
  46.2 5.3 %collective-permute-done.5.refs_3_ = bf16[1024,128]{1,0:T(8,128)(2,1)S(1)} collective-permute-done((bf16[1024,128]{1,0:T(8,128)(2,1)S(1)}, bf16[1024,128]{1,0:T(8,128)(2,1)S(1)}, u32[]{:S(2)}, u32[]{:S(2)}) %collective-permute-start.5) | collective-permute-done | bytes 262176 | tf_op jit(solution)/shard_map/ppermute | solution.py:336
  51.5 1.5 %collective-permute-done.9.refs_7_ = bf16[1024,128]{1,0:T(8,128)(2,1)S(1)} collective-permute-done((bf16[1024,128]{1,0:T(8,128)(2,1)S(1)}, bf16[1024,128]{1,0:T(8,128)(2,1)S(1)}, u32[]{:S(2)}, u32[]{:S(2)}) %collective-permute-start.9) | collective-permute-done | bytes 262176 | tf_op jit(solution)/shard_map/ppermute | solution.py:336
  53.1 4.9 %shard_map.105.own_ref = bf16[2048,128]{1,0:T(8,128)(2,1)S(1)} custom-call(s32[16,1,512]{2,1,0:T(1,128)S(1)} %all_to_all.10.asked_ref, bf16[1024,128]{1,0:T(8,128)(2,1)S(1)} %constant_dynamic-update-slice_fusion.refs_0_, bf16[1024,128]{1,0:T(8,128)(2,1)S(1)} %collective-permute-done.3.refs_1_, bf16[1024,128]{1,0:T(8,128)(2,1)S(1)} %collective-permute-done.4.refs_2_, ...), custom_call_target="tpu_custom_call" | custom-call | tf_op jit(solution)/shard_map/pallas_call | solution.py:129
  58.0 1.7 %collective-permute-start.12 = (bf16[2048,128]{1,0:T(8,128)(2,1)S(1)}, bf16[2048,128]{1,0:T(8,128)(2,1)S(1)}, u32[]{:S(2)}, u32[]{:S(2)}) collective-permute-start(bf16[2048,128]{1,0:T(8,128)(2,1)S(1)} %shard_map.105.own_ref), channel_id=1, source_target_pairs={{0,1},{1,0},{2,3},{3,2},{4,5},{5,4},{6,7},{7,6},{8,9},{9,8},{10,11... | collective-permute-start | bytes 1572872 | tf_op jit(solution)/shard_map/ppermute | solution.py:371
  59.7 4.9 %shard_map.103.own_ref = bf16[2048,128]{1,0:T(8,128)(2,1)S(1)} custom-call(s32[16,1,512]{2,1,0:T(1,128)S(1)} %all_to_all.10.asked_ref, bf16[1024,128]{1,0:T(8,128)(2,1)S(1)} %constant_dynamic-update-slice_fusion.refs_0_, bf16[1024,128]{1,0:T(8,128)(2,1)S(1)} %collective-permute-done.3.refs_1_, bf16[1024,128]{1,0:T(8,128)(2,1)S(1)} %collective-permute-done.4.refs_2_, ...), custom_call_target="tpu_custom_call" | custom-call | tf_op jit(solution)/shard_map/pallas_call | solution.py:129
  66.5 4.4 %all-to-all-start.1 = ((bf16[8,512,128]{2,1,0:T(8,128)(2,1)}), bf16[8,512,128]{2,1,0:T(8,128)(2,1)}, u32[]{:S(2)}, u32[]{:S(2)}) async-start(bf16[8,512,128]{2,1,0:T(8,128)(2,1)} %bitcast.13), calls=%async_computation.1 | async-start | bytes 2097152 | tf_op jit(solution)/shard_map/all_to_all | solution.py:339
  70.8 2.2 %collective-permute-done.12.other_ref = bf16[2048,128]{1,0:T(8,128)(2,1)S(1)} collective-permute-done((bf16[2048,128]{1,0:T(8,128)(2,1)S(1)}, bf16[2048,128]{1,0:T(8,128)(2,1)S(1)}, u32[]{:S(2)}, u32[]{:S(2)}) %collective-permute-start.12) | collective-permute-done | bytes 524320 | tf_op jit(solution)/shard_map/ppermute | solution.py:371
  73.0 1.6 %shard_map.106 = (f32[16,128]{1,0:T(8,128)}, bf16[2048,128]{1,0:T(8,128)(2,1)S(1)}) custom-call(bf16[2048,128]{1,0:T(8,128)(2,1)S(1)} %shard_map.105.own_ref, bf16[2048,128]{1,0:T(8,128)(2,1)S(1)} %collective-permute-done.12.other_ref, f32[32,128]{1,0:T(8,128)S(1)} %bitcast.11), custom_call_target="tpu_custom_call" | custom-call | tf_op jit(solution)/shard_map/pallas_call | solution.py:224
  74.6 8.8 %collective-permute-done.10.other_ref = bf16[2048,128]{1,0:T(8,128)(2,1)S(1)} collective-permute-done((bf16[2048,128]{1,0:T(8,128)(2,1)S(1)}, bf16[2048,128]{1,0:T(8,128)(2,1)S(1)}, u32[]{:S(2)}, u32[]{:S(2)}) %collective-permute-start.10) | collective-permute-done | bytes 524320 | tf_op jit(solution)/shard_map/ppermute | solution.py:371
  83.4 1.6 %shard_map.104 = (f32[16,128]{1,0:T(8,128)}, bf16[2048,128]{1,0:T(8,128)(2,1)S(1)}) custom-call(bf16[2048,128]{1,0:T(8,128)(2,1)S(1)} %shard_map.103.own_ref, bf16[2048,128]{1,0:T(8,128)(2,1)S(1)} %collective-permute-done.10.other_ref, f32[32,128]{1,0:T(8,128)S(1)} %bitcast.12), custom_call_target="tpu_custom_call" | custom-call | tf_op jit(solution)/shard_map/pallas_call | solution.py:224
  87.0 4.7 %shard_map.107 = (f32[4096,128]{1,0:T(8,128)}, f32[512,512]{1,0:T(8,128)}) custom-call(s32[8,512]{1,0:T(8,128)S(1)} %reshape.53.refs_0_, s32[8,512]{1,0:T(8,128)S(1)} %collective-permute-done.1.refs_1_, bf16[2048,128]{1,0:T(8,128)(2,1)S(1)} %get-tuple-element.24.refs_2_, bf16[2048,128]{1,0:T(8,128)(2,1)S(1)} %collective-permute-done.13.refs_3_, ...), custom_call_target="tpu_custom_call" | custom-call | tf_op jit(solution)/shard_map/pallas_call | solution.py:304
  91.7 3.7 %shard_map.108 = (f32[4096,128]{1,0:T(8,128)}, bf16[256,128]{1,0:T(8,128)(2,1)S(1)}, bf16[256,128]{1,0:T(8,128)(2,1)S(1)}, bf16[256,128]{1,0:T(8,128)(2,1)S(1)},...) custom-call(s32[8,512]{1,0:T(8,128)S(1)} %reshape.53.refs_0_, ...), custom_call_target="tpu_custom_call", output_to_operand_aliasing={{0}: (6, {})} | custom-call | tf_op jit(solution)/shard_map/pallas_call | solution.py:304
  96.3 2.7 %collective-permute-start.16 = (bf16[256,128]{1,0:T(8,128)(2,1)S(1)}, bf16[256,128]{1,0:T(8,128)(2,1)S(1)}, u32[]{:S(2)}, u32[]{:S(2)}) collective-permute-start(bf16[256,128]{1,0:T(8,128)(2,1)S(1)} %get-tuple-element.33), channel_id=1, source_target_pairs={{0,12},{2,14},{4,8},{6,10},{8,4},{10,6},{12,0},{14,2},{16,28},{18,... | collective-permute-start | bytes 196616 | tf_op jit(solution)/shard_map/ppermute | solution.py:336
  99.0 2.8 %collective-permute-start.18 = (bf16[256,128]{1,0:T(8,128)(2,1)S(1)}, bf16[256,128]{1,0:T(8,128)(2,1)S(1)}, u32[]{:S(2)}, u32[]{:S(2)}) collective-permute-start(bf16[256,128]{1,0:T(8,128)(2,1)S(1)} %get-tuple-element.35), channel_id=1, source_target_pairs={{0,20},{2,22},{4,16},{6,18},{8,28},{10,30},{12,24},{14,26},{16,4},... | collective-permute-start | bytes 196616 | tf_op jit(solution)/shard_map/ppermute | solution.py:336
  102.1 4.6 %collective-permute-start.20 = (bf16[256,128]{1,0:T(8,128)(2,1)S(1)}, bf16[256,128]{1,0:T(8,128)(2,1)S(1)}, u32[]{:S(2)}, u32[]{:S(2)}) collective-permute-start(bf16[256,128]{1,0:T(8,128)(2,1)S(1)} %get-tuple-element.37), channel_id=1, source_target_pairs={{0,28},{2,30},{4,24},{6,26},{8,20},{10,22},{12,16},{14,18},{16,12}... | collective-permute-start | bytes 196616 | tf_op jit(solution)/shard_map/ppermute | solution.py:336
  108.1 2.2 %collective-permute-done.18 = bf16[256,128]{1,0:T(8,128)(2,1)S(1)} collective-permute-done((bf16[256,128]{1,0:T(8,128)(2,1)S(1)}, bf16[256,128]{1,0:T(8,128)(2,1)S(1)}, u32[]{:S(2)}, u32[]{:S(2)}) %collective-permute-start.18) | collective-permute-done | bytes 65568 | tf_op jit(solution)/shard_map/ppermute | solution.py:336
  110.4 1.6 %collective-permute-start.21 = (bf16[256,128]{1,0:T(8,128)(2,1)S(1)}, bf16[256,128]{1,0:T(8,128)(2,1)S(1)}, u32[]{:S(2)}, u32[]{:S(2)}) collective-permute-start(bf16[256,128]{1,0:T(8,128)(2,1)S(1)} %add_convert_fusion.1), channel_id=1, source_target_pairs={{0,1},{1,0},{2,3},{3,2},{4,5},{5,4},{6,7},{7,6},{8,9},{9,8},{10,11... | collective-permute-start | bytes 196616 | tf_op jit(solution)/shard_map/ppermute | solution.py:398
  112.6 2.2 %collective-permute-done.21 = bf16[256,128]{1,0:T(8,128)(2,1)S(1)} collective-permute-done((bf16[256,128]{1,0:T(8,128)(2,1)S(1)}, bf16[256,128]{1,0:T(8,128)(2,1)S(1)}, u32[]{:S(2)}, u32[]{:S(2)}) %collective-permute-start.21) | collective-permute-done | bytes 65568 | tf_op jit(solution)/shard_map/ppermute | solution.py:398
  115.5 2.1 %reduce_sum.12 = bf16[512,128]{1,0:T(8,128)(2,1)} reduce(bf16[8,512,128]{2,1,0:T(8,128)(2,1)} %all-to-all-done.1, bf16[]{:T(256)} %constant.3.clone.1), dimensions={0}, to_apply=%region_1.2 | reduce | flops 458752 | bytes 1179650 | tf_op jit(solution)/shard_map/reduce_sum | solution.py:394
  (55 shorter events, 11.4 us)
Async XLA Ops:
  26.9 38.3 %collective-permute-start = (bf16[4096,128]{1,0:T(8,128)(2,1)}, bf16[4096,128]{1,0:T(8,128)(2,1)S(1)}, u32[]{:S(2)}, u32[]{:S(2)}) collective-permute-start(bf16[4096,128]{1,0:T(8,128)(2,1)} %get-tuple-element.22), channel_id=1, source_target_pairs={{0,2},{2,0},{4,6},{6,4},{8,10},{10,8},{12,14},{14,12},{16,18},{18,... | collective-permute-start | bytes 3145736 | tf_op jit(solution)/shard_map/ppermute | solution.py:336
  27.0 9.4 %collective-permute-start.2 = (bf16[512,128]{1,0:T(8,128)(2,1)S(1)}, bf16[512,128]{1,0:T(8,128)(2,1)S(1)}, u32[]{:S(2)}, u32[]{:S(2)}) collective-permute-start(bf16[512,128]{1,0:T(8,128)(2,1)S(1)} %copy-done.3), channel_id=1, source_target_pairs={{0,16},{2,18},{4,20},{6,22},{8,24},{10,26},{12,28},{14,30},{16,0},... | collective-permute-start | bytes 393224 | tf_op jit(solution)/shard_map/ppermute | solution.py:336
  36.4 28.9 %copy-start.1 = (bf16[4096,128]{1,0:T(8,128)(2,1)S(1)}, bf16[4096,128]{1,0:T(8,128)(2,1)}, u32[]{:S(2)}) copy-start(bf16[4096,128]{1,0:T(8,128)(2,1)} %get-tuple-element.21) | copy-start | bytes 3145732
  36.4 8.3 %collective-permute-start.3 = (bf16[1024,128]{1,0:T(8,128)(2,1)S(1)}, bf16[1024,128]{1,0:T(8,128)(2,1)S(1)}, u32[]{:S(2)}, u32[]{:S(2)}) collective-permute-start(bf16[1024,128]{1,0:T(8,128)(2,1)S(1)} %constant_dynamic-update-slice_fusion.refs_0_), channel_id=1, source_target_pairs={{0,4},{2,6},{4,0},{6,2},{8,12},{10,14},{12,8},{14,10},{16,20},{18,... | collective-permute-start | bytes 786440 | tf_op jit(solution)/shard_map/ppermute | solution.py:336
  37.0 9.2 %collective-permute-start.4 = (bf16[1024,128]{1,0:T(8,128)(2,1)S(1)}, bf16[1024,128]{1,0:T(8,128)(2,1)S(1)}, u32[]{:S(2)}, u32[]{:S(2)}) collective-permute-start(bf16[1024,128]{1,0:T(8,128)(2,1)S(1)} %constant_dynamic-update-slice_fusion.refs_0_), channel_id=1, source_target_pairs={{0,8},{2,10},{4,12},{6,14},{8,0},{10,2},{12,4},{14,6},{16,24},{18,... | collective-permute-start | bytes 786440 | tf_op jit(solution)/shard_map/ppermute | solution.py:336
  37.0 14.5 %collective-permute-start.5 = (bf16[1024,128]{1,0:T(8,128)(2,1)S(1)}, bf16[1024,128]{1,0:T(8,128)(2,1)S(1)}, u32[]{:S(2)}, u32[]{:S(2)}) collective-permute-start(bf16[1024,128]{1,0:T(8,128)(2,1)S(1)} %constant_dynamic-update-slice_fusion.refs_0_), channel_id=1, source_target_pairs={{0,12},{2,14},{4,8},{6,10},{8,4},{10,6},{12,0},{14,2},{16,28},{18,... | collective-permute-start | bytes 786440 | tf_op jit(solution)/shard_map/ppermute | solution.py:336
  39.9 11.6 %collective-permute-start.6 = (bf16[1024,128]{1,0:T(8,128)(2,1)S(1)}, bf16[1024,128]{1,0:T(8,128)(2,1)S(1)}, u32[]{:S(2)}, u32[]{:S(2)}) collective-permute-start(bf16[1024,128]{1,0:T(8,128)(2,1)S(1)} %constant_dynamic-update-slice_fusion.refs_0_), channel_id=1, source_target_pairs={{0,2},{2,0},{4,6},{6,4},{8,10},{10,8},{12,14},{14,12},{16,18},{18,... | collective-permute-start | bytes 786440 | tf_op jit(solution)/shard_map/ppermute | solution.py:336
  44.7 6.8 %collective-permute-start.7 = (bf16[1024,128]{1,0:T(8,128)(2,1)S(1)}, bf16[1024,128]{1,0:T(8,128)(2,1)S(1)}, u32[]{:S(2)}, u32[]{:S(2)}) collective-permute-start(bf16[1024,128]{1,0:T(8,128)(2,1)S(1)} %collective-permute-done.3.refs_1_), channel_id=1, source_target_pairs={{0,2},{2,0},{4,6},{6,4},{8,10},{10,8},{12,14},{14,12},{16,18},{18,... | collective-permute-start | bytes 786440 | tf_op jit(solution)/shard_map/ppermute | solution.py:336
  46.2 5.3 %collective-permute-start.8 = (bf16[1024,128]{1,0:T(8,128)(2,1)S(1)}, bf16[1024,128]{1,0:T(8,128)(2,1)S(1)}, u32[]{:S(2)}, u32[]{:S(2)}) collective-permute-start(bf16[1024,128]{1,0:T(8,128)(2,1)S(1)} %collective-permute-done.4.refs_2_), channel_id=1, source_target_pairs={{0,2},{2,0},{4,6},{6,4},{8,10},{10,8},{12,14},{14,12},{16,18},{18,... | collective-permute-start | bytes 786440 | tf_op jit(solution)/shard_map/ppermute | solution.py:336
  51.5 1.5 %collective-permute-start.9 = (bf16[1024,128]{1,0:T(8,128)(2,1)S(1)}, bf16[1024,128]{1,0:T(8,128)(2,1)S(1)}, u32[]{:S(2)}, u32[]{:S(2)}) collective-permute-start(bf16[1024,128]{1,0:T(8,128)(2,1)S(1)} %collective-permute-done.5.refs_3_), channel_id=1, source_target_pairs={{0,2},{2,0},{4,6},{6,4},{8,10},{10,8},{12,14},{14,12},{16,18},{18,... | collective-permute-start | bytes 786440 | tf_op jit(solution)/shard_map/ppermute | solution.py:336
  58.0 15.0 %collective-permute-start.12 = (bf16[2048,128]{1,0:T(8,128)(2,1)S(1)}, bf16[2048,128]{1,0:T(8,128)(2,1)S(1)}, u32[]{:S(2)}, u32[]{:S(2)}) collective-permute-start(bf16[2048,128]{1,0:T(8,128)(2,1)S(1)} %shard_map.105.own_ref), channel_id=1, source_target_pairs={{0,1},{1,0},{2,3},{3,2},{4,5},{5,4},{6,7},{7,6},{8,9},{9,8},{10,11... | collective-permute-start | bytes 1572872 | tf_op jit(solution)/shard_map/ppermute | solution.py:371
  64.6 18.8 %collective-permute-start.10 = (bf16[2048,128]{1,0:T(8,128)(2,1)S(1)}, bf16[2048,128]{1,0:T(8,128)(2,1)S(1)}, u32[]{:S(2)}, u32[]{:S(2)}) collective-permute-start(bf16[2048,128]{1,0:T(8,128)(2,1)S(1)} %shard_map.103.own_ref), channel_id=1, source_target_pairs={{0,1},{1,0},{2,3},{3,2},{4,5},{5,4},{6,7},{7,6},{8,9},{9,8},{10,11... | collective-permute-start | bytes 1572872 | tf_op jit(solution)/shard_map/ppermute | solution.py:371
  66.5 49.1 %all-to-all-start.1 = ((bf16[8,512,128]{2,1,0:T(8,128)(2,1)}), bf16[8,512,128]{2,1,0:T(8,128)(2,1)}, u32[]{:S(2)}, u32[]{:S(2)}) async-start(bf16[8,512,128]{2,1,0:T(8,128)(2,1)} %bitcast.13), calls=%async_computation.1 | async-start | bytes 2097152 | tf_op jit(solution)/shard_map/all_to_all | solution.py:339
  74.6 12.3 %collective-permute-start.13 = (bf16[2048,128]{1,0:T(8,128)(2,1)S(1)}, bf16[2048,128]{1,0:T(8,128)(2,1)S(1)}, u32[]{:S(2)}, u32[]{:S(2)}) collective-permute-start(bf16[2048,128]{1,0:T(8,128)(2,1)S(1)} %get-tuple-element.24.refs_2_), channel_id=1, source_target_pairs={{0,2},{2,0},{4,6},{6,4},{8,10},{10,8},{12,14},{14,12},{16,18},{18,... | collective-permute-start | bytes 1572872 | tf_op jit(solution)/shard_map/ppermute | solution.py:336
  85.0 6.6 %collective-permute-start.11 = (bf16[2048,128]{1,0:T(8,128)(2,1)S(1)}, bf16[2048,128]{1,0:T(8,128)(2,1)S(1)}, u32[]{:S(2)}, u32[]{:S(2)}) collective-permute-start(bf16[2048,128]{1,0:T(8,128)(2,1)S(1)} %get-tuple-element.23.refs_2_), channel_id=1, source_target_pairs={{0,2},{2,0},{4,6},{6,4},{8,10},{10,8},{12,14},{14,12},{16,18},{18,... | collective-permute-start | bytes 1572872 | tf_op jit(solution)/shard_map/ppermute | solution.py:336
  85.0 1.9 %collective-permute-start.1 = (s32[8,512]{1,0:T(8,128)S(1)}, s32[8,512]{1,0:T(8,128)S(1)}, u32[]{:S(2)}, u32[]{:S(2)}) collective-permute-start(s32[8,512]{1,0:T(8,128)S(1)} %reshape.53.refs_0_), channel_id=1, source_target_pairs={{0,2},{2,0},{4,6},{6,4},{8,10},{10,8},{12,14},{14,12},{16,18},{18,... | collective-permute-start | bytes 49160 | tf_op jit(solution)/shard_map/ppermute | solution.py:336
  95.5 6.4 %collective-permute-start.14 = (bf16[256,128]{1,0:T(8,128)(2,1)S(1)}, bf16[256,128]{1,0:T(8,128)(2,1)S(1)}, u32[]{:S(2)}, u32[]{:S(2)}) collective-permute-start(bf16[256,128]{1,0:T(8,128)(2,1)S(1)} %get-tuple-element.31), channel_id=1, source_target_pairs={{0,4},{2,6},{4,0},{6,2},{8,12},{10,14},{12,8},{14,10},{16,20},{18,... | collective-permute-start | bytes 196616 | tf_op jit(solution)/shard_map/ppermute | solution.py:336
  96.0 6.1 %collective-permute-start.15 = (bf16[256,128]{1,0:T(8,128)(2,1)S(1)}, bf16[256,128]{1,0:T(8,128)(2,1)S(1)}, u32[]{:S(2)}, u32[]{:S(2)}) collective-permute-start(bf16[256,128]{1,0:T(8,128)(2,1)S(1)} %get-tuple-element.32), channel_id=1, source_target_pairs={{0,8},{2,10},{4,12},{6,14},{8,0},{10,2},{12,4},{14,6},{16,24},{18,... | collective-permute-start | bytes 196616 | tf_op jit(solution)/shard_map/ppermute | solution.py:336
  96.3 10.4 %collective-permute-start.16 = (bf16[256,128]{1,0:T(8,128)(2,1)S(1)}, bf16[256,128]{1,0:T(8,128)(2,1)S(1)}, u32[]{:S(2)}, u32[]{:S(2)}) collective-permute-start(bf16[256,128]{1,0:T(8,128)(2,1)S(1)} %get-tuple-element.33), channel_id=1, source_target_pairs={{0,12},{2,14},{4,8},{6,10},{8,4},{10,6},{12,0},{14,2},{16,28},{18,... | collective-permute-start | bytes 196616 | tf_op jit(solution)/shard_map/ppermute | solution.py:336
  99.0 9.1 %collective-permute-start.17 = (bf16[256,128]{1,0:T(8,128)(2,1)S(1)}, bf16[256,128]{1,0:T(8,128)(2,1)S(1)}, u32[]{:S(2)}, u32[]{:S(2)}) collective-permute-start(bf16[256,128]{1,0:T(8,128)(2,1)S(1)} %get-tuple-element.34), channel_id=1, source_target_pairs={{0,16},{2,18},{4,20},{6,22},{8,24},{10,26},{12,28},{14,30},{16,0},... | collective-permute-start | bytes 196616 | tf_op jit(solution)/shard_map/ppermute | solution.py:336
  99.0 11.3 %collective-permute-start.18 = (bf16[256,128]{1,0:T(8,128)(2,1)S(1)}, bf16[256,128]{1,0:T(8,128)(2,1)S(1)}, u32[]{:S(2)}, u32[]{:S(2)}) collective-permute-start(bf16[256,128]{1,0:T(8,128)(2,1)S(1)} %get-tuple-element.35), channel_id=1, source_target_pairs={{0,20},{2,22},{4,16},{6,18},{8,28},{10,30},{12,24},{14,26},{16,4},... | collective-permute-start | bytes 196616 | tf_op jit(solution)/shard_map/ppermute | solution.py:336
  101.9 8.5 %collective-permute-start.19 = (bf16[256,128]{1,0:T(8,128)(2,1)S(1)}, bf16[256,128]{1,0:T(8,128)(2,1)S(1)}, u32[]{:S(2)}, u32[]{:S(2)}) collective-permute-start(bf16[256,128]{1,0:T(8,128)(2,1)S(1)} %get-tuple-element.36), channel_id=1, source_target_pairs={{0,24},{2,26},{4,28},{6,30},{8,16},{10,18},{12,20},{14,22},{16,8},... | collective-permute-start | bytes 196616 | tf_op jit(solution)/shard_map/ppermute | solution.py:336
  102.1 8.3 %collective-permute-start.20 = (bf16[256,128]{1,0:T(8,128)(2,1)S(1)}, bf16[256,128]{1,0:T(8,128)(2,1)S(1)}, u32[]{:S(2)}, u32[]{:S(2)}) collective-permute-start(bf16[256,128]{1,0:T(8,128)(2,1)S(1)} %get-tuple-element.37), channel_id=1, source_target_pairs={{0,28},{2,30},{4,24},{6,26},{8,20},{10,22},{12,16},{14,18},{16,12}... | collective-permute-start | bytes 196616 | tf_op jit(solution)/shard_map/ppermute | solution.py:336
  110.4 4.3 %collective-permute-start.21 = (bf16[256,128]{1,0:T(8,128)(2,1)S(1)}, bf16[256,128]{1,0:T(8,128)(2,1)S(1)}, u32[]{:S(2)}, u32[]{:S(2)}) collective-permute-start(bf16[256,128]{1,0:T(8,128)(2,1)S(1)} %add_convert_fusion.1), channel_id=1, source_target_pairs={{0,1},{1,0},{2,3},{3,2},{4,5},{5,4},{6,7},{7,6},{8,9},{9,8},{10,11... | collective-permute-start | bytes 196616 | tf_op jit(solution)/shard_map/ppermute | solution.py:398
  (6 other events, 116.4 us)
